TPU v7x, 32 devices: a whole 2x2x4 slice. The times are simulated.
32 devices in a mesh: groups: 2 (over y), ell: 4 (over z), batch: 4 (over x, core).
Axes of the slice: x: 2, y: 2, z: 4, core: 2. Of those that a mesh axis runs over, the one named last changes fastest.
Arguments:
- hidden_act: bfloat16 [128, 1024], P('groups'), parts along dimension 0, may hold values from -1.5 to 1.5
- weight: bfloat16 [8, 1024, 8192], P('groups', 'batch', 'ell'), parts along dimension 0, may hold values from -0.09375 to 0.09375
- first_moment: float32 [8, 1024, 8192], P('groups', 'batch', 'ell'), parts along dimension 0, may hold values from -3 to 3
- second_moment: float32 [8, 1024, 8192], P('groups', 'batch', 'ell'), parts along dimension 0, may hold values from 0.05 to 1
- wigner: bfloat16 [4, 8192, 8192], P(None, 'ell', 'batch'), may hold values from -0.0625 to 0.0625
- quad_weight: float32 [8192], P('batch'), may hold values from 0.5 to 2
- target: bfloat16 [6, 64, 8192], P('groups', None, 'ell'), parts along dimension 0, may hold values from -9 to 9
Outputs:
- new_weight: bfloat16 [8, 1024, 8192], P('groups', 'batch', 'ell'), parts along dimension 0
- new_first: float32 [8, 1024, 8192], P('groups', 'batch', 'ell'), parts along dimension 0
- new_second: float32 [8, 1024, 8192], P('groups', 'batch', 'ell'), parts along dimension 0
There are 2 independent parts, one for each index of `groups`. A program takes and returns all parts, laid end to end along the dimension named above; an argument that names none is the same for every part. Nothing has to cross between parts.
All inputs are finite; a program needn't handle non-finite values.
Results may differ from a plain program's by a relative error of at most 0.012.
Values may be sent and summed in bfloat16 or wider, within the bound.
No kernel may reach another device: no remote copies, remote signals or barrier semaphores. Data moves between devices by JAX's collectives and lax.ppermute only.
A program may use at most 128 MiB of HBM per device.

v0:
```python
import jax
import jax.numpy as jnp
from jax import lax
from jax.sharding import PartitionSpec as P

L = 8192


first_fix = 0.9999734386
second_fix = 0.0952078528


def forward_terms(rows, wigner):
    parts = []
    for table in range(3):
        parts.append(
            jnp.einsum(
                "rcl,la->rca",
                rows[2 * table : 2 * table + 2],
                wigner[table],
                preferred_element_type=jnp.float32,
            )
        )
    parts.append(
        jnp.einsum("rcl,la->rca", rows[6:7], wigner[3], preferred_element_type=jnp.float32)
    )
    return jnp.concatenate(parts, 0)


def backward_terms(piece, tables):
    parts = []
    for table in range(3):
        parts.append(
            jnp.einsum(
                "rca,la->rcl",
                piece[2 * table : 2 * table + 2],
                tables[table],
                preferred_element_type=jnp.float32,
            )
        )
    parts.append(
        jnp.einsum("rca,la->rcl", piece[6:7], tables[3], preferred_element_type=jnp.float32)
    )
    return jnp.concatenate(parts, 0)


def angle_reduce(partial_value):
    return lax.psum(partial_value.astype(jnp.bfloat16), "ell").astype(jnp.float32)


def angle_apply(share, work, init):
    return work(init, share, 0)


def multipole_reduce(partial_value):
    return lax.psum(partial_value.astype(jnp.bfloat16), "batch").astype(jnp.float32)


def local(hidden_act, weight, first_moment, second_moment, wigner, quad_weight, target):
    batch_rows = hidden_act.shape[0]
    h_local = weight.shape[1]
    l_local = weight.shape[2]
    ell_start = lax.axis_index("ell") * l_local
    multipole = (ell_start + lax.iota(jnp.int32, l_local)).astype(jnp.float32)
    lens_rate = multipole * (multipole + 1.0) / (float(L) * float(L))
    loss_weight = 1.0 + 2.0 * multipole / float(L)
    own_hidden = lax.dynamic_slice_in_dim(hidden_act, lax.axis_index("batch") * h_local, h_local, 1)
    local_terms = jnp.einsum("cj,sjl->scl", own_hidden, weight, preferred_element_type=jnp.float32)
    log_power = lax.psum(local_terms, "batch")
    power_temp = jnp.exp(log_power[0])
    power_pol = jnp.exp(log_power[2])
    cross_scale = jnp.exp(0.5 * (log_power[0] + log_power[2]))
    cross_ratio = jnp.tanh(log_power[1])
    power_cross = cross_ratio * cross_scale
    power_lens = jnp.exp(log_power[3])
    rows = jnp.stack(
        [
            power_temp,
            lens_rate * power_temp,
            power_cross,
            lens_rate * power_cross,
            power_pol,
            lens_rate * power_pol,
            power_lens,
        ]
    ).astype(jnp.bfloat16)
    angle_sums = angle_reduce(forward_terms(rows, wigner))
    lensed_corr = angle_sums[0:6:2] - angle_sums[6:7] * angle_sums[1:6:2]
    back_rows = (lensed_corr * quad_weight).astype(jnp.bfloat16)

    def project_back(total, piece, start):
        return jnp.stack(
            [
                jnp.einsum(
                    "ca,la->cl", piece[table], wigner[table], preferred_element_type=jnp.float32
                )
                for table in range(3)
            ]
        )

    back_empty = jnp.zeros((3, batch_rows, l_local), jnp.float32)
    lensed_power = multipole_reduce(angle_apply(back_rows, project_back, back_empty))
    residual_grad = (loss_weight * (lensed_power - target.astype(jnp.float32)) / batch_rows).astype(
        jnp.bfloat16
    )
    back_partial = jnp.stack(
        [
            jnp.einsum(
                "cl,la->ca", residual_grad[table], wigner[table], preferred_element_type=jnp.float32
            )
            for table in range(3)
        ]
    )
    corr_grad = angle_reduce(back_partial) * quad_weight
    lens_sigma = angle_sums[6:7]
    sigma_grad = -jnp.sum(corr_grad * angle_sums[1:6:2], axis=0, keepdims=True)
    term_grad = jnp.concatenate(
        [
            corr_grad[0:1],
            -lens_sigma * corr_grad[0:1],
            corr_grad[1:2],
            -lens_sigma * corr_grad[1:2],
            corr_grad[2:3],
            -lens_sigma * corr_grad[2:3],
            sigma_grad,
        ],
        0,
    ).astype(jnp.bfloat16)

    def project_rows(total, piece, start):
        return backward_terms(piece, wigner)

    row_empty = jnp.zeros((7, batch_rows, l_local), jnp.float32)
    row_grad = multipole_reduce(angle_apply(term_grad, project_rows, row_empty))
    temp_coef = row_grad[0] + lens_rate * row_grad[1]
    cross_coef = row_grad[2] + lens_rate * row_grad[3]
    pol_coef = row_grad[4] + lens_rate * row_grad[5]
    log_grad = jnp.stack(
        [
            temp_coef * power_temp + 0.5 * cross_coef * power_cross,
            cross_coef * (1.0 - cross_ratio * cross_ratio) * cross_scale,
            pol_coef * power_pol + 0.5 * cross_coef * power_cross,
            row_grad[6] * power_lens,
        ]
    ).astype(jnp.bfloat16)
    weight_grad = jnp.einsum(
        "cj,scl->sjl", own_hidden, log_grad, preferred_element_type=jnp.float32
    )
    new_first = 0.9 * first_moment + 0.1 * weight_grad
    new_second = 0.999 * second_moment + 0.001 * weight_grad * weight_grad
    update = new_first / first_fix / (jnp.sqrt(new_second / second_fix) + 1e-08)
    new_weight = (weight.astype(jnp.float32) - 0.001 * update).astype(jnp.bfloat16)
    return (new_weight, new_first, new_second)


def solution(mesh):
    return jax.shard_map(
        local,
        mesh=mesh,
        in_specs=(
            P("groups", None),
            P("groups", "batch", "ell"),
            P("groups", "batch", "ell"),
            P("groups", "batch", "ell"),
            P(None, "ell", "batch"),
            P("batch"),
            P("groups", None, "ell"),
        ),
        out_specs=(
            P("groups", "batch", "ell"),
            P("groups", "batch", "ell"),
            P("groups", "batch", "ell"),
        ),
        check_vma=False,
    )
```

profile of v0, /device:TPU:0, one launch (start us, length us, event | category | flops | bytes accessed | tf_op | source)
XLA Modules:
  0.0 409.2 jit_solution(16231795014506757940)
XLA Ops:
  12.5 54.2 %all-reduce.6.cloned.1.call-done = f32[4,64,2048]{2,1,0:T(8,128)} async-done(((f32[4,64,2048]{2,1,0:T(8,128)}), f32[4,64,2048]{2,1,0:T(8,128)}) %all-reduce.6.cloned.1.call-update) | async-done | bytes 2097168 | tf_op jit(solution)/shard_map/psum | solution.py:69
  77.8 4.8 %fusion.56 = bf16[2,64,2048]{2,1,0:T(8,128)(2,1)S(1)} fusion(bf16[4,2048,2048]{2,1,0:T(8,128)(2,1)} %param.11, bf16[1,64,2048]{2,1,0:T(8,128)(2,1)S(1)} %get-tuple-element.19, bf16[1,64,2048]{2,1,0:T(8,128)(2,1)S(1)} %get-tuple-element.21), kind=kOutput, calls=%fused_computation.52 | convolution fusion | flops 1074266112 | bytes 9437184 | tf_op jit(solution)/shard_map/rcl,la->rca/dot_general | solution.py:17
  82.6 4.9 %fusion.89 = bf16[1,64,2048]{2,1,0:T(8,128)(2,1)S(1)} fusion(bf16[4,2048,2048]{2,1,0:T(8,128)(2,1)} %param.11, f32[4,64,2048]{2,1,0:T(8,128)S(1)} %copy-done.3), kind=kOutput, calls=%fused_computation.63 | convolution fusion | flops 537133056 | bytes 9175040 | tf_op jit(solution)/shard_map/rcl,la->rca/dot_general | solution.py:25
  89.3 77.7 %all-reduce.8.cloned.1.call-done = bf16[7,64,2048]{2,1,0:T(8,128)(2,1)} async-done(((bf16[7,64,2048]{2,1,0:T(8,128)(2,1)}), bf16[7,64,2048]{2,1,0:T(8,128)(2,1)}) %all-reduce.8.cloned.1.call-update) | async-done | bytes 1835024 | tf_op jit(solution)/shard_map/psum | solution.py:48
  171.1 6.0 %fusion.92 = bf16[1,64,2048]{2,1,0:T(8,128)(2,1)S(1)} fusion(bf16[4,2048,2048]{2,1,0:T(8,128)(2,1)} %param.11, bf16[3,64,2048]{2,1,0:T(8,128)(2,1)S(1)} %multiply_convert_fusion.1), kind=kOutput, calls=%fused_computation.64 | convolution fusion | flops 537001984 | bytes 8912896 | tf_op jit(solution)/shard_map/ca,la->cl/dot_general | solution.py:94
  177.2 6.0 %fusion.98 = bf16[1,64,2048]{2,1,0:T(8,128)(2,1)S(1)} fusion(bf16[4,2048,2048]{2,1,0:T(8,128)(2,1)} %param.11, bf16[3,64,2048]{2,1,0:T(8,128)(2,1)S(1)} %multiply_convert_fusion.1), kind=kOutput, calls=%fused_computation.66 | convolution fusion | flops 537001984 | bytes 8912896 | tf_op jit(solution)/shard_map/ca,la->cl/dot_general | solution.py:94
  183.2 6.1 %fusion.104 = bf16[1,64,2048]{2,1,0:T(8,128)(2,1)S(1)} fusion(bf16[4,2048,2048]{2,1,0:T(8,128)(2,1)} %param.11, bf16[3,64,2048]{2,1,0:T(8,128)(2,1)S(1)} %multiply_convert_fusion.1), kind=kOutput, calls=%fused_computation.68 | convolution fusion | flops 537001984 | bytes 8912896 | tf_op jit(solution)/shard_map/ca,la->cl/dot_general | solution.py:94
  191.0 33.2 %all-reduce.10.cloned.1.call-done = bf16[3,64,2048]{2,1,0:T(8,128)(2,1)} async-done(((bf16[3,64,2048]{2,1,0:T(8,128)(2,1)}), bf16[3,64,2048]{2,1,0:T(8,128)(2,1)}) %all-reduce.10.cloned.1.call-update) | async-done | bytes 786448 | tf_op jit(solution)/shard_map/psum | solution.py:56
  225.6 5.0 %fusion.95 = bf16[1,64,2048]{2,1,0:T(8,128)(2,1)S(1)} fusion(bf16[4,2048,2048]{2,1,0:T(8,128)(2,1)} %param.11, bf16[3,64,2048]{2,1,0:T(8,128)(2,1)S(1)} %multiply_convert_fusion), kind=kOutput, calls=%fused_computation.65 | convolution fusion | flops 537001984 | bytes 8912896 | tf_op jit(solution)/shard_map/cl,la->ca/dot_general | solution.py:108
  230.6 5.0 %fusion.101 = bf16[1,64,2048]{2,1,0:T(8,128)(2,1)S(1)} fusion(bf16[4,2048,2048]{2,1,0:T(8,128)(2,1)} %param.11, bf16[3,64,2048]{2,1,0:T(8,128)(2,1)S(1)} %multiply_convert_fusion), kind=kOutput, calls=%fused_computation.67 | convolution fusion | flops 537001984 | bytes 8912896 | tf_op jit(solution)/shard_map/cl,la->ca/dot_general | solution.py:108
  235.6 5.0 %fusion.107 = bf16[1,64,2048]{2,1,0:T(8,128)(2,1)S(1)} fusion(bf16[4,2048,2048]{2,1,0:T(8,128)(2,1)} %param.11, bf16[3,64,2048]{2,1,0:T(8,128)(2,1)S(1)} %multiply_convert_fusion), kind=kOutput, calls=%fused_computation.69 | convolution fusion | flops 537001984 | bytes 8912896 | tf_op jit(solution)/shard_map/cl,la->ca/dot_general | solution.py:108
  241.8 43.6 %all-reduce.12.cloned.1.call-done = bf16[3,64,2048]{2,1,0:T(8,128)(2,1)} async-done(((bf16[3,64,2048]{2,1,0:T(8,128)(2,1)}), bf16[3,64,2048]{2,1,0:T(8,128)(2,1)}) %all-reduce.12.cloned.1.call-update) | async-done | bytes 786448 | tf_op jit(solution)/shard_map/psum | solution.py:48
  288.7 6.0 %fusion.86 = bf16[1,64,2048]{2,1,0:T(8,128)(2,1)S(1)} fusion(bf16[4,2048,2048]{2,1,0:T(8,128)(2,1)} %param.11, f32[64,2048]{1,0:T(8,128)S(1)} %get-tuple-element.28), kind=kOutput, calls=%fused_computation.62 | convolution fusion | flops 537264128 | bytes 9175040 | tf_op jit(solution)/shard_map/rca,la->rcl/dot_general | solution.py:42
  294.7 6.3 %fusion.47 = bf16[2,64,2048]{2,1,0:T(8,128)(2,1)S(1)} fusion(bf16[4,2048,2048]{2,1,0:T(8,128)(2,1)} %param.11, bf16[1,64,2048]{2,1,0:T(8,128)(2,1)S(1)} %get-tuple-element.15, bf16[1,64,2048]{2,1,0:T(8,128)(2,1)S(1)} %get-tuple-element.24), kind=kOutput, calls=%fused_computation.49 | convolution fusion | flops 1074266112 | bytes 9437184 | tf_op jit(solution)/shard_map/rca,la->rcl/dot_general | solution.py:34
  301.0 6.3 %fusion.59 = bf16[2,64,2048]{2,1,0:T(8,128)(2,1)S(1)} fusion(bf16[4,2048,2048]{2,1,0:T(8,128)(2,1)} %param.11, bf16[1,64,2048]{2,1,0:T(8,128)(2,1)S(1)} %get-tuple-element.17, bf16[1,64,2048]{2,1,0:T(8,128)(2,1)S(1)} %get-tuple-element.25), kind=kOutput, calls=%fused_computation.53 | convolution fusion | flops 1074266112 | bytes 9437184 | tf_op jit(solution)/shard_map/rca,la->rcl/dot_general | solution.py:34
  307.3 6.3 %fusion.53 = bf16[2,64,2048]{2,1,0:T(8,128)(2,1)S(1)} fusion(bf16[4,2048,2048]{2,1,0:T(8,128)(2,1)} %param.11, bf16[1,64,2048]{2,1,0:T(8,128)(2,1)S(1)} %get-tuple-element.16, bf16[1,64,2048]{2,1,0:T(8,128)(2,1)S(1)} %get-tuple-element.26), kind=kOutput, calls=%fused_computation.51 | convolution fusion | flops 1074266112 | bytes 9437184 | tf_op jit(solution)/shard_map/rca,la->rcl/dot_general | solution.py:34
  315.1 6.6 %copy.10 = bf16[4,256,2048]{1,2,0:T(8,128)(2,1)} copy(bf16[4,256,2048]{2,1,0:T(8,128)(2,1)} %param.8) | data formatting | bytes 8388608 | tf_op args[1]
  321.7 8.7 %copy.11 = f32[4,256,2048]{1,2,0:T(8,128)} copy(f32[4,256,2048]{2,1,0:T(8,128)} %param.9) | data formatting | bytes 16777216 | tf_op args[2]
  330.4 8.7 %copy.12 = f32[4,256,2048]{1,2,0:T(8,128)} copy(f32[4,256,2048]{2,1,0:T(8,128)} %param.10) | data formatting | bytes 16777216 | tf_op args[3]
  339.1 22.6 %all-reduce.14.cloned.1.call-done = bf16[7,64,2048]{2,1,0:T(8,128)(2,1)} async-done(((bf16[7,64,2048]{2,1,0:T(8,128)(2,1)}), bf16[7,64,2048]{2,1,0:T(8,128)(2,1)}) %all-reduce.14.cloned.1.call-update) | async-done | bytes 1835024 | tf_op jit(solution)/shard_map/psum | solution.py:56
  365.6 13.5 %subtract_convert_fusion = (bf16[4,256,2048]{1,2,0:T(8,128)(2,1)}, f32[4,256,2048]{1,2,0:T(8,128)}, f32[4,256,2048]{1,2,0:T(8,128)}) fusion(bf16[4,256,2048]{1,2,0:T(8,128)(2,1)} %copy.10, f32[4,256,2048]{1,2,0:T(8,128)S(1)} %copy-done.2, f32[4,256,2048]{1,2,0:T(8,128)} %copy.12, bf16[64,1024]{1,0:T(8,128)(2,1)S(1)} %copy-done, s32[]{:T(128)S(6)} %select_n.3, ...), kind=kOutput, calls=%fused_computation.32 | convolution fusion | flops 301465600 | bytes 43024388 | tf_op jit(solution)/shard_map/cj,scl->sjl/dot_general | solution.py:146
  379.2 6.2 %copy.13 = bf16[4,256,2048]{2,1,0:T(8,128)(2,1)} copy(bf16[4,256,2048]{1,2,0:T(8,128)(2,1)} %get-tuple-element.6) | data formatting | bytes 8388608
  385.4 8.7 %copy.14 = f32[4,256,2048]{2,1,0:T(8,128)} copy(f32[4,256,2048]{1,2,0:T(8,128)} %get-tuple-element.7) | data formatting | bytes 16777216
  394.0 8.7 %copy.15 = f32[4,256,2048]{2,1,0:T(8,128)} copy(f32[4,256,2048]{1,2,0:T(8,128)} %get-tuple-element.8) | data formatting | bytes 16777216
  (42 shorter events, 35.2 us)
Async XLA Ops:
  7.2 0.9 copy-start
  7.2 59.5 %all-reduce.6.cloned.1.call-start = ((), (), s32[]{:S(2)}) async-start(), calls=%async_computation | async-start | bytes 4194304 | tf_op jit(solution)/shard_map/psum | solution.py:69
  12.4 154.6 %all-reduce.8.cloned.1.call-start = ((), (), s32[]{:S(2)}) async-start(), calls=%async_computation.1 | async-start | bytes 3670016 | tf_op jit(solution)/shard_map/psum | solution.py:48
  77.8 4.8 %copy-start.3 = (f32[4,64,2048]{2,1,0:T(8,128)S(1)}, f32[4,64,2048]{2,1,0:T(8,128)}, u32[]{:S(2)}) copy-start(f32[4,64,2048]{2,1,0:T(8,128)} %all-reduce.6.cloned.1.call-done) | copy-start | bytes 6291460
  87.6 83.2 %copy-start.5 = (f32[2048]{0:T(1024)S(1)}, f32[2048]{0:T(1024)}, u32[]{:S(2)}) copy-start(f32[2048]{0:T(1024)} %param.12) | copy-start | bytes 24580
  89.1 135.1 %all-reduce.10.cloned.1.call-start = ((), (), s32[]{:S(2)}) async-start(), calls=%async_computation.2 | async-start | bytes 1572864 | tf_op jit(solution)/shard_map/psum | solution.py:56
  169.0 1.8 copy-start.1
  183.2 41.0 %copy-start.4 = (bf16[3,64,2048]{2,1,0:T(8,128)(2,1)S(1)}, bf16[3,64,2048]{2,1,0:T(8,128)(2,1)}, u32[]{:S(2)}) copy-start(bf16[3,64,2048]{2,1,0:T(8,128)(2,1)} %param.13) | copy-start | bytes 2359300
  190.4 95.0 %all-reduce.12.cloned.1.call-start = ((), (), s32[]{:S(2)}) async-start(), calls=%async_computation.3 | async-start | bytes 1572864 | tf_op jit(solution)/shard_map/psum | solution.py:48
  241.5 120.2 %all-reduce.14.cloned.1.call-start = ((), (), s32[]{:S(2)}) async-start(), calls=%async_computation.4 | async-start | bytes 3670016 | tf_op jit(solution)/shard_map/psum | solution.py:56
  361.7 3.9 copy-start.2
Sparse Core Ops, SparseCore 0:
  12.6 54.0 all-reduce.5
  89.2 77.7 all-reduce.7
  190.5 33.6 all-reduce.9
  241.6 43.7 all-reduce.11
  315.2 46.4 all-reduce.13
where the time goes:
time: 411 us; the launch traced here: 409 us
  waiting for transfers between devices  231 us (56%)
  matrix products  94.9 us (23%)
  local copies, waits for them, and re-layouts  51.4 us (13%)
  other arithmetic  16.9 us (4%)
  between operations  14 us (3%)
    psum x2, waiting for transfers between devices, angle_reduce(): lax.psum(partial_value.astype(jnp.bfloat16), 'ell').astype(jnp.float32)  121 us
    psum x2, waiting for transfers between devices, multipole_reduce(): lax.psum(partial_value.astype(jnp.bfloat16), 'batch').astype(jnp.float32)  55.8 us
    psum x1, waiting for transfers between devices, local(): log_power = lax.psum(local_terms, 'batch')  54.2 us
    unnamed x18, local copies, waits for them, and re-layouts  51.3 us
    dot_general x3, matrix products, backward_terms(): jnp.einsum('rca,la->rcl', piece[2 * table:2 * table + 2], tables[table],...  18.8 us
    dot_general x3, matrix products, project_back(): jnp.einsum('ca,la->cl', piece[table], wigner[table], preferred_element_ty...  18.2 us
    dot_general x3, matrix products, local(): jnp.einsum('cl,la->ca', residual_grad[table], wigner[table], preferred_el...  14.9 us
    dot_general x3, matrix products, forward_terms(): jnp.einsum('rcl,la->rca', rows[2 * table:2 * table + 2], wigner[table], p...  14.2 us
  transfers between devices with their start and end apart: 5, of which 5 were waited for; matrix products, arithmetic and copies ran while one was open for 6% of the time, Pallas kernels for 0%

commit v1 on v0

--- a/solution.py
+++ b/solution.py
@@ -1,6 +1,8 @@
 import jax
 import jax.numpy as jnp
 from jax import lax
+from jax.experimental import pallas as pl
+from jax.experimental.pallas import tpu as pltpu
 from jax.sharding import PartitionSpec as P
 
 L = 8192
@@ -56,7 +58,7 @@
     return lax.psum(partial_value.astype(jnp.bfloat16), "batch").astype(jnp.float32)
 
 
-def local(hidden_act, weight, first_moment, second_moment, wigner, quad_weight, target):
+def local_plain(hidden_act, weight, first_moment, second_moment, wigner, quad_weight, target):
     batch_rows = hidden_act.shape[0]
     h_local = weight.shape[1]
     l_local = weight.shape[2]
@@ -153,9 +155,311 @@
     return (new_weight, new_first, new_second)
 
 
+bf16 = jnp.bfloat16
+f32 = jnp.float32
+ORDER = (0, 2, 1, 3)
+
+
+def swap(value, axis, mask):
+    count = lax.axis_size(axis)
+    return lax.ppermute(value, axis, [(i, i ^ mask) for i in range(count)])
+
+
+def scatter(keep, send, axis):
+    half = keep.shape[0] // 2
+    near = keep + swap(send, axis, 1).astype(f32)
+    return near[:half] + swap(near[half:].astype(bf16), axis, 2).astype(f32)
+
+
+def gather(own, axis):
+    far = swap(own, axis, 2)
+    near = swap(own, axis, 1)
+    return (own, near, far, swap(far, axis, 1))
+
+
+def call(kernel, out_shape, *args, in_hbm=(), scratch=(), aliases=None, flops=0, moved=0):
+    vmem = pl.BlockSpec(memory_space=pltpu.VMEM)
+    hbm = pl.BlockSpec(memory_space=pl.ANY)
+    return pl.pallas_call(
+        kernel,
+        out_shape=out_shape,
+        in_specs=[hbm if i in in_hbm else vmem for i in range(len(args))],
+        out_specs=jax.tree.map(lambda _: vmem, out_shape),
+        scratch_shapes=list(scratch),
+        compiler_params=pltpu.CompilerParams(vmem_limit_bytes=8 << 20),
+        cost_estimate=pl.CostEstimate(flops=flops, transcendentals=0, bytes_accessed=moved),
+    )(*args)
+
+
+def fetch_table(wigner, table):
+    _, rows, cols = wigner.shape
+    pieces = 8
+    step = rows // pieces
+
+    def kernel(source, out, sem):
+        copies = [
+            pltpu.make_async_copy(
+                source.at[table, pl.ds(i * step, step)], out.at[pl.ds(i * step, step)], sem.at[i]
+            )
+            for i in range(pieces)
+        ]
+        for copy in copies:
+            copy.start()
+        for copy in copies:
+            copy.wait()
+
+    return call(
+        kernel,
+        pltpu.VMEM((rows, cols), bf16),
+        wigner,
+        in_hbm=(0,),
+        scratch=[pltpu.SemaphoreType.DMA((pieces,))],
+        moved=rows * cols * 4,
+    )
+
+
+def fill(lhs, chunks, second):
+    rows = chunks[0].shape[0]
+    for place, position in enumerate(ORDER):
+        value = chunks[position][...]
+        if second is None:
+            lhs[place * rows : (place + 1) * rows] = value
+        else:
+            lhs[2 * place * rows : (2 * place + 1) * rows] = value
+            lhs[(2 * place + 1) * rows : (2 * place + 2) * rows] = second(position, value)
+
+
+def onto_angles(chunks, table, rate=None):
+    kinds = 1 if rate is None else 2
+    rows = 4 * kinds * chunks[0].shape[0]
+    depth, cols = table.shape
+    step = cols // 4
+
+    def kernel(*refs):
+        parts, rest = refs[:4], refs[4:]
+        if rate is None:
+            tab, keep, send, lhs = rest
+            second = None
+        else:
+            rate_ref, tab, keep, send, lhs = rest
+
+            def second(_, value):
+                return (value.astype(f32) * rate_ref[...]).astype(bf16)
+
+        fill(lhs, parts, second)
+        for i in range(4):
+            cut = slice(i * step, (i + 1) * step)
+            total = jnp.dot(lhs[...], tab[:, cut], preferred_element_type=f32)
+            keep[:, cut] = total[: rows // 2]
+            send[:, cut] = total[rows // 2 :].astype(bf16)
+
+    args = list(chunks) + ([] if rate is None else [rate]) + [table]
+    return call(
+        kernel,
+        (
+            jax.ShapeDtypeStruct((rows // 2, cols), f32),
+            jax.ShapeDtypeStruct((rows // 2, cols), bf16),
+        ),
+        *args,
+        scratch=[pltpu.VMEM((rows, depth), bf16)],
+        flops=2 * rows * depth * cols,
+        moved=rows * cols * 6,
+    )
+
+
+def onto_multipoles(chunks, table, sigma=None, rate=None):
+    kinds = 1 if rate is None else 2
+    count = chunks[0].shape[0]
+    rows = 4 * kinds * count
+    cols, depth = table.shape
+    step = cols // 4
+
+    def kernel(*refs):
+        parts, rest = refs[:4], refs[4:]
+        if rate is None:
+            tab, keep, send, lhs = rest
+            second = None
+        else:
+            sigmas, (rate_ref, tab, keep, send, lhs) = rest[:4], rest[4:]
+
+            def second(position, value):
+                return (-(value.astype(f32) * sigmas[position][...].astype(f32))).astype(bf16)
+
+        fill(lhs, parts, second)
+        for i in range(4):
+            cut = slice(i * step, (i + 1) * step)
+            total = lax.dot_general(
+                tab[cut, :], lhs[...], (((1,), (1,)), ((), ())), preferred_element_type=f32
+            ).T
+            for place in range(4):
+                if rate is None:
+                    value = total[place * count : (place + 1) * count]
+                else:
+                    value = (
+                        total[2 * place * count : (2 * place + 1) * count]
+                        + total[(2 * place + 1) * count : (2 * place + 2) * count]
+                        * rate_ref[:, cut]
+                    )
+                if place < 2:
+                    keep[place * count : (place + 1) * count, cut] = value
+                else:
+                    send[(place - 2) * count : (place - 1) * count, cut] = value.astype(bf16)
+
+    args = list(chunks) + ([] if rate is None else list(sigma) + [rate]) + [table]
+    return call(
+        kernel,
+        (
+            jax.ShapeDtypeStruct((2 * count, cols), f32),
+            jax.ShapeDtypeStruct((2 * count, cols), bf16),
+        ),
+        *args,
+        scratch=[pltpu.VMEM((rows, depth), bf16)],
+        flops=2 * rows * depth * cols,
+        moved=count * cols * 12,
+    )
+
+
+def spectra(hidden, weight):
+    rows, depth = hidden.shape
+    kinds, _, cols = weight.shape
+
+    def kernel(hid, wgt, keep, send):
+        total = jnp.dot(hid[...], wgt[...], preferred_element_type=f32)
+        keep[...] = total[: rows // 2]
+        send[...] = total[rows // 2 :].astype(bf16)
+
+    out = pl.BlockSpec((None, rows // 2, cols), lambda s: (s, 0, 0))
+    return pl.pallas_call(
+        kernel,
+        grid=(kinds,),
+        out_shape=(
+            jax.ShapeDtypeStruct((kinds, rows // 2, cols), f32),
+            jax.ShapeDtypeStruct((kinds, rows // 2, cols), bf16),
+        ),
+        in_specs=[
+            pl.BlockSpec((rows, depth), lambda s: (0, 0)),
+            pl.BlockSpec((None, depth, cols), lambda s: (s, 0, 0)),
+        ],
+        out_specs=(out, out),
+        compiler_params=pltpu.CompilerParams(vmem_limit_bytes=12 << 20),
+    )(hidden, weight)
+
+
+def adam(hidden, log_grad, weight, first, second):
+    rows, depth = hidden.shape
+    kinds, _, cols = weight.shape
+    tile = depth // 2
+
+    def kernel(hid, grad, wgt, one, two, new_wgt, new_one, new_two):
+        slope = lax.dot_general(
+            hid[...], grad[...], (((0,), (0,)), ((), ())), preferred_element_type=f32
+        )
+        moved = 0.9 * one[...] + 0.1 * slope
+        spread = 0.999 * two[...] + 0.001 * slope * slope
+        new_one[...] = moved
+        new_two[...] = spread
+        update = moved * (1.0 / first_fix) / (jnp.sqrt(spread * (1.0 / second_fix)) + 1e-08)
+        new_wgt[...] = (wgt[...].astype(f32) - 0.001 * update).astype(bf16)
+
+    block = pl.BlockSpec((None, tile, cols), lambda s, i: (s, i, 0))
+    return pl.pallas_call(
+        kernel,
+        grid=(kinds, depth // tile),
+        out_shape=(
+            jax.ShapeDtypeStruct(weight.shape, bf16),
+            jax.ShapeDtypeStruct(weight.shape, f32),
+            jax.ShapeDtypeStruct(weight.shape, f32),
+        ),
+        in_specs=[
+            pl.BlockSpec((rows, tile), lambda s, i: (0, i)),
+            pl.BlockSpec((None, rows, cols), lambda s, i: (s, 0, 0)),
+            block,
+            block,
+            block,
+        ],
+        out_specs=(block, block, block),
+        compiler_params=pltpu.CompilerParams(vmem_limit_bytes=24 << 20),
+    )(hidden, log_grad, weight, first, second)
+
+
+def local_fast(hidden_act, weight, first_moment, second_moment, wigner, quad_weight, target):
+    count = hidden_act.shape[0] // 4
+    h_local = weight.shape[1]
+    l_local = weight.shape[2]
+    at_ell = lax.axis_index("ell")
+    at_batch = lax.axis_index("batch")
+    chunk = jnp.bitwise_xor(at_ell, at_batch)
+    multipole = (at_ell * l_local + lax.iota(jnp.int32, l_local)).astype(f32)[None]
+    lens_rate = multipole * (multipole + 1.0) / (float(L) * float(L))
+    loss_weight = (1.0 + 2.0 * multipole / float(L)) / hidden_act.shape[0]
+    quad = quad_weight[None]
+    own_hidden = jnp.concatenate(
+        [
+            lax.dynamic_slice(
+                hidden_act,
+                (jnp.bitwise_xor(chunk, position) * count, at_batch * h_local),
+                (count, h_local),
+            )
+            for position in ORDER
+        ]
+    )
+    own_target = lax.dynamic_slice_in_dim(target, chunk * count, count, 1).astype(f32)
+
+    keep, send = spectra(own_hidden, weight)
+    table = {t: fetch_table(wigner, t) for t in (3, 0, 2, 1)}
+    log_power = {s: scatter(keep[s], send[s], "batch") for s in (3, 0, 2, 1)}
+    power_lens = jnp.exp(log_power[3])
+    power_temp = jnp.exp(log_power[0])
+    power_pol = jnp.exp(log_power[2])
+    cross_scale = jnp.exp(0.5 * (log_power[0] + log_power[2]))
+    cross_ratio = jnp.tanh(log_power[1])
+    power_cross = cross_ratio * cross_scale
+
+    def sums_of(power, t, rate):
+        return scatter(*onto_angles(gather(power.astype(bf16), "batch"), table[t], rate), "ell")
+
+    sigma = sums_of(power_lens, 3, None)
+    all_sigma = gather(sigma.astype(bf16), "ell")
+    corr_grad = {}
+    second_sum = {}
+    for x, power in ((0, power_temp), (2, power_pol), (1, power_cross)):
+        sums = sums_of(power, x, lens_rate)
+        first_sum, second_sum[x] = sums[:count], sums[count:]
+        back_row = ((first_sum - sigma * second_sum[x]) * quad).astype(bf16)
+        lensed = scatter(*onto_multipoles(gather(back_row, "ell"), table[x]), "batch")
+        residual = (loss_weight * (lensed - own_target[x])).astype(bf16)
+        corr_grad[x] = scatter(*onto_angles(gather(residual, "batch"), table[x]), "ell") * quad
+
+    coef = {}
+    for x in (0, 2, 1):
+        coef[x] = scatter(
+            *onto_multipoles(
+                gather(corr_grad[x].astype(bf16), "ell"), table[x], all_sigma, lens_rate
+            ),
+            "batch",
+        )
+    sigma_grad = -sum(corr_grad[x] * second_sum[x] for x in range(3))
+    coef[3] = scatter(
+        *onto_multipoles(gather(sigma_grad.astype(bf16), "ell"), table[3]), "batch"
+    )
+    half_cross = 0.5 * coef[1] * power_cross
+    log_grad = (
+        coef[0] * power_temp + half_cross,
+        coef[1] * (1.0 - cross_ratio * cross_ratio) * cross_scale,
+        coef[2] * power_pol + half_cross,
+        coef[3] * power_lens,
+    )
+    log_grad = [gather(value.astype(bf16), "batch") for value in log_grad]
+    log_grad = jnp.stack(
+        [jnp.concatenate([value[position] for position in ORDER]) for value in log_grad]
+    )
+    return adam(own_hidden, log_grad, weight, first_moment, second_moment)
+
+
 def solution(mesh):
+    four = mesh.shape["ell"] == 4 and mesh.shape["batch"] == 4
     return jax.shard_map(
-        local,
+        local_fast if four else local_plain,
         mesh=mesh,
         in_specs=(
             P("groups", None),

time: 411 us -> 205 us (0.50)
  waiting for transfers between devices: 231 us -> 62.6 us
  matrix products: 94.9 us -> 0 us
  starting transfers between devices: 0.61 us -> 75.9 us
  Pallas kernels: 0 us -> 41.9 us
  local copies, waits for them, and re-layouts: 51.4 us -> 20.5 us
  other arithmetic: 16.9 us -> 2.41 us
  between operations: 14 us -> 1.4 us
    psum x5 -> x0, waiting for transfers between devices: 231 us -> none  [the longest x2 121 us: angle_reduce(): lax.psum(partial_value.astype(jnp.bfloat16), 'ell').astype(jnp.float32)]
    dot_general x16 -> x0, matrix products: 94.9 us -> none  [the longest x3 18.8 us: backward_terms(): jnp.einsum('rca,la->rcl', piece[2 * table:2 * table + 2], tables[table],...]
    ppermute x0 -> x93, starting transfers between devices: none -> 75.9 us  [swap(): return lax.ppermute(value, axis, [(i, i ^ mask) for i in range(count)])]
    ppermute x0 -> x93, waiting for transfers between devices: none -> 62.6 us  [swap(): return lax.ppermute(value, axis, [(i, i ^ mask) for i in range(count)])]
    pallas_call x0 -> x20, Pallas kernels: none -> 41.9 us  [the longest x18 29.9 us: call(): pl.pallas_call(kernel, out_shape=out_shape, in_specs=[hbm if i in in_hbm...]
    unnamed x18 -> x26, local copies, waits for them, and re-layouts: 51.3 us -> 19.6 us
    another operation x6 -> x5, other arithmetic: 5.59 us -> 0.21 us  [local_fast(): jnp.stack([jnp.concatenate([value[position] for position in ORDER]) for v...]
    convert_element_type x4 -> x8, other arithmetic: 5.74 us -> 1.51 us  [the longest x1 0.97 us: local_fast(): lax.dynamic_slice_in_dim(target, chunk * count, count, 1).astype(f32)]
  transfers between devices with their start and end apart: 5 -> 93, of which waited for: 5 -> 37; matrix products, arithmetic and copies ran while one was open for 6% -> 1% of each run, Pallas kernels for 0% -> 15%
where the time goes in v1:
time: 205 us
  starting transfers between devices  75.9 us (37%)
  waiting for transfers between devices  62.6 us (31%)
  Pallas kernels  41.9 us (20%)
  local copies, waits for them, and re-layouts  20.5 us (10%)
  other arithmetic  2.41 us (1%)
    ppermute x93, starting transfers between devices, swap(): return lax.ppermute(value, axis, [(i, i ^ mask) for i in range(count)])  75.9 us
    ppermute x93, waiting for transfers between devices, swap(): return lax.ppermute(value, axis, [(i, i ^ mask) for i in range(count)])  62.6 us
    pallas_call x18, Pallas kernels, call(): pl.pallas_call(kernel, out_shape=out_shape, in_specs=[hbm if i in in_hbm...  29.9 us
    unnamed x26, local copies, waits for them, and re-layouts  19.6 us
    pallas_call x1, Pallas kernels, adam(): pl.pallas_call(kernel, grid=(kinds, depth // tile), out_shape=(jax.ShapeD...  10.8 us
  transfers between devices with their start and end apart: 93, of which 37 were waited for; matrix products, arithmetic and copies ran while one was open for 1% of the time, Pallas kernels for 15%

profile of v1, /device:TPU:0, one launch (start us, length us, event | category | flops | bytes accessed | tf_op | source)
XLA Modules:
  0.0 204.8 jit_solution(11929868788348248537)
XLA Ops:
  7.4 2.7 %collective-permute-start.1 = (bf16[16,2048]{1,0:T(8,128)(2,1)S(1)}, bf16[16,2048]{1,0:T(8,128)(2,1)S(1)}, u32[]{:S(2)}, u32[]{:S(2)}) collective-permute-start(bf16[16,2048]{1,0:T(8,128)(2,1)S(1)} %slice.462), channel_id=1, source_target_pairs={{0,2},{1,3},{2,0},{3,1},{4,6},{5,7},{6,4},{7,5},{8,10},{9,11},{10,... | collective-permute-start | bytes 196616 | tf_op jit(solution)/shard_map/ppermute | solution.py:165
  12.7 2.4 %collective-permute-done.33 = bf16[16,2048]{1,0:T(8,128)(2,1)S(1)} collective-permute-done((bf16[16,2048]{1,0:T(8,128)(2,1)S(1)}, bf16[16,2048]{1,0:T(8,128)(2,1)S(1)}, u32[]{:S(2)}, u32[]{:S(2)}) %collective-permute-start.33) | collective-permute-done | bytes 65568 | tf_op jit(solution)/shard_map/ppermute | solution.py:165
  20.8 10.5 %copy-done = bf16[4,2048,2048]{2,1,0:T(8,128)(2,1)S(1)} copy-done((bf16[4,2048,2048]{2,1,0:T(8,128)(2,1)S(1)}, bf16[4,2048,2048]{2,1,0:T(8,128)(2,1)}, u32[]{:S(2)}) %copy-start) | copy-done | bytes 33554456
  32.7 3.4 %copy-done.1 = bf16[2048,2048]{1,0:T(8,128)(2,1)} copy-done((bf16[2048,2048]{1,0:T(8,128)(2,1)}, bf16[2048,2048]{1,0:T(8,128)(2,1)S(1)}, u32[]{:S(2)}) %copy-start.1) | copy-done | bytes 8388632
  36.7 3.4 %copy-done.2 = bf16[2048,2048]{1,0:T(8,128)(2,1)} copy-done((bf16[2048,2048]{1,0:T(8,128)(2,1)}, bf16[2048,2048]{1,0:T(8,128)(2,1)S(1)}, u32[]{:S(2)}) %copy-start.2) | copy-done | bytes 8388632
  54.9 3.5 %collective-permute-done.12 = bf16[32,2048]{1,0:T(8,128)(2,1)S(1)} collective-permute-done((bf16[32,2048]{1,0:T(8,128)(2,1)S(1)}, bf16[32,2048]{1,0:T(8,128)(2,1)S(1)}, u32[]{:S(2)}, u32[]{:S(2)}) %collective-permute-start.12) | collective-permute-done | bytes 131104 | tf_op jit(solution)/shard_map/ppermute | solution.py:165
  58.4 2.5 %collective-permute-start.13 = (bf16[16,2048]{1,0:T(8,128)(2,1)S(1)}, bf16[16,2048]{1,0:T(8,128)(2,1)S(1)}, u32[]{:S(2)}, u32[]{:S(2)}) collective-permute-start(bf16[16,2048]{1,0:T(8,128)(2,1)S(1)} %slice.460), channel_id=1, source_target_pairs={{0,8},{4,12},{8,0},{12,4},{1,9},{5,13},{9,1},{13,5},{2,10},{6,14},... | collective-permute-start | bytes 196616 | tf_op jit(solution)/shard_map/ppermute | solution.py:165
  61.5 6.6 %collective-permute-done.39 = bf16[64,2048]{1,0:T(8,128)(2,1)S(1)} collective-permute-done((bf16[64,2048]{1,0:T(8,128)(2,1)S(1)}, bf16[64,2048]{1,0:T(8,128)(2,1)S(1)}, u32[]{:S(2)}, u32[]{:S(2)}) %collective-permute-start.39) | collective-permute-done | bytes 262176 | tf_op jit(solution)/shard_map/ppermute | solution.py:165
  69.9 3.8 %collective-permute-done.65 = bf16[64,2048]{1,0:T(8,128)(2,1)S(1)} collective-permute-done((bf16[64,2048]{1,0:T(8,128)(2,1)S(1)}, bf16[64,2048]{1,0:T(8,128)(2,1)S(1)}, u32[]{:S(2)}, u32[]{:S(2)}) %collective-permute-start.65) | collective-permute-done | bytes 262176 | tf_op jit(solution)/shard_map/ppermute | solution.py:165
  75.3 8.6 %collective-permute-done.40 = bf16[32,2048]{1,0:T(8,128)(2,1)S(1)} collective-permute-done((bf16[32,2048]{1,0:T(8,128)(2,1)S(1)}, bf16[32,2048]{1,0:T(8,128)(2,1)S(1)}, u32[]{:S(2)}, u32[]{:S(2)}) %collective-permute-start.40) | collective-permute-done | bytes 131104 | tf_op jit(solution)/shard_map/ppermute | solution.py:165
  83.9 2.5 %collective-permute-done.66 = bf16[32,2048]{1,0:T(8,128)(2,1)S(1)} collective-permute-done((bf16[32,2048]{1,0:T(8,128)(2,1)S(1)}, bf16[32,2048]{1,0:T(8,128)(2,1)S(1)}, u32[]{:S(2)}, u32[]{:S(2)}) %collective-permute-start.66) | collective-permute-done | bytes 131104 | tf_op jit(solution)/shard_map/ppermute | solution.py:165
  98.7 2.4 %shard_map.99 = (f32[32,2048]{1,0:T(8,128)S(1)}, bf16[32,2048]{1,0:T(8,128)(2,1)S(1)}) custom-call(bf16[16,2048]{1,0:T(8,128)(2,1)S(1)} %get-tuple-element.85.refs_0_, bf16[16,2048]{1,0:T(8,128)(2,1)S(1)} %collective-permute-done.14.refs_1_, bf16[16,2048]{1,0:T(8,128)(2,1)S(1)} %collective-permute-done.15.refs_2_, ...), custom_call_target="tpu_custom_call" | custom-call | flops 536870912 | bytes 393216 | tf_op jit(solution)/shard_map/pallas_call | solution.py:183
  105.1 2.4 %shard_map.109 = (f32[32,2048]{1,0:T(8,128)S(1)}, bf16[32,2048]{1,0:T(8,128)(2,1)S(1)}) custom-call(bf16[16,2048]{1,0:T(8,128)(2,1)S(1)} %get-tuple-element.83.refs_0_, bf16[16,2048]{1,0:T(8,128)(2,1)S(1)} %collective-permute-done.67.refs_1_, bf16[16,2048]{1,0:T(8,128)(2,1)S(1)} %collective-permute-done.68.refs_2_, ...), custom_call_target="tpu_custom_call" | custom-call | flops 536870912 | bytes 393216 | tf_op jit(solution)/shard_map/pallas_call | solution.py:183
  117.5 2.9 %collective-permute-done.47.refs_2_ = bf16[16,2048]{1,0:T(8,128)(2,1)S(1)} collective-permute-done((bf16[16,2048]{1,0:T(8,128)(2,1)S(1)}, bf16[16,2048]{1,0:T(8,128)(2,1)S(1)}, u32[]{:S(2)}, u32[]{:S(2)}) %collective-permute-start.47) | collective-permute-done | bytes 65568 | tf_op jit(solution)/shard_map/ppermute | solution.py:165
  134.9 2.8 %collective-permute-done.22 = bf16[32,2048]{1,0:T(8,128)(2,1)S(1)} collective-permute-done((bf16[32,2048]{1,0:T(8,128)(2,1)S(1)}, bf16[32,2048]{1,0:T(8,128)(2,1)S(1)}, u32[]{:S(2)}, u32[]{:S(2)}) %collective-permute-start.22) | collective-permute-done | bytes 131104 | tf_op jit(solution)/shard_map/ppermute | solution.py:165
  137.8 2.9 %collective-permute-start.28 = (bf16[16,2048]{1,0:T(8,128)(2,1)S(1)}, bf16[16,2048]{1,0:T(8,128)(2,1)S(1)}, u32[]{:S(2)}, u32[]{:S(2)}) collective-permute-start(bf16[16,2048]{1,0:T(8,128)(2,1)S(1)} %get-tuple-element.86.refs_4_), channel_id=1, source_target_pairs={{0,8},{4,12},{8,0},{12,4},{1,9},{5,13},{9,1},{13,5},{2,10},{6,14},... | collective-permute-start | bytes 196616 | tf_op jit(solution)/shard_map/ppermute | solution.py:165
  141.1 3.9 %collective-permute-done.23 = bf16[16,2048]{1,0:T(8,128)(2,1)S(1)} collective-permute-done((bf16[16,2048]{1,0:T(8,128)(2,1)S(1)}, bf16[16,2048]{1,0:T(8,128)(2,1)S(1)}, u32[]{:S(2)}, u32[]{:S(2)}) %collective-permute-start.23) | collective-permute-done | bytes 65568 | tf_op jit(solution)/shard_map/ppermute | solution.py:165
  145.1 2.5 %collective-permute-start.27 = (bf16[16,2048]{1,0:T(8,128)(2,1)S(1)}, bf16[16,2048]{1,0:T(8,128)(2,1)S(1)}, u32[]{:S(2)}, u32[]{:S(2)}) collective-permute-start(bf16[16,2048]{1,0:T(8,128)(2,1)S(1)} %get-tuple-element.86.refs_4_), channel_id=1, source_target_pairs={{0,4},{4,0},{8,12},{12,8},{1,5},{5,1},{9,13},{13,9},{2,6},{6,2},{1... | collective-permute-start | bytes 196616 | tf_op jit(solution)/shard_map/ppermute | solution.py:165
  159.0 2.4 %shard_map.111 = (f32[32,2048]{1,0:T(8,128)S(1)}, bf16[32,2048]{1,0:T(8,128)(2,1)S(1)}) custom-call(bf16[16,2048]{1,0:T(8,128)(2,1)S(1)} %get-tuple-element.82.refs_0_, bf16[16,2048]{1,0:T(8,128)(2,1)S(1)} %collective-permute-done.77.refs_1_, bf16[16,2048]{1,0:T(8,128)(2,1)S(1)} %collective-permute-done.78.refs_2_, ...), custom_call_target="tpu_custom_call" | custom-call | flops 1073741824 | bytes 393216 | tf_op jit(solution)/shard_map/pallas_call | solution.py:183
  165.4 2.4 %shard_map.106 = (f32[32,2048]{1,0:T(8,128)S(1)}, bf16[32,2048]{1,0:T(8,128)(2,1)S(1)}) custom-call(bf16[16,2048]{1,0:T(8,128)(2,1)S(1)} %get-tuple-element.81.refs_0_, bf16[16,2048]{1,0:T(8,128)(2,1)S(1)} %collective-permute-done.51.refs_1_, bf16[16,2048]{1,0:T(8,128)(2,1)S(1)} %collective-permute-done.52.refs_2_, ...), custom_call_target="tpu_custom_call" | custom-call | flops 1073741824 | bytes 393216 | tf_op jit(solution)/shard_map/pallas_call | solution.py:183
  168.4 2.4 %shard_map.101 = (f32[32,2048]{1,0:T(8,128)S(1)}, bf16[32,2048]{1,0:T(8,128)(2,1)S(1)}) custom-call(bf16[16,2048]{1,0:T(8,128)(2,1)S(1)} %get-tuple-element.79.refs_0_, bf16[16,2048]{1,0:T(8,128)(2,1)S(1)} %collective-permute-done.24.refs_1_, bf16[16,2048]{1,0:T(8,128)(2,1)S(1)} %collective-permute-done.25.refs_2_, ...), custom_call_target="tpu_custom_call" | custom-call | flops 1073741824 | bytes 393216 | tf_op jit(solution)/shard_map/pallas_call | solution.py:183
  171.0 2.7 %shard_map.112 = (f32[32,2048]{1,0:T(8,128)S(1)}, bf16[32,2048]{1,0:T(8,128)(2,1)S(1)}) custom-call(bf16[16,2048]{1,0:T(8,128)(2,1)S(1)} %get-tuple-element.80.refs_0_, bf16[16,2048]{1,0:T(8,128)(2,1)S(1)} %collective-permute-done.85.refs_1_, bf16[16,2048]{1,0:T(8,128)(2,1)S(1)} %collective-permute-done.86.refs_2_, ...), custom_call_target="tpu_custom_call" | custom-call | flops 536870912 | bytes 393216 | tf_op jit(solution)/shard_map/pallas_call | solution.py:183
  190.0 2.5 %collective-permute-done.90 = bf16[16,2048]{1,0:T(8,128)(2,1)S(1)} collective-permute-done((bf16[16,2048]{1,0:T(8,128)(2,1)S(1)}, bf16[16,2048]{1,0:T(8,128)(2,1)S(1)}, u32[]{:S(2)}, u32[]{:S(2)}) %collective-permute-start.90) | collective-permute-done | bytes 65568 | tf_op jit(solution)/shard_map/ppermute | solution.py:165
  194.0 10.8 %shard_map.113 = (bf16[4,256,2048]{2,1,0:T(8,128)(2,1)}, f32[4,256,2048]{2,1,0:T(8,128)}, f32[4,256,2048]{2,1,0:T(8,128)}) custom-call(bf16[64,256]{1,0:T(8,128)(2,1)S(1)} %pad_maximum_fusion.1.hid, bf16[4,64,2048]{2,1,0:T(8,128)(2,1)S(1)} %pad_maximum_fusion.grad, bf16[4,256,2048]{2,1,0:T(8,128)(2,1)S(1)} %copy-done.5, f32[4,256,2048]{2,1,0:T(8,128)S(1)} %bitcast.51, ...), custom_call_target="tpu_custom_call" | custom-call | tf_op jit(solution)/shard_map/pallas_call | solution.py:365
  (265 shorter events, 110.4 us)
Async XLA Ops:
  18.0 23.5 %collective-permute-start.2 = (bf16[16,2048]{1,0:T(8,128)(2,1)S(1)}, bf16[16,2048]{1,0:T(8,128)(2,1)S(1)}, u32[]{:S(2)}, u32[]{:S(2)}) collective-permute-start(bf16[16,2048]{1,0:T(8,128)(2,1)S(1)} %get-tuple-element.87.refs_0_), channel_id=1, source_target_pairs={{0,1},{1,0},{2,3},{3,2},{4,5},{5,4},{6,7},{7,6},{8,9},{9,8},{10,11... | collective-permute-start | bytes 196616 | tf_op jit(solution)/shard_map/ppermute | solution.py:165
  18.0 23.6 %collective-permute-start.37 = (bf16[16,2048]{1,0:T(8,128)(2,1)S(1)}, bf16[16,2048]{1,0:T(8,128)(2,1)S(1)}, u32[]{:S(2)}, u32[]{:S(2)}) collective-permute-start(bf16[16,2048]{1,0:T(8,128)(2,1)S(1)} %get-tuple-element.63.refs_0_), channel_id=1, source_target_pairs={{0,2},{1,3},{2,0},{3,1},{4,6},{5,7},{6,4},{7,5},{8,10},{9,11},{10,... | collective-permute-start | bytes 196616 | tf_op jit(solution)/shard_map/ppermute | solution.py:165
  18.6 25.2 %collective-permute-start.10 = (bf16[16,2048]{1,0:T(8,128)(2,1)S(1)}, bf16[16,2048]{1,0:T(8,128)(2,1)S(1)}, u32[]{:S(2)}, u32[]{:S(2)}) collective-permute-start(bf16[16,2048]{1,0:T(8,128)(2,1)S(1)} %fusion.28.refs_0_), channel_id=1, source_target_pairs={{0,2},{1,3},{2,0},{3,1},{4,6},{5,7},{6,4},{7,5},{8,10},{9,11},{10,... | collective-permute-start | bytes 196616 | tf_op jit(solution)/shard_map/ppermute | solution.py:165
  20.8 23.1 %collective-permute-start.4 = (bf16[16,2048]{1,0:T(8,128)(2,1)S(1)}, bf16[16,2048]{1,0:T(8,128)(2,1)S(1)}, u32[]{:S(2)}, u32[]{:S(2)}) collective-permute-start(bf16[16,2048]{1,0:T(8,128)(2,1)S(1)} %collective-permute-done.3.refs_2_), channel_id=1, source_target_pairs={{0,1},{1,0},{2,3},{3,2},{4,5},{5,4},{6,7},{7,6},{8,9},{9,8},{10,11... | collective-permute-start | bytes 196616 | tf_op jit(solution)/shard_map/ppermute | solution.py:165
  41.0 8.5 %collective-permute-start.36 = (bf16[16,2048]{1,0:T(8,128)(2,1)S(1)}, bf16[16,2048]{1,0:T(8,128)(2,1)S(1)}, u32[]{:S(2)}, u32[]{:S(2)}) collective-permute-start(bf16[16,2048]{1,0:T(8,128)(2,1)S(1)} %get-tuple-element.63.refs_0_), channel_id=1, source_target_pairs={{0,1},{1,0},{2,3},{3,2},{4,5},{5,4},{6,7},{7,6},{8,9},{9,8},{10,11... | collective-permute-start | bytes 196616 | tf_op jit(solution)/shard_map/ppermute | solution.py:165
  46.4 14.5 %collective-permute-start.5 = (bf16[64,2048]{1,0:T(8,128)(2,1)S(1)}, bf16[64,2048]{1,0:T(8,128)(2,1)S(1)}, u32[]{:S(2)}, u32[]{:S(2)}) collective-permute-start(bf16[64,2048]{1,0:T(8,128)(2,1)S(1)} %get-tuple-element.36), channel_id=1, source_target_pairs={{0,4},{4,0},{8,12},{12,8},{1,5},{5,1},{9,13},{13,9},{2,6},{6,2},{1... | collective-permute-start | bytes 786440 | tf_op jit(solution)/shard_map/ppermute | solution.py:165
  49.5 8.9 %collective-permute-start.12 = (bf16[32,2048]{1,0:T(8,128)(2,1)S(1)}, bf16[32,2048]{1,0:T(8,128)(2,1)S(1)}, u32[]{:S(2)}, u32[]{:S(2)}) collective-permute-start(bf16[32,2048]{1,0:T(8,128)(2,1)S(1)} %get-tuple-element.38), channel_id=1, source_target_pairs={{0,4},{4,0},{8,12},{12,8},{1,5},{5,1},{9,13},{13,9},{2,6},{6,2},{1... | collective-permute-start | bytes 393224 | tf_op jit(solution)/shard_map/ppermute | solution.py:165
  51.4 16.7 %collective-permute-start.39 = (bf16[64,2048]{1,0:T(8,128)(2,1)S(1)}, bf16[64,2048]{1,0:T(8,128)(2,1)S(1)}, u32[]{:S(2)}, u32[]{:S(2)}) collective-permute-start(bf16[64,2048]{1,0:T(8,128)(2,1)S(1)} %get-tuple-element.46), channel_id=1, source_target_pairs={{0,4},{4,0},{8,12},{12,8},{1,5},{5,1},{9,13},{13,9},{2,6},{6,2},{1... | collective-permute-start | bytes 786440 | tf_op jit(solution)/shard_map/ppermute | solution.py:165
  54.2 19.4 %collective-permute-start.65 = (bf16[64,2048]{1,0:T(8,128)(2,1)S(1)}, bf16[64,2048]{1,0:T(8,128)(2,1)S(1)}, u32[]{:S(2)}, u32[]{:S(2)}) collective-permute-start(bf16[64,2048]{1,0:T(8,128)(2,1)S(1)} %get-tuple-element.54), channel_id=1, source_target_pairs={{0,4},{4,0},{8,12},{12,8},{1,5},{5,1},{9,13},{13,9},{2,6},{6,2},{1... | collective-permute-start | bytes 786440 | tf_op jit(solution)/shard_map/ppermute | solution.py:165
  58.4 28.0 %collective-permute-start.13 = (bf16[16,2048]{1,0:T(8,128)(2,1)S(1)}, bf16[16,2048]{1,0:T(8,128)(2,1)S(1)}, u32[]{:S(2)}, u32[]{:S(2)}) collective-permute-start(bf16[16,2048]{1,0:T(8,128)(2,1)S(1)} %slice.460), channel_id=1, source_target_pairs={{0,8},{4,12},{8,0},{12,4},{1,9},{5,13},{9,1},{13,5},{2,10},{6,14},... | collective-permute-start | bytes 196616 | tf_op jit(solution)/shard_map/ppermute | solution.py:165
  61.0 14.2 %collective-permute-start.6 = (bf16[32,2048]{1,0:T(8,128)(2,1)S(1)}, bf16[32,2048]{1,0:T(8,128)(2,1)S(1)}, u32[]{:S(2)}, u32[]{:S(2)}) collective-permute-start(bf16[32,2048]{1,0:T(8,128)(2,1)S(1)} %slice.447), channel_id=1, source_target_pairs={{0,8},{4,12},{8,0},{12,4},{1,9},{5,13},{9,1},{13,5},{2,10},{6,14},... | collective-permute-start | bytes 393224 | tf_op jit(solution)/shard_map/ppermute | solution.py:165
  68.3 15.6 %collective-permute-start.40 = (bf16[32,2048]{1,0:T(8,128)(2,1)S(1)}, bf16[32,2048]{1,0:T(8,128)(2,1)S(1)}, u32[]{:S(2)}, u32[]{:S(2)}) collective-permute-start(bf16[32,2048]{1,0:T(8,128)(2,1)S(1)} %slice.446), channel_id=1, source_target_pairs={{0,8},{4,12},{8,0},{12,4},{1,9},{5,13},{9,1},{13,5},{2,10},{6,14},... | collective-permute-start | bytes 393224 | tf_op jit(solution)/shard_map/ppermute | solution.py:165
  73.8 12.6 %collective-permute-start.66 = (bf16[32,2048]{1,0:T(8,128)(2,1)S(1)}, bf16[32,2048]{1,0:T(8,128)(2,1)S(1)}, u32[]{:S(2)}, u32[]{:S(2)}) collective-permute-start(bf16[32,2048]{1,0:T(8,128)(2,1)S(1)} %slice.445), channel_id=1, source_target_pairs={{0,8},{4,12},{8,0},{12,4},{1,9},{5,13},{9,1},{13,5},{2,10},{6,14},... | collective-permute-start | bytes 393224 | tf_op jit(solution)/shard_map/ppermute | solution.py:165
  92.8 9.3 %collective-permute-start.41 = (bf16[16,2048]{1,0:T(8,128)(2,1)S(1)}, bf16[16,2048]{1,0:T(8,128)(2,1)S(1)}, u32[]{:S(2)}, u32[]{:S(2)}) collective-permute-start(bf16[16,2048]{1,0:T(8,128)(2,1)S(1)} %get-tuple-element.84.refs_0_), channel_id=1, source_target_pairs={{0,4},{4,0},{8,12},{12,8},{1,5},{5,1},{9,13},{13,9},{2,6},{6,2},{1... | collective-permute-start | bytes 196616 | tf_op jit(solution)/shard_map/ppermute | solution.py:165
  94.8 10.3 %collective-permute-start.67 = (bf16[16,2048]{1,0:T(8,128)(2,1)S(1)}, bf16[16,2048]{1,0:T(8,128)(2,1)S(1)}, u32[]{:S(2)}, u32[]{:S(2)}) collective-permute-start(bf16[16,2048]{1,0:T(8,128)(2,1)S(1)} %get-tuple-element.83.refs_0_), channel_id=1, source_target_pairs={{0,4},{4,0},{8,12},{12,8},{1,5},{5,1},{9,13},{13,9},{2,6},{6,2},{1... | collective-permute-start | bytes 196616 | tf_op jit(solution)/shard_map/ppermute | solution.py:165
  129.4 8.3 %collective-permute-start.22 = (bf16[32,2048]{1,0:T(8,128)(2,1)S(1)}, bf16[32,2048]{1,0:T(8,128)(2,1)S(1)}, u32[]{:S(2)}, u32[]{:S(2)}) collective-permute-start(bf16[32,2048]{1,0:T(8,128)(2,1)S(1)} %get-tuple-element.42), channel_id=1, source_target_pairs={{0,4},{4,0},{8,12},{12,8},{1,5},{5,1},{9,13},{13,9},{2,6},{6,2},{1... | collective-permute-start | bytes 393224 | tf_op jit(solution)/shard_map/ppermute | solution.py:165
  130.6 10.1 %collective-permute-start.50 = (bf16[16,2048]{1,0:T(8,128)(2,1)S(1)}, bf16[16,2048]{1,0:T(8,128)(2,1)S(1)}, u32[]{:S(2)}, u32[]{:S(2)}) collective-permute-start(bf16[16,2048]{1,0:T(8,128)(2,1)S(1)} %slice.453), channel_id=1, source_target_pairs={{0,8},{4,12},{8,0},{12,4},{1,9},{5,13},{9,1},{13,5},{2,10},{6,14},... | collective-permute-start | bytes 196616 | tf_op jit(solution)/shard_map/ppermute | solution.py:165
  137.8 9.8 %collective-permute-start.28 = (bf16[16,2048]{1,0:T(8,128)(2,1)S(1)}, bf16[16,2048]{1,0:T(8,128)(2,1)S(1)}, u32[]{:S(2)}, u32[]{:S(2)}) collective-permute-start(bf16[16,2048]{1,0:T(8,128)(2,1)S(1)} %get-tuple-element.86.refs_4_), channel_id=1, source_target_pairs={{0,8},{4,12},{8,0},{12,4},{1,9},{5,13},{9,1},{13,5},{2,10},{6,14},... | collective-permute-start | bytes 196616 | tf_op jit(solution)/shard_map/ppermute | solution.py:165
  147.7 8.8 %collective-permute-start.77 = (bf16[16,2048]{1,0:T(8,128)(2,1)S(1)}, bf16[16,2048]{1,0:T(8,128)(2,1)S(1)}, u32[]{:S(2)}, u32[]{:S(2)}) collective-permute-start(bf16[16,2048]{1,0:T(8,128)(2,1)S(1)} %get-tuple-element.82.refs_0_), channel_id=1, source_target_pairs={{0,4},{4,0},{8,12},{12,8},{1,5},{5,1},{9,13},{13,9},{2,6},{6,2},{1... | collective-permute-start | bytes 196616 | tf_op jit(solution)/shard_map/ppermute | solution.py:165
  152.1 9.3 %collective-permute-start.51 = (bf16[16,2048]{1,0:T(8,128)(2,1)S(1)}, bf16[16,2048]{1,0:T(8,128)(2,1)S(1)}, u32[]{:S(2)}, u32[]{:S(2)}) collective-permute-start(bf16[16,2048]{1,0:T(8,128)(2,1)S(1)} %get-tuple-element.81.refs_0_), channel_id=1, source_target_pairs={{0,4},{4,0},{8,12},{12,8},{1,5},{5,1},{9,13},{13,9},{2,6},{6,2},{1... | collective-permute-start | bytes 196616 | tf_op jit(solution)/shard_map/ppermute | solution.py:165
  154.1 9.3 %collective-permute-start.25 = (bf16[16,2048]{1,0:T(8,128)(2,1)S(1)}, bf16[16,2048]{1,0:T(8,128)(2,1)S(1)}, u32[]{:S(2)}, u32[]{:S(2)}) collective-permute-start(bf16[16,2048]{1,0:T(8,128)(2,1)S(1)} %get-tuple-element.79.refs_0_), channel_id=1, source_target_pairs={{0,8},{4,12},{8,0},{12,4},{1,9},{5,13},{9,1},{13,5},{2,10},{6,14},... | collective-permute-start | bytes 196616 | tf_op jit(solution)/shard_map/ppermute | solution.py:165
  156.5 11.3 %collective-permute-start.24 = (bf16[16,2048]{1,0:T(8,128)(2,1)S(1)}, bf16[16,2048]{1,0:T(8,128)(2,1)S(1)}, u32[]{:S(2)}, u32[]{:S(2)}) collective-permute-start(bf16[16,2048]{1,0:T(8,128)(2,1)S(1)} %get-tuple-element.79.refs_0_), channel_id=1, source_target_pairs={{0,4},{4,0},{8,12},{12,8},{1,5},{5,1},{9,13},{13,9},{2,6},{6,2},{1... | collective-permute-start | bytes 196616 | tf_op jit(solution)/shard_map/ppermute | solution.py:165
  161.5 9.5 %collective-permute-start.85 = (bf16[16,2048]{1,0:T(8,128)(2,1)S(1)}, bf16[16,2048]{1,0:T(8,128)(2,1)S(1)}, u32[]{:S(2)}, u32[]{:S(2)}) collective-permute-start(bf16[16,2048]{1,0:T(8,128)(2,1)S(1)} %get-tuple-element.80.refs_0_), channel_id=1, source_target_pairs={{0,4},{4,0},{8,12},{12,8},{1,5},{5,1},{9,13},{13,9},{2,6},{6,2},{1... | collective-permute-start | bytes 196616 | tf_op jit(solution)/shard_map/ppermute | solution.py:165
  165.4 8.8 %collective-permute-start.80 = (bf16[32,2048]{1,0:T(8,128)(2,1)S(1)}, bf16[32,2048]{1,0:T(8,128)(2,1)S(1)}, u32[]{:S(2)}, u32[]{:S(2)}) collective-permute-start(bf16[32,2048]{1,0:T(8,128)(2,1)S(1)} %get-tuple-element.60), channel_id=1, source_target_pairs={{0,1},{1,0},{2,3},{3,2},{4,5},{5,4},{6,7},{7,6},{8,9},{9,8},{10,11... | collective-permute-start | bytes 393224 | tf_op jit(solution)/shard_map/ppermute | solution.py:165
  (82 other events, 553.2 us)

commit v2 on v0

--- a/solution.py
+++ b/solution.py
@@ -1,6 +1,8 @@
 import jax
 import jax.numpy as jnp
 from jax import lax
+from jax.experimental import pallas as pl
+from jax.experimental.pallas import tpu as pltpu
 from jax.sharding import PartitionSpec as P
 
 L = 8192
@@ -56,7 +58,7 @@
     return lax.psum(partial_value.astype(jnp.bfloat16), "batch").astype(jnp.float32)
 
 
-def local(hidden_act, weight, first_moment, second_moment, wigner, quad_weight, target):
+def local_plain(hidden_act, weight, first_moment, second_moment, wigner, quad_weight, target):
     batch_rows = hidden_act.shape[0]
     h_local = weight.shape[1]
     l_local = weight.shape[2]
@@ -153,9 +155,394 @@
     return (new_weight, new_first, new_second)
 
 
+bf16 = jnp.bfloat16
+SHRINK = 64
+f32 = jnp.float32
+ORDER = (0, 2, 1, 3)
+PLAN = (
+    "L0", "a0", "a3", "a2", "a1", "F0", "E0", "K0", "F3", "E3", "K3", "F2",
+    "s0", "s3", "E2", "K2", "F1", "E1", "K1", "S3", "B0", "s2", "b0", "B2",
+    "s1", "T0", "P0", "b2", "H3", "p0", "B1", "P2", "g3", "p2", "b1", "Q0",
+    "P1", "c0", "Q2", "p1", "C0", "c2", "d0", "Q1", "C2", "W0", "c1", "w0",
+    "d2", "C1", "G3", "W2", "F3", "d1", "w2", "W1", "d3", "w1", "W3", "w3", "U0",
+    "U3",
+)
+
+
+def swap(value, axis, mask):
+    count = lax.axis_size(axis)
+    return lax.ppermute(value, axis, [(i, i ^ mask) for i in range(count)])
+
+
+def call(kernel, out_shape, *args, waits=(), in_hbm=(), scratch=(), flops=0, moved=0):
+    count = len(args)
+    vmem = pl.BlockSpec(memory_space=pltpu.VMEM)
+    hbm = pl.BlockSpec(memory_space=pl.ANY)
+
+    def body(*refs):
+        kernel(*refs[:count], *refs[count + len(waits) :])
+
+    return pl.pallas_call(
+        body,
+        out_shape=out_shape,
+        in_specs=[hbm if i in in_hbm else vmem for i in range(count)] + [hbm] * len(waits),
+        out_specs=jax.tree.map(lambda _: vmem, out_shape),
+        scratch_shapes=list(scratch),
+        compiler_params=pltpu.CompilerParams(vmem_limit_bytes=3 << 20),
+        cost_estimate=pl.CostEstimate(flops=flops // SHRINK, transcendentals=0, bytes_accessed=moved // SHRINK),
+    )(*args, *waits)
+
+
+def fetch_table(wigner, table, waits):
+    _, rows, cols = wigner.shape
+    pieces = 8
+    step = rows // pieces
+
+    def kernel(source, out, mark, sem):
+        copies = [
+            pltpu.make_async_copy(
+                source.at[table, pl.ds(i * step, step)], out.at[pl.ds(i * step, step)], sem.at[i]
+            )
+            for i in range(pieces)
+        ]
+        for copy in copies:
+            copy.start()
+        mark[...] = jnp.zeros_like(mark)
+        for copy in copies:
+            copy.wait()
+
+    return call(
+        kernel,
+        (pltpu.VMEM((rows, cols), bf16), jax.ShapeDtypeStruct((8, 128), f32)),
+        wigner,
+        waits=waits,
+        in_hbm=(0,),
+        scratch=[pltpu.SemaphoreType.DMA((pieces,))],
+        moved=rows * cols * 4,
+    )
+
+
+def onto_angles(rows, table, rate=None):
+    kinds = 1 if rate is None else 2
+    count = rows.shape[0] // 4
+    total_rows = kinds * rows.shape[0]
+    depth, cols = table.shape
+    step = cols // 4
+
+    def kernel(*refs):
+        if rate is None:
+            lhs, tab, keep, send = refs
+        else:
+            row, rate_ref, tab, keep, send, lhs = refs
+            for place in range(4):
+                value = row[place * count : (place + 1) * count, :]
+                lhs[2 * place * count : (2 * place + 1) * count, :] = value
+                lhs[(2 * place + 1) * count : (2 * place + 2) * count, :] = (
+                    value.astype(f32) * rate_ref[...]
+                ).astype(bf16)
+        for i in range(4):
+            cut = slice(i * step, (i + 1) * step)
+            total = jnp.dot(lhs[...], tab[:, cut], preferred_element_type=f32)
+            keep[:, cut] = total[: total_rows // 2]
+            send[:, cut] = total[total_rows // 2 :].astype(bf16)
+
+    args = [rows] + ([] if rate is None else [rate]) + [table]
+    return call(
+        kernel,
+        (
+            jax.ShapeDtypeStruct((total_rows // 2, cols), f32),
+            jax.ShapeDtypeStruct((total_rows // 2, cols), bf16),
+        ),
+        *args,
+        scratch=[] if rate is None else [pltpu.VMEM((total_rows, depth), bf16)],
+        flops=2 * total_rows * depth * cols,
+        moved=total_rows * cols * 6,
+    )
+
+
+def onto_multipoles(halves, table, sigma=None, rate=None, waits=()):
+    kinds = 1 if rate is None else 2
+    half = halves[0].shape[0]
+    rows = 2 * half
+    cols, depth = table.shape
+    step = cols // 4
+
+    def kernel(*refs):
+        if rate is None:
+            one, two, tab, keep, send, lhs = refs
+        else:
+            one, two, sigma_one, sigma_two, rate_ref, tab, keep, send, lhs = refs
+        lhs[:half, :] = one[...]
+        lhs[half:rows, :] = two[...]
+        if rate is not None:
+            lhs[rows : rows + half, :] = (-(one[...].astype(f32) * sigma_one[...].astype(f32))).astype(bf16)
+            lhs[rows + half :, :] = (-(two[...].astype(f32) * sigma_two[...].astype(f32))).astype(bf16)
+        for i in range(4):
+            cut = slice(i * step, (i + 1) * step)
+            total = lax.dot_general(
+                tab[cut, :], lhs[...], (((1,), (1,)), ((), ())), preferred_element_type=f32
+            ).T
+            if rate is not None:
+                total = total[:rows] + total[rows:] * rate_ref[:, cut]
+            keep[:, cut] = total
+            send[:, cut] = total.astype(bf16)
+
+    args = list(halves) + ([] if rate is None else list(sigma) + [rate]) + [table]
+    return call(
+        kernel,
+        (jax.ShapeDtypeStruct((rows, cols), f32), jax.ShapeDtypeStruct((rows, cols), bf16)),
+        *args,
+        waits=waits,
+        scratch=[pltpu.VMEM((kinds * rows, depth), bf16)],
+        flops=2 * kinds * rows * depth * cols,
+        moved=rows * cols * 6,
+    )
+
+
+def spectra(hidden, weight, wanted):
+    rows, depth = hidden.shape
+    cols = weight.shape[2]
+    count = len(wanted)
+
+    def kernel(hid, *refs):
+        wgts, keeps, sends = refs[:count], refs[count : 2 * count], refs[2 * count :]
+        for wgt, keep, send in zip(wgts, keeps, sends):
+            total = jnp.dot(hid[...], wgt[...], preferred_element_type=f32)
+            keep[...] = total
+            send[...] = total.astype(bf16)
+
+    def part(kind):
+        return pl.BlockSpec((None, depth, cols), lambda i: (kind, 0, 0))
+
+    whole = pl.BlockSpec((rows, cols), lambda i: (0, 0))
+    return pl.pallas_call(
+        kernel,
+        grid=(1,),
+        out_shape=[jax.ShapeDtypeStruct((rows, cols), f32)] * count
+        + [jax.ShapeDtypeStruct((rows, cols), bf16)] * count,
+        in_specs=[pl.BlockSpec((rows, depth), lambda i: (0, 0))] + [part(k) for k in wanted],
+        out_specs=[whole] * (2 * count),
+        compiler_params=pltpu.CompilerParams(vmem_limit_bytes=12 << 20),
+    )(hidden, *[weight] * count)
+
+
+def adam(hidden, log_grad, first_kind, weight, first, second, made):
+    rows, depth = hidden.shape
+    kinds, _, cols = log_grad.shape
+    tile = depth // 2
+
+    def kernel(hid, grad, wgt, one, two, *refs):
+        new_wgt, new_one, new_two = refs[-3:]
+        slope = lax.dot_general(
+            hid[...], grad[...], (((0,), (0,)), ((), ())), preferred_element_type=f32
+        )
+        moved = 0.9 * one[...] + 0.1 * slope
+        spread = 0.999 * two[...] + 0.001 * slope * slope
+        new_one[...] = moved
+        new_two[...] = spread
+        update = moved * (1.0 / first_fix) / (jnp.sqrt(spread * (1.0 / second_fix)) + 1e-08)
+        new_wgt[...] = (wgt[...].astype(f32) - 0.001 * update).astype(bf16)
+
+    block = pl.BlockSpec((None, tile, cols), lambda s, i: (first_kind + s, i, 0))
+    made = () if made is None else made
+    return pl.pallas_call(
+        kernel,
+        grid=(kinds, depth // tile),
+        out_shape=(
+            jax.ShapeDtypeStruct(weight.shape, bf16),
+            jax.ShapeDtypeStruct(weight.shape, f32),
+            jax.ShapeDtypeStruct(weight.shape, f32),
+        ),
+        in_specs=[
+            pl.BlockSpec((rows, tile), lambda s, i: (0, i)),
+            pl.BlockSpec((None, rows, cols), lambda s, i: (s, 0, 0)),
+        ]
+        + [block] * 3
+        + [pl.BlockSpec(memory_space=pl.ANY)] * len(made),
+        out_specs=(block, block, block),
+        input_output_aliases={5 + i: i for i in range(len(made))},
+        compiler_params=pltpu.CompilerParams(vmem_limit_bytes=14 << 20),
+        cost_estimate=pl.CostEstimate(
+            flops=2 * kinds * rows * depth * cols,
+            transcendentals=0,
+            bytes_accessed=20 * kinds * depth * cols,
+        ),
+    )(hidden, log_grad, weight, first, second, *made)
+
+
+def local_fast(hidden_act, weight, first_moment, second_moment, wigner, quad_weight, target):
+    count = hidden_act.shape[0] // 4
+    h_local = weight.shape[1]
+    l_local = weight.shape[2]
+    at_ell = lax.axis_index("ell")
+    at_batch = lax.axis_index("batch")
+    multipole = (at_ell * l_local + lax.iota(jnp.int32, l_local)).astype(f32)[None]
+    lens_rate = multipole * (multipole + 1.0) / (float(L) * float(L))
+    loss_weight = (1.0 + 2.0 * multipole / float(L)) / hidden_act.shape[0]
+    quad = quad_weight[None]
+    starts = [jnp.bitwise_xor(at_ell, position) * count for position in ORDER]
+    own_hidden = jnp.concatenate(
+        [
+            lax.dynamic_slice(hidden_act, (start, at_batch * h_local), (count, h_local))
+            for start in starts
+        ]
+    )
+    wigner = pltpu.with_memory_space_constraint(wigner, pltpu.HBM)
+    token = [own_hidden]
+
+    def after(value):
+        value, token[0] = lax.optimization_barrier((value, token[0]))
+        return value
+
+    def done(*values):
+        token[0] = values[0]
+        return values if len(values) > 1 else values[0]
+
+    held, passed = {}, {}
+
+    def begin(name, kept, sent, axis):
+        held[name] = (kept, swap(sent, axis, 1))
+
+    def join(name, axis):
+        kept, received = held[name]
+        total = after(kept) + received.astype(f32)
+        if axis == "batch":
+            kept, sent = total, total.astype(bf16)
+        else:
+            rows = total.shape[0] // 2
+            kept, sent = total[:rows], total[rows:].astype(bf16)
+        sent, kept = done(sent, kept)
+        held[name] = (kept, swap(sent, axis, 2))
+        passed[name] = sent
+
+    def total_of(name):
+        kept, received = held[name]
+        return after(kept) + received.astype(f32)
+
+    def spread(name, own):
+        held[name] = (own, swap(own, "ell", 2))
+
+    def widen(name):
+        own, far = held[name]
+        both = done(jnp.concatenate([after(own), far]))
+        held[name] = (both, swap(both, "ell", 1))
+
+    def halves_of(name):
+        both, near = held[name]
+        return after(both), near
+
+    table, log_power, power, second_sum, corr, coef, made = {}, {}, {}, {}, {}, {}, [None]
+
+    def log_spectra(_):
+        wanted = (0, 3, 2, 1)
+        parts = spectra(own_hidden, weight, wanted)
+        done(parts[-1])
+        for i, s in enumerate(wanted):
+            begin(("log", s), parts[i], parts[4 + i], "batch")
+
+    def fetch(t):
+        waits = (token[0],)
+        if not table:
+            waits = tuple(passed["log", s] for s in range(4))
+        table[t], mark = fetch_table(wigner, t, waits)
+        done(mark)
+
+    def own_target(_):
+        value = after(target)
+        held["target"] = done(
+            jnp.concatenate([lax.dynamic_slice_in_dim(value, start, count, 1) for start in starts], 1)
+        )
+
+    def spectrum(s):
+        log_power[s] = total_of(("log", s))
+        if s == 1:
+            power["scale"] = jnp.exp(0.5 * (log_power[0] + log_power[2]))
+            power["ratio"] = jnp.tanh(log_power[1])
+            power[s] = power["ratio"] * power["scale"]
+        else:
+            power[s] = jnp.exp(log_power[s])
+        held["rows", s] = done(power[s].astype(bf16))
+
+    def forward(t):
+        rate = None if t == 3 else lens_rate
+        sent, kept = done(*onto_angles(after(held["rows", t]), table[t], rate)[::-1])
+        begin(("sum", t), kept, sent, "ell")
+
+    def sigma(_):
+        power["sigma"] = done(total_of(("sum", 3)))
+
+    def correlate(x):
+        sums = total_of(("sum", x))
+        second_sum[x] = sums[count:]
+        value = ((sums[:count] - power["sigma"] * second_sum[x]) * quad).astype(bf16)
+        spread(("back", x), done(value))
+
+    def project(x):
+        sent, kept = done(*onto_multipoles(halves_of(("back", x)), table[x])[::-1])
+        begin(("power", x), kept, sent, "batch")
+
+    def pull(x):
+        lensed = total_of(("power", x))
+        own = held["target"][x].astype(f32)
+        residual = done((loss_weight * (lensed - own)).astype(bf16))
+        sent, kept = done(*onto_angles(residual, table[x])[::-1])
+        begin(("corr", x), kept, sent, "ell")
+
+    def correct(x):
+        corr[x] = total_of(("corr", x)) * quad
+        spread(("term", x), done(corr[x].astype(bf16)))
+
+    def spread_sigma(_):
+        spread("sigma", done(after(power["sigma"]).astype(bf16)))
+
+    def sigma_grad(_):
+        value = -(after(corr[0]) * second_sum[0] + corr[1] * second_sum[1] + corr[2] * second_sum[2])
+        spread(("term", 3), done(value.astype(bf16)))
+
+    def backward(t):
+        more = (None, None) if t == 3 else (held["sigma"], lens_rate)
+        halves = halves_of(("term", t))
+        waits = tuple(passed["coef", before] for before in {2: (0,), 1: (2,), 3: (1,)}.get(t, ()))
+        sent, kept = done(*onto_multipoles(halves, table[t], *more, waits)[::-1])
+        begin(("coef", t), kept, sent, "batch")
+
+    def update(first_kind):
+        if first_kind == 3:
+            slopes = [total_of(("coef", 3)) * power[3]]
+        else:
+            for t in (1, 0, 2):
+                coef[t] = total_of(("coef", t))
+            half_cross = 0.5 * coef[1] * power[1]
+            slopes = [
+                coef[0] * power[0] + half_cross,
+                coef[1] * (1.0 - power["ratio"] * power["ratio"]) * power["scale"],
+                coef[2] * power[2] + half_cross,
+            ]
+        log_grad = done(jnp.stack([slope.astype(bf16) for slope in slopes]))
+        made[0] = adam(own_hidden, log_grad, first_kind, weight, first_moment, second_moment, made[0])
+
+    actions = {
+        "L": log_spectra, "F": fetch, "T": own_target, "E": spectrum, "K": forward, "S": sigma,
+        "B": correlate, "P": project, "Q": pull, "C": correct, "H": spread_sigma, "G": sigma_grad,
+        "W": backward, "U": update,
+        "a": lambda s: join(("log", s), "batch"),
+        "s": lambda t: join(("sum", t), "ell"),
+        "p": lambda x: join(("power", x), "batch"),
+        "c": lambda x: join(("corr", x), "ell"),
+        "w": lambda t: join(("coef", t), "batch"),
+        "b": lambda x: widen(("back", x)),
+        "d": lambda t: widen(("term", t)),
+        "g": lambda _: widen("sigma"),
+    }
+    for step in PLAN:
+        actions[step[0]](int(step[1]))
+    return made[0]
+
+
 def solution(mesh):
+    four = mesh.shape["ell"] == 4 and mesh.shape["batch"] == 4
     return jax.shard_map(
-        local,
+        local_fast if four else local_plain,
         mesh=mesh,
         in_specs=(
             P("groups", None),

time: 411 us -> 178 us (0.43)
  waiting for transfers between devices: 231 us -> 46.8 us
  matrix products: 94.9 us -> 0 us
  Pallas kernels: 0 us -> 60.6 us
  starting transfers between devices: 0.61 us -> 59.2 us
  local copies, waits for them, and re-layouts: 51.4 us -> 3.32 us
  between operations: 14 us -> 1.54 us
  other arithmetic: 16.9 us -> 5.88 us
    psum x5 -> x0, waiting for transfers between devices: 231 us -> none  [the longest x2 121 us: angle_reduce(): lax.psum(partial_value.astype(jnp.bfloat16), 'ell').astype(jnp.float32)]
    dot_general x16 -> x0, matrix products: 94.9 us -> none  [the longest x3 18.8 us: backward_terms(): jnp.einsum('rca,la->rcl', piece[2 * table:2 * table + 2], tables[table],...]
    pallas_call x0 -> x22, Pallas kernels: none -> 60.6 us  [the longest x19 48 us: call(): pl.pallas_call(body, out_shape=out_shape, in_specs=[hbm if i in in_hbm el...]
    ppermute x0 -> x52, starting transfers between devices: none -> 59.2 us  [swap(): return lax.ppermute(value, axis, [(i, i ^ mask) for i in range(count)])]
    unnamed x18 -> x27, local copies, waits for them, and re-layouts: 51.3 us -> 2.28 us
    ppermute x0 -> x52, waiting for transfers between devices: none -> 46.8 us  [swap(): return lax.ppermute(value, axis, [(i, i ^ mask) for i in range(count)])]
    another operation x6 -> x3, other arithmetic: 5.59 us -> 0.83 us  [update(): log_grad = done(jnp.stack([slope.astype(bf16) for slope in slopes]))]
  transfers between devices with their start and end apart: 5 -> 52, of which waited for: 5 -> 24; matrix products, arithmetic and copies ran while one was open for 6% -> 3% of each run, Pallas kernels for 0% -> 30%
where the time goes in v2:
time: 178 us; the launch traced here: 177 us
  Pallas kernels  60.6 us (34%)
  starting transfers between devices  59.2 us (33%)
  waiting for transfers between devices  46.8 us (26%)
  other arithmetic  5.88 us (3%)
  local copies, waits for them, and re-layouts  3.32 us (2%)
    ppermute x52, starting transfers between devices, swap(): return lax.ppermute(value, axis, [(i, i ^ mask) for i in range(count)])  59.2 us
    pallas_call x19, Pallas kernels, call(): pl.pallas_call(body, out_shape=out_shape, in_specs=[hbm if i in in_hbm el...  48 us
    ppermute x52, waiting for transfers between devices, swap(): return lax.ppermute(value, axis, [(i, i ^ mask) for i in range(count)])  46.8 us
    pallas_call x2, Pallas kernels, adam(): pl.pallas_call(kernel, grid=(kinds, depth // tile), out_shape=(jax.ShapeD...  11.8 us
    convert_element_type x11, other arithmetic, join(): kept, sent = (total, total.astype(bf16))  3.57 us
  transfers between devices with their start and end apart: 52, of which 24 were waited for; matrix products, arithmetic and copies ran while one was open for 3% of the time, Pallas kernels for 30%

profile of v2, /device:TPU:0, one launch (start us, length us, event | category | flops | bytes accessed | tf_op | source)
XLA Modules:
  0.0 177.3 jit_solution(15698844081093176374)
XLA Ops:
  7.3 2.9 %collective-permute-start.1 = (bf16[64,2048]{1,0:T(8,128)(2,1)S(1)}, bf16[64,2048]{1,0:T(8,128)(2,1)S(1)}, u32[]{:S(2)}, u32[]{:S(2)}) collective-permute-start(bf16[64,2048]{1,0:T(8,128)(2,1)S(1)} %get-tuple-element.208.refs_1_), channel_id=1, source_target_pairs={{0,2},{1,3},{2,0},{3,1},{4,6},{5,7},{6,4},{7,5},{8,10},{9,11},{10,... | collective-permute-start | bytes 786440 | tf_op jit(solution)/shard_map/ppermute | solution.py:174
  14.6 4.1 %shard_map.95 = (bf16[2048,2048]{1,0:T(8,128)(2,1)S(1)}, f32[8,128]{1,0:T(8,128)}) custom-call(bf16[4,2048,2048]{2,1,0:T(8,128)(2,1)} %refs_0_.11, bf16[64,2048]{1,0:T(8,128)(2,1)S(1)} %get-tuple-element.208.refs_1_, bf16[64,2048]{1,0:T(8,128)(2,1)S(1)} %get-tuple-element.202.refs_2_, bf16[64,2048]{1,0:T(8,128)(2,1)S(1)} %get-tuple-element.204.refs_3_, ...), custom_call_target="tpu_custom_call" | custom-call | bytes 262144 | tf_op jit(solution)/shard_map/pallas_call | solution.py:185
  22.2 4.1 %shard_map.97 = (bf16[2048,2048]{1,0:T(8,128)(2,1)S(1)}, f32[8,128]{1,0:T(8,128)}) custom-call(bf16[4,2048,2048]{2,1,0:T(8,128)(2,1)} %refs_0_.11, bf16[64,2048]{1,0:T(8,128)(2,1)S(1)} %get-tuple-element.108.refs_1_), custom_call_target="tpu_custom_call" | custom-call | bytes 262144 | tf_op jit(solution)/shard_map/pallas_call | solution.py:185
  28.1 4.1 %shard_map.99 = (bf16[2048,2048]{1,0:T(8,128)(2,1)S(1)}, f32[8,128]{1,0:T(8,128)}) custom-call(bf16[4,2048,2048]{2,1,0:T(8,128)(2,1)} %refs_0_.11, bf16[32,2048]{1,0:T(8,128)(2,1)S(1)} %get-tuple-element.112.refs_1_), custom_call_target="tpu_custom_call" | custom-call | bytes 262144 | tf_op jit(solution)/shard_map/pallas_call | solution.py:185
  32.3 3.1 %collective-permute-start.11 = (bf16[32,2048]{1,0:T(8,128)(2,1)S(1)}, bf16[32,2048]{1,0:T(8,128)(2,1)S(1)}, u32[]{:S(2)}, u32[]{:S(2)}) collective-permute-start(bf16[32,2048]{1,0:T(8,128)(2,1)S(1)} %slice.161), channel_id=1, source_target_pairs={{0,8},{4,12},{8,0},{12,4},{1,9},{5,13},{9,1},{13,5},{2,10},{6,14},... | collective-permute-start | bytes 393224 | tf_op jit(solution)/shard_map/ppermute | solution.py:174
  39.0 4.1 %shard_map.101 = (bf16[2048,2048]{1,0:T(8,128)(2,1)S(1)}, f32[8,128]{1,0:T(8,128)}) custom-call(bf16[4,2048,2048]{2,1,0:T(8,128)(2,1)} %refs_0_.11, bf16[64,2048]{1,0:T(8,128)(2,1)S(1)} %get-tuple-element.115.refs_1_), custom_call_target="tpu_custom_call" | custom-call | bytes 262144 | tf_op jit(solution)/shard_map/pallas_call | solution.py:185
  45.1 2.7 %collective-permute-start.13 = (bf16[16,2048]{1,0:T(8,128)(2,1)S(1)}, bf16[16,2048]{1,0:T(8,128)(2,1)S(1)}, u32[]{:S(2)}, u32[]{:S(2)}) collective-permute-start(bf16[16,2048]{1,0:T(8,128)(2,1)S(1)} %fusion.17), channel_id=1, source_target_pairs={{0,8},{4,12},{8,0},{12,4},{1,9},{5,13},{9,1},{13,5},{2,10},{6,14},... | collective-permute-start | bytes 196616 | tf_op jit(solution)/shard_map/ppermute | solution.py:174
  47.9 3.5 %collective-permute-start.14 = (bf16[32,2048]{1,0:T(8,128)(2,1)S(1)}, bf16[32,2048]{1,0:T(8,128)(2,1)S(1)}, u32[]{:S(2)}, u32[]{:S(2)}) collective-permute-start(bf16[32,2048]{1,0:T(8,128)(2,1)S(1)} %slice.160), channel_id=1, source_target_pairs={{0,8},{4,12},{8,0},{12,4},{1,9},{5,13},{9,1},{13,5},{2,10},{6,14},... | collective-permute-start | bytes 393224 | tf_op jit(solution)/shard_map/ppermute | solution.py:174
  53.1 3.3 %collective-permute-start.16 = (bf16[32,2048]{1,0:T(8,128)(2,1)S(1)}, bf16[32,2048]{1,0:T(8,128)(2,1)S(1)}, u32[]{:S(2)}, u32[]{:S(2)}) collective-permute-start(bf16[32,2048]{1,0:T(8,128)(2,1)S(1)} %constant_dynamic-update-slice_fusion.refs_0_), channel_id=1, source_target_pairs={{0,4},{4,0},{8,12},{12,8},{1,5},{5,1},{9,13},{13,9},{2,6},{6,2},{1... | collective-permute-start | bytes 393224 | tf_op jit(solution)/shard_map/ppermute | solution.py:174
  63.6 2.9 %collective-permute-start.20 = (bf16[32,2048]{1,0:T(8,128)(2,1)S(1)}, bf16[32,2048]{1,0:T(8,128)(2,1)S(1)}, u32[]{:S(2)}, u32[]{:S(2)}) collective-permute-start(bf16[32,2048]{1,0:T(8,128)(2,1)S(1)} %constant_dynamic-update-slice_fusion.2.refs_0_), channel_id=1, source_target_pairs={{0,4},{4,0},{8,12},{12,8},{1,5},{5,1},{9,13},{13,9},{2,6},{6,2},{1... | collective-permute-start | bytes 393224 | tf_op jit(solution)/shard_map/ppermute | solution.py:174
  66.5 3.0 %collective-permute-start.21 = (bf16[16,2048]{1,0:T(8,128)(2,1)S(1)}, bf16[16,2048]{1,0:T(8,128)(2,1)S(1)}, u32[]{:S(2)}, u32[]{:S(2)}) collective-permute-start(bf16[16,2048]{1,0:T(8,128)(2,1)S(1)} %convert_element_type.265), channel_id=1, source_target_pairs={{0,8},{4,12},{8,0},{12,4},{1,9},{5,13},{9,1},{13,5},{2,10},{6,14},... | collective-permute-start | bytes 196616 | tf_op jit(solution)/shard_map/ppermute | solution.py:174
  86.5 2.9 %collective-permute-start.29 = (bf16[16,2048]{1,0:T(8,128)(2,1)S(1)}, bf16[16,2048]{1,0:T(8,128)(2,1)S(1)}, u32[]{:S(2)}, u32[]{:S(2)}) collective-permute-start(bf16[16,2048]{1,0:T(8,128)(2,1)S(1)} %slice.164), channel_id=1, source_target_pairs={{0,8},{4,12},{8,0},{12,4},{1,9},{5,13},{9,1},{13,5},{2,10},{6,14},... | collective-permute-start | bytes 196616 | tf_op jit(solution)/shard_map/ppermute | solution.py:174
  93.5 3.2 %collective-permute-done.30 = bf16[32,2048]{1,0:T(8,128)(2,1)S(1)} collective-permute-done((bf16[32,2048]{1,0:T(8,128)(2,1)S(1)}, bf16[32,2048]{1,0:T(8,128)(2,1)S(1)}, u32[]{:S(2)}, u32[]{:S(2)}) %collective-permute-start.30) | collective-permute-done | bytes 131104 | tf_op jit(solution)/shard_map/ppermute | solution.py:174
  101.4 3.9 %collective-permute-done.31 = bf16[16,2048]{1,0:T(8,128)(2,1)S(1)} collective-permute-done((bf16[16,2048]{1,0:T(8,128)(2,1)S(1)}, bf16[16,2048]{1,0:T(8,128)(2,1)S(1)}, u32[]{:S(2)}, u32[]{:S(2)}) %collective-permute-start.31) | collective-permute-done | bytes 65568 | tf_op jit(solution)/shard_map/ppermute | solution.py:174
  111.4 2.4 %shard_map.109 = (f32[64,2048]{1,0:T(8,128)S(1)}, bf16[64,2048]{1,0:T(8,128)(2,1)S(1)}) custom-call(bf16[32,2048]{1,0:T(8,128)(2,1)S(1)} %constant_dynamic-update-slice_fusion.8.refs_0_, bf16[32,2048]{1,0:T(8,128)(2,1)S(1)} %collective-permute-done.34.refs_1_, bf16[32,2048]{1,0:T(8,128)(2,1)S(1)} %constant_dynamic-update-slice_fusion.4.refs_2_, ...), custom_call_target="tpu_custom_call" | custom-call | flops 16777216 | bytes 12288 | tf_op jit(solution)/shard_map/pallas_call | solution.py:185
  116.7 4.2 %collective-permute-done.39 = bf16[16,2048]{1,0:T(8,128)(2,1)S(1)} collective-permute-done((bf16[16,2048]{1,0:T(8,128)(2,1)S(1)}, bf16[16,2048]{1,0:T(8,128)(2,1)S(1)}, u32[]{:S(2)}, u32[]{:S(2)}) %collective-permute-start.39) | collective-permute-done | bytes 65568 | tf_op jit(solution)/shard_map/ppermute | solution.py:174
  127.6 4.4 %shard_map.112 = (bf16[2048,2048]{1,0:T(8,128)(2,1)S(1)}, f32[8,128]{1,0:T(8,128)}) custom-call(bf16[4,2048,2048]{2,1,0:T(8,128)(2,1)} %refs_0_.11, bf16[64,2048]{1,0:T(8,128)(2,1)S(1)} %get-tuple-element.169.refs_1_), custom_call_target="tpu_custom_call" | custom-call | bytes 262144 | tf_op jit(solution)/shard_map/pallas_call | solution.py:185
  133.0 2.7 %shard_map.111 = (f32[64,2048]{1,0:T(8,128)S(1)}, bf16[64,2048]{1,0:T(8,128)(2,1)S(1)}) custom-call(bf16[32,2048]{1,0:T(8,128)(2,1)S(1)} %pad_maximum_fusion.2.refs_0_, bf16[32,2048]{1,0:T(8,128)(2,1)S(1)} %collective-permute-done.43.refs_1_, bf16[32,2048]{1,0:T(8,128)(2,1)S(1)} %constant_dynamic-update-slice_fusion.4.refs_2_, ...), custom_call_target="tpu_custom_call" | custom-call | flops 16777216 | bytes 12288 | tf_op jit(solution)/shard_map/pallas_call | solution.py:185
  137.3 4.4 %collective-permute-done.46.refs_1_ = bf16[32,2048]{1,0:T(8,128)(2,1)S(1)} collective-permute-done((bf16[32,2048]{1,0:T(8,128)(2,1)S(1)}, bf16[32,2048]{1,0:T(8,128)(2,1)S(1)}, u32[]{:S(2)}, u32[]{:S(2)}) %collective-permute-start.46) | collective-permute-done | bytes 131104 | tf_op jit(solution)/shard_map/ppermute | solution.py:174
  148.5 4.9 %collective-permute-done.48 = bf16[64,2048]{1,0:T(8,128)(2,1)S(1)} collective-permute-done((bf16[64,2048]{1,0:T(8,128)(2,1)S(1)}, bf16[64,2048]{1,0:T(8,128)(2,1)S(1)}, u32[]{:S(2)}, u32[]{:S(2)}) %collective-permute-start.48) | collective-permute-done | bytes 262176 | tf_op jit(solution)/shard_map/ppermute | solution.py:174
  153.4 5.6 %collective-permute-done.50 = bf16[64,2048]{1,0:T(8,128)(2,1)S(1)} collective-permute-done((bf16[64,2048]{1,0:T(8,128)(2,1)S(1)}, bf16[64,2048]{1,0:T(8,128)(2,1)S(1)}, u32[]{:S(2)}, u32[]{:S(2)}) %collective-permute-start.50) | collective-permute-done | bytes 262176 | tf_op jit(solution)/shard_map/ppermute | solution.py:174
  159.0 5.6 %collective-permute-done.49 = bf16[64,2048]{1,0:T(8,128)(2,1)S(1)} collective-permute-done((bf16[64,2048]{1,0:T(8,128)(2,1)S(1)}, bf16[64,2048]{1,0:T(8,128)(2,1)S(1)}, u32[]{:S(2)}, u32[]{:S(2)}) %collective-permute-start.49) | collective-permute-done | bytes 262176 | tf_op jit(solution)/shard_map/ppermute | solution.py:174
  165.3 8.3 %shard_map.114 = (bf16[4,256,2048]{2,1,0:T(8,128)(2,1)}, f32[4,256,2048]{2,1,0:T(8,128)}, f32[4,256,2048]{2,1,0:T(8,128)}) custom-call(bf16[64,256]{1,0:T(8,128)(2,1)S(1)} %pad_maximum_fusion.3.hid, bf16[3,64,2048]{2,1,0:T(8,128)(2,1)S(1)} %pad_maximum_fusion.1.grad, bf16[4,256,2048]{2,1,0:T(8,128)(2,1)S(1)} %copy-done.1, f32[4,256,2048]{2,1,0:T(8,128)S(1)} %bitcast.24, ...), custom_call_target="tpu_custom_call" | custom-call | flops 201326592 | bytes 31457280 | tf_op jit(solution)/shard_map/pallas_call | solution.py:348
  173.8 3.5 %shard_map.115 = (bf16[4,256,2048]{2,1,0:T(8,128)(2,1)}, f32[4,256,2048]{2,1,0:T(8,128)}, f32[4,256,2048]{2,1,0:T(8,128)}) custom-call(bf16[64,256]{1,0:T(8,128)(2,1)S(1)} %pad_maximum_fusion.3.hid, bf16[1,64,2048]{2,1,0:T(8,128)(2,1)S(1)} %fusion.11.grad, ...), custom_call_target="tpu_custom_call", output_to_operand_aliasing={{0}: (5, {}), {1}: (6, {}), {2}: (7, {})} | custom-call | flops 67108864 | bytes 10485760 | tf_op jit(solution)/shard_map/pallas_call | solution.py:348
  (200 shorter events, 82.1 us)
Async XLA Ops:
  5.5 8.9 %collective-permute-start.4 = (bf16[64,2048]{1,0:T(8,128)(2,1)S(1)}, bf16[64,2048]{1,0:T(8,128)(2,1)S(1)}, u32[]{:S(2)}, u32[]{:S(2)}) collective-permute-start(bf16[64,2048]{1,0:T(8,128)(2,1)S(1)} %get-tuple-element.95), channel_id=1, source_target_pairs={{0,1},{1,0},{2,3},{3,2},{4,5},{5,4},{6,7},{7,6},{8,9},{9,8},{10,11... | collective-permute-start | bytes 786440 | tf_op jit(solution)/shard_map/ppermute | solution.py:174
  7.3 11.3 %collective-permute-start.1 = (bf16[64,2048]{1,0:T(8,128)(2,1)S(1)}, bf16[64,2048]{1,0:T(8,128)(2,1)S(1)}, u32[]{:S(2)}, u32[]{:S(2)}) collective-permute-start(bf16[64,2048]{1,0:T(8,128)(2,1)S(1)} %get-tuple-element.208.refs_1_), channel_id=1, source_target_pairs={{0,2},{1,3},{2,0},{3,1},{4,6},{5,7},{6,4},{7,5},{8,10},{9,11},{10,... | collective-permute-start | bytes 786440 | tf_op jit(solution)/shard_map/ppermute | solution.py:174
  11.2 15.1 %collective-permute-start.6 = (bf16[64,2048]{1,0:T(8,128)(2,1)S(1)}, bf16[64,2048]{1,0:T(8,128)(2,1)S(1)}, u32[]{:S(2)}, u32[]{:S(2)}) collective-permute-start(bf16[64,2048]{1,0:T(8,128)(2,1)S(1)} %get-tuple-element.206.refs_4_), channel_id=1, source_target_pairs={{0,2},{1,3},{2,0},{3,1},{4,6},{5,7},{6,4},{7,5},{8,10},{9,11},{10,... | collective-permute-start | bytes 786440 | tf_op jit(solution)/shard_map/ppermute | solution.py:174
  12.3 23.4 %collective-permute-start.9 = (bf16[64,2048]{1,0:T(8,128)(2,1)S(1)}, bf16[64,2048]{1,0:T(8,128)(2,1)S(1)}, u32[]{:S(2)}, u32[]{:S(2)}) collective-permute-start(bf16[64,2048]{1,0:T(8,128)(2,1)S(1)} %get-tuple-element.204.refs_3_), channel_id=1, source_target_pairs={{0,2},{1,3},{2,0},{3,1},{4,6},{5,7},{6,4},{7,5},{8,10},{9,11},{10,... | collective-permute-start | bytes 786440 | tf_op jit(solution)/shard_map/ppermute | solution.py:174
  14.5 21.2 %collective-permute-start.8 = (bf16[64,2048]{1,0:T(8,128)(2,1)S(1)}, bf16[64,2048]{1,0:T(8,128)(2,1)S(1)}, u32[]{:S(2)}, u32[]{:S(2)}) collective-permute-start(bf16[64,2048]{1,0:T(8,128)(2,1)S(1)} %get-tuple-element.202.refs_2_), channel_id=1, source_target_pairs={{0,2},{1,3},{2,0},{3,1},{4,6},{5,7},{6,4},{7,5},{8,10},{9,11},{10,... | collective-permute-start | bytes 786440 | tf_op jit(solution)/shard_map/ppermute | solution.py:174
  20.1 12.1 %collective-permute-start.5 = (bf16[64,2048]{1,0:T(8,128)(2,1)S(1)}, bf16[64,2048]{1,0:T(8,128)(2,1)S(1)}, u32[]{:S(2)}, u32[]{:S(2)}) collective-permute-start(bf16[64,2048]{1,0:T(8,128)(2,1)S(1)} %get-tuple-element.108.refs_1_), channel_id=1, source_target_pairs={{0,4},{4,0},{8,12},{12,8},{1,5},{5,1},{9,13},{13,9},{2,6},{6,2},{1... | collective-permute-start | bytes 786440 | tf_op jit(solution)/shard_map/ppermute | solution.py:174
  32.3 12.7 %collective-permute-start.11 = (bf16[32,2048]{1,0:T(8,128)(2,1)S(1)}, bf16[32,2048]{1,0:T(8,128)(2,1)S(1)}, u32[]{:S(2)}, u32[]{:S(2)}) collective-permute-start(bf16[32,2048]{1,0:T(8,128)(2,1)S(1)} %slice.161), channel_id=1, source_target_pairs={{0,8},{4,12},{8,0},{12,4},{1,9},{5,13},{9,1},{13,5},{2,10},{6,14},... | collective-permute-start | bytes 393224 | tf_op jit(solution)/shard_map/ppermute | solution.py:174
  35.4 9.5 %collective-permute-start.10 = (bf16[16,2048]{1,0:T(8,128)(2,1)S(1)}, bf16[16,2048]{1,0:T(8,128)(2,1)S(1)}, u32[]{:S(2)}, u32[]{:S(2)}) collective-permute-start(bf16[16,2048]{1,0:T(8,128)(2,1)S(1)} %slice.165), channel_id=1, source_target_pairs={{0,8},{4,12},{8,0},{12,4},{1,9},{5,13},{9,1},{13,5},{2,10},{6,14},... | collective-permute-start | bytes 196616 | tf_op jit(solution)/shard_map/ppermute | solution.py:174
  37.3 10.4 %collective-permute-start.12 = (bf16[64,2048]{1,0:T(8,128)(2,1)S(1)}, bf16[64,2048]{1,0:T(8,128)(2,1)S(1)}, u32[]{:S(2)}, u32[]{:S(2)}) collective-permute-start(bf16[64,2048]{1,0:T(8,128)(2,1)S(1)} %get-tuple-element.115.refs_1_), channel_id=1, source_target_pairs={{0,4},{4,0},{8,12},{12,8},{1,5},{5,1},{9,13},{13,9},{2,6},{6,2},{1... | collective-permute-start | bytes 786440 | tf_op jit(solution)/shard_map/ppermute | solution.py:174
  44.5 14.4 %collective-permute-start.15 = (bf16[64,2048]{1,0:T(8,128)(2,1)S(1)}, bf16[64,2048]{1,0:T(8,128)(2,1)S(1)}, u32[]{:S(2)}, u32[]{:S(2)}) collective-permute-start(bf16[64,2048]{1,0:T(8,128)(2,1)S(1)} %get-tuple-element.117), channel_id=1, source_target_pairs={{0,4},{4,0},{8,12},{12,8},{1,5},{5,1},{9,13},{13,9},{2,6},{6,2},{1... | collective-permute-start | bytes 786440 | tf_op jit(solution)/shard_map/ppermute | solution.py:174
  45.1 8.0 %collective-permute-start.13 = (bf16[16,2048]{1,0:T(8,128)(2,1)S(1)}, bf16[16,2048]{1,0:T(8,128)(2,1)S(1)}, u32[]{:S(2)}, u32[]{:S(2)}) collective-permute-start(bf16[16,2048]{1,0:T(8,128)(2,1)S(1)} %fusion.17), channel_id=1, source_target_pairs={{0,8},{4,12},{8,0},{12,4},{1,9},{5,13},{9,1},{13,5},{2,10},{6,14},... | collective-permute-start | bytes 196616 | tf_op jit(solution)/shard_map/ppermute | solution.py:174
  47.9 8.6 %collective-permute-start.14 = (bf16[32,2048]{1,0:T(8,128)(2,1)S(1)}, bf16[32,2048]{1,0:T(8,128)(2,1)S(1)}, u32[]{:S(2)}, u32[]{:S(2)}) collective-permute-start(bf16[32,2048]{1,0:T(8,128)(2,1)S(1)} %slice.160), channel_id=1, source_target_pairs={{0,8},{4,12},{8,0},{12,4},{1,9},{5,13},{9,1},{13,5},{2,10},{6,14},... | collective-permute-start | bytes 393224 | tf_op jit(solution)/shard_map/ppermute | solution.py:174
  53.1 8.0 %collective-permute-start.16 = (bf16[32,2048]{1,0:T(8,128)(2,1)S(1)}, bf16[32,2048]{1,0:T(8,128)(2,1)S(1)}, u32[]{:S(2)}, u32[]{:S(2)}) collective-permute-start(bf16[32,2048]{1,0:T(8,128)(2,1)S(1)} %constant_dynamic-update-slice_fusion.refs_0_), channel_id=1, source_target_pairs={{0,4},{4,0},{8,12},{12,8},{1,5},{5,1},{9,13},{13,9},{2,6},{6,2},{1... | collective-permute-start | bytes 393224 | tf_op jit(solution)/shard_map/ppermute | solution.py:174
  59.0 10.6 %collective-permute-start.19 = (bf16[32,2048]{1,0:T(8,128)(2,1)S(1)}, bf16[32,2048]{1,0:T(8,128)(2,1)S(1)}, u32[]{:S(2)}, u32[]{:S(2)}) collective-permute-start(bf16[32,2048]{1,0:T(8,128)(2,1)S(1)} %slice.159), channel_id=1, source_target_pairs={{0,8},{4,12},{8,0},{12,4},{1,9},{5,13},{9,1},{13,5},{2,10},{6,14},... | collective-permute-start | bytes 393224 | tf_op jit(solution)/shard_map/ppermute | solution.py:174
  63.6 8.5 %collective-permute-start.20 = (bf16[32,2048]{1,0:T(8,128)(2,1)S(1)}, bf16[32,2048]{1,0:T(8,128)(2,1)S(1)}, u32[]{:S(2)}, u32[]{:S(2)}) collective-permute-start(bf16[32,2048]{1,0:T(8,128)(2,1)S(1)} %constant_dynamic-update-slice_fusion.2.refs_0_), channel_id=1, source_target_pairs={{0,4},{4,0},{8,12},{12,8},{1,5},{5,1},{9,13},{13,9},{2,6},{6,2},{1... | collective-permute-start | bytes 393224 | tf_op jit(solution)/shard_map/ppermute | solution.py:174
  66.5 8.0 %collective-permute-start.21 = (bf16[16,2048]{1,0:T(8,128)(2,1)S(1)}, bf16[16,2048]{1,0:T(8,128)(2,1)S(1)}, u32[]{:S(2)}, u32[]{:S(2)}) collective-permute-start(bf16[16,2048]{1,0:T(8,128)(2,1)S(1)} %convert_element_type.265), channel_id=1, source_target_pairs={{0,8},{4,12},{8,0},{12,4},{1,9},{5,13},{9,1},{13,5},{2,10},{6,14},... | collective-permute-start | bytes 196616 | tf_op jit(solution)/shard_map/ppermute | solution.py:174
  69.7 8.2 %collective-permute-start.24 = (bf16[64,2048]{1,0:T(8,128)(2,1)S(1)}, bf16[64,2048]{1,0:T(8,128)(2,1)S(1)}, u32[]{:S(2)}, u32[]{:S(2)}) collective-permute-start(bf16[64,2048]{1,0:T(8,128)(2,1)S(1)} %get-tuple-element.198), channel_id=1, source_target_pairs={{0,2},{1,3},{2,0},{3,1},{4,6},{5,7},{6,4},{7,5},{8,10},{9,11},{10,... | collective-permute-start | bytes 786440 | tf_op jit(solution)/shard_map/ppermute | solution.py:174
  81.0 29.7 %collective-permute-start.35 = (bf16[32,2048]{1,0:T(8,128)(2,1)S(1)}, bf16[32,2048]{1,0:T(8,128)(2,1)S(1)}, u32[]{:S(2)}, u32[]{:S(2)}) collective-permute-start(bf16[32,2048]{1,0:T(8,128)(2,1)S(1)} %constant_dynamic-update-slice_fusion.4.refs_2_), channel_id=1, source_target_pairs={{0,4},{4,0},{8,12},{12,8},{1,5},{5,1},{9,13},{13,9},{2,6},{6,2},{1... | collective-permute-start | bytes 393224 | tf_op jit(solution)/shard_map/ppermute | solution.py:174
  96.8 12.7 %collective-permute-start.33 = (bf16[16,2048]{1,0:T(8,128)(2,1)S(1)}, bf16[16,2048]{1,0:T(8,128)(2,1)S(1)}, u32[]{:S(2)}, u32[]{:S(2)}) collective-permute-start(bf16[16,2048]{1,0:T(8,128)(2,1)S(1)} %slice.163), channel_id=1, source_target_pairs={{0,8},{4,12},{8,0},{12,4},{1,9},{5,13},{9,1},{13,5},{2,10},{6,14},... | collective-permute-start | bytes 196616 | tf_op jit(solution)/shard_map/ppermute | solution.py:174
  124.8 11.0 %collective-permute-start.44 = (bf16[16,2048]{1,0:T(8,128)(2,1)S(1)}, bf16[16,2048]{1,0:T(8,128)(2,1)S(1)}, u32[]{:S(2)}, u32[]{:S(2)}) collective-permute-start(bf16[16,2048]{1,0:T(8,128)(2,1)S(1)} %negate_convert_fusion), channel_id=1, source_target_pairs={{0,8},{4,12},{8,0},{12,4},{1,9},{5,13},{9,1},{13,5},{2,10},{6,14},... | collective-permute-start | bytes 196616 | tf_op jit(solution)/shard_map/ppermute | solution.py:174
  144.2 9.2 %collective-permute-start.48 = (bf16[64,2048]{1,0:T(8,128)(2,1)S(1)}, bf16[64,2048]{1,0:T(8,128)(2,1)S(1)}, u32[]{:S(2)}, u32[]{:S(2)}) collective-permute-start(bf16[64,2048]{1,0:T(8,128)(2,1)S(1)} %get-tuple-element.190.refs_6_), channel_id=1, source_target_pairs={{0,2},{1,3},{2,0},{3,1},{4,6},{5,7},{6,4},{7,5},{8,10},{9,11},{10,... | collective-permute-start | bytes 786440 | tf_op jit(solution)/shard_map/ppermute | solution.py:174
  145.9 13.1 %collective-permute-start.50 = (bf16[64,2048]{1,0:T(8,128)(2,1)S(1)}, bf16[64,2048]{1,0:T(8,128)(2,1)S(1)}, u32[]{:S(2)}, u32[]{:S(2)}) collective-permute-start(bf16[64,2048]{1,0:T(8,128)(2,1)S(1)} %get-tuple-element.188.refs_6_), channel_id=1, source_target_pairs={{0,2},{1,3},{2,0},{3,1},{4,6},{5,7},{6,4},{7,5},{8,10},{9,11},{10,... | collective-permute-start | bytes 786440 | tf_op jit(solution)/shard_map/ppermute | solution.py:174
  146.3 18.3 %collective-permute-start.49 = (bf16[64,2048]{1,0:T(8,128)(2,1)S(1)}, bf16[64,2048]{1,0:T(8,128)(2,1)S(1)}, u32[]{:S(2)}, u32[]{:S(2)}) collective-permute-start(bf16[64,2048]{1,0:T(8,128)(2,1)S(1)} %get-tuple-element.186.refs_3_), channel_id=1, source_target_pairs={{0,2},{1,3},{2,0},{3,1},{4,6},{5,7},{6,4},{7,5},{8,10},{9,11},{10,... | collective-permute-start | bytes 786440 | tf_op jit(solution)/shard_map/ppermute | solution.py:174
  148.0 25.6 %collective-permute-start.51 = (bf16[64,2048]{1,0:T(8,128)(2,1)S(1)}, bf16[64,2048]{1,0:T(8,128)(2,1)S(1)}, u32[]{:S(2)}, u32[]{:S(2)}) collective-permute-start(bf16[64,2048]{1,0:T(8,128)(2,1)S(1)} %get-tuple-element.184), channel_id=1, source_target_pairs={{0,2},{1,3},{2,0},{3,1},{4,6},{5,7},{6,4},{7,5},{8,10},{9,11},{10,... | collective-permute-start | bytes 786440 | tf_op jit(solution)/shard_map/ppermute | solution.py:174
  (40 other events, 358.4 us)

commit v3 on v2

--- a/solution.py
+++ b/solution.py
@@ -156,15 +156,15 @@
 
 
 bf16 = jnp.bfloat16
-SHRINK = 64
+SHRINK = 1 << 20
 f32 = jnp.float32
 ORDER = (0, 2, 1, 3)
 PLAN = (
     "L0", "a0", "a3", "a2", "a1", "F0", "E0", "K0", "F3", "E3", "K3", "F2",
     "s0", "s3", "E2", "K2", "F1", "E1", "K1", "S3", "B0", "s2", "b0", "B2",
-    "s1", "T0", "P0", "b2", "H3", "p0", "B1", "P2", "g3", "p2", "b1", "Q0",
-    "P1", "c0", "Q2", "p1", "C0", "c2", "d0", "Q1", "C2", "W0", "c1", "w0",
-    "d2", "C1", "G3", "W2", "F3", "d1", "w2", "W1", "d3", "w1", "W3", "w3", "U0",
+    "s1", "T0", "P0", "b2", "p0", "B1", "P2", "b1", "p2", "H3", "Q0", "P1",
+    "g3", "c0", "p1", "Q2", "C0", "c2", "d0", "Q1", "C2", "W0", "c1", "w0",
+    "d2", "C1", "G3", "W2", "d1", "w2", "d3", "F3", "W1", "w1", "W3", "w3", "U0",
     "U3",
 )
 
@@ -222,7 +222,7 @@
     )
 
 
-def onto_angles(rows, table, rate=None):
+def onto_angles(rows, table, rate=None, waits=()):
     kinds = 1 if rate is None else 2
     count = rows.shape[0] // 4
     total_rows = kinds * rows.shape[0]
@@ -254,6 +254,7 @@
             jax.ShapeDtypeStruct((total_rows // 2, cols), bf16),
         ),
         *args,
+        waits=waits,
         scratch=[] if rate is None else [pltpu.VMEM((total_rows, depth), bf16)],
         flops=2 * total_rows * depth * cols,
         moved=total_rows * cols * 6,
@@ -405,6 +406,10 @@
 
     def join(name, axis):
         kept, received = held[name]
+        if name == ("corr", 2):
+            own, arrived = held["power", 1]
+            kept, arrived = lax.optimization_barrier((kept, arrived))
+            held["power", 1] = (own, arrived)
         total = after(kept) + received.astype(f32)
         if axis == "batch":
             kept, sent = total, total.astype(bf16)
@@ -444,7 +449,10 @@
         waits = (token[0],)
         if not table:
             waits = tuple(passed["log", s] for s in range(4))
+        if ("coef", 2) in passed:
+            waits += (passed["coef", 2], held["term", 3][0])
         table[t], mark = fetch_table(wigner, t, waits)
+        passed["table"] = mark
         done(mark)
 
     def own_target(_):
@@ -478,14 +486,17 @@
         spread(("back", x), done(value))
 
     def project(x):
-        sent, kept = done(*onto_multipoles(halves_of(("back", x)), table[x])[::-1])
+        waits = (passed["power", 0],) if x == 2 else ()
+        halves = halves_of(("back", x))
+        sent, kept = done(*onto_multipoles(halves, table[x], None, None, waits)[::-1])
         begin(("power", x), kept, sent, "batch")
 
     def pull(x):
         lensed = total_of(("power", x))
         own = held["target"][x].astype(f32)
         residual = done((loss_weight * (lensed - own)).astype(bf16))
-        sent, kept = done(*onto_angles(residual, table[x])[::-1])
+        waits = (passed["power", 1],) if x == 2 else ()
+        sent, kept = done(*onto_angles(residual, table[x], None, waits)[::-1])
         begin(("corr", x), kept, sent, "ell")
 
     def correct(x):
@@ -502,7 +513,10 @@
     def backward(t):
         more = (None, None) if t == 3 else (held["sigma"], lens_rate)
         halves = halves_of(("term", t))
-        waits = tuple(passed["coef", before] for before in {2: (0,), 1: (2,), 3: (1,)}.get(t, ()))
+        waits = tuple(passed["coef", before] for before in {2: (0,), 1: (2,)}.get(t, ()))
+        if t == 1:
+            waits += held["term", 3] + (passed["table"],)
+        waits += tuple(held["coef", before][1] for before in {1: (0, 2)}.get(t, ()))
         sent, kept = done(*onto_multipoles(halves, table[t], *more, waits)[::-1])
         begin(("coef", t), kept, sent, "batch")
 

time: 178 us -> 162 us (0.910)
  waiting for transfers between devices: 46.8 us -> 22.6 us
  starting transfers between devices: 59.2 us -> 68.4 us
    ppermute x52, waiting for transfers between devices: 46.8 us -> 22.6 us  [swap(): return lax.ppermute(value, axis, [(i, i ^ mask) for i in range(count)])]
    ppermute x52, starting transfers between devices: 59.2 us -> 68.4 us  [swap(): return lax.ppermute(value, axis, [(i, i ^ mask) for i in range(count)])]
  transfers between devices with their start and end apart: 52 -> 52, of which waited for: 24 -> 14; matrix products, arithmetic and copies ran while one was open for 3% -> 4% of each run, Pallas kernels for 30% -> 31%
where the time goes in v3:
time: 162 us
  starting transfers between devices  68.4 us (42%)
  Pallas kernels  59.7 us (37%)
  waiting for transfers between devices  22.6 us (14%)
  other arithmetic  6.12 us (4%)
  local copies, waits for them, and re-layouts  3.34 us (2%)
    ppermute x52, starting transfers between devices, swap(): return lax.ppermute(value, axis, [(i, i ^ mask) for i in range(count)])  68.4 us
    pallas_call x19, Pallas kernels, call(): pl.pallas_call(body, out_shape=out_shape, in_specs=[hbm if i in in_hbm el...  47.1 us
    ppermute x52, waiting for transfers between devices, swap(): return lax.ppermute(value, axis, [(i, i ^ mask) for i in range(count)])  22.6 us
    pallas_call x2, Pallas kernels, adam(): pl.pallas_call(kernel, grid=(kinds, depth // tile), out_shape=(jax.ShapeD...  11.8 us
    convert_element_type x11, other arithmetic, join(): kept, sent = (total, total.astype(bf16))  3.55 us
  transfers between devices with their start and end apart: 52, of which 14 were waited for; matrix products, arithmetic and copies ran while one was open for 4% of the time, Pallas kernels for 31%

profile of v3, /device:TPU:0, one launch (start us, length us, event | category | flops | bytes accessed | tf_op | source)
XLA Modules:
  0.0 161.7 jit_solution(11864077683107819899)
XLA Ops:
  7.3 2.9 %collective-permute-start.1 = (bf16[64,2048]{1,0:T(8,128)(2,1)S(1)}, bf16[64,2048]{1,0:T(8,128)(2,1)S(1)}, u32[]{:S(2)}, u32[]{:S(2)}) collective-permute-start(bf16[64,2048]{1,0:T(8,128)(2,1)S(1)} %get-tuple-element.215.refs_1_), channel_id=1, source_target_pairs={{0,2},{1,3},{2,0},{3,1},{4,6},{5,7},{6,4},{7,5},{8,10},{9,11},{10,... | collective-permute-start | bytes 786440 | tf_op jit(solution)/shard_map/ppermute | solution.py:174
  14.6 4.1 %shard_map.95 = (bf16[2048,2048]{1,0:T(8,128)(2,1)S(1)}, f32[8,128]{1,0:T(8,128)}) custom-call(bf16[4,2048,2048]{2,1,0:T(8,128)(2,1)} %refs_0_.11, bf16[64,2048]{1,0:T(8,128)(2,1)S(1)} %get-tuple-element.215.refs_1_, bf16[64,2048]{1,0:T(8,128)(2,1)S(1)} %get-tuple-element.209.refs_2_, bf16[64,2048]{1,0:T(8,128)(2,1)S(1)} %get-tuple-element.211.refs_3_, ...), custom_call_target="tpu_custom_call" | custom-call | bytes 16 | tf_op jit(solution)/shard_map/pallas_call | solution.py:185
  22.2 4.1 %shard_map.97 = (bf16[2048,2048]{1,0:T(8,128)(2,1)S(1)}, f32[8,128]{1,0:T(8,128)}) custom-call(bf16[4,2048,2048]{2,1,0:T(8,128)(2,1)} %refs_0_.11, bf16[64,2048]{1,0:T(8,128)(2,1)S(1)} %get-tuple-element.112.refs_1_), custom_call_target="tpu_custom_call" | custom-call | bytes 16 | tf_op jit(solution)/shard_map/pallas_call | solution.py:185
  28.1 4.1 %shard_map.99 = (bf16[2048,2048]{1,0:T(8,128)(2,1)S(1)}, f32[8,128]{1,0:T(8,128)}) custom-call(bf16[4,2048,2048]{2,1,0:T(8,128)(2,1)} %refs_0_.11, bf16[32,2048]{1,0:T(8,128)(2,1)S(1)} %get-tuple-element.116.refs_1_), custom_call_target="tpu_custom_call" | custom-call | bytes 16 | tf_op jit(solution)/shard_map/pallas_call | solution.py:185
  32.3 3.1 %collective-permute-start.11 = (bf16[32,2048]{1,0:T(8,128)(2,1)S(1)}, bf16[32,2048]{1,0:T(8,128)(2,1)S(1)}, u32[]{:S(2)}, u32[]{:S(2)}) collective-permute-start(bf16[32,2048]{1,0:T(8,128)(2,1)S(1)} %slice.161), channel_id=1, source_target_pairs={{0,8},{4,12},{8,0},{12,4},{1,9},{5,13},{9,1},{13,5},{2,10},{6,14},... | collective-permute-start | bytes 393224 | tf_op jit(solution)/shard_map/ppermute | solution.py:174
  39.0 4.1 %shard_map.101 = (bf16[2048,2048]{1,0:T(8,128)(2,1)S(1)}, f32[8,128]{1,0:T(8,128)}) custom-call(bf16[4,2048,2048]{2,1,0:T(8,128)(2,1)} %refs_0_.11, bf16[64,2048]{1,0:T(8,128)(2,1)S(1)} %get-tuple-element.119.refs_1_), custom_call_target="tpu_custom_call" | custom-call | bytes 16 | tf_op jit(solution)/shard_map/pallas_call | solution.py:185
  45.1 2.7 %collective-permute-start.13 = (bf16[16,2048]{1,0:T(8,128)(2,1)S(1)}, bf16[16,2048]{1,0:T(8,128)(2,1)S(1)}, u32[]{:S(2)}, u32[]{:S(2)}) collective-permute-start(bf16[16,2048]{1,0:T(8,128)(2,1)S(1)} %fusion.17), channel_id=1, source_target_pairs={{0,8},{4,12},{8,0},{12,4},{1,9},{5,13},{9,1},{13,5},{2,10},{6,14},... | collective-permute-start | bytes 196616 | tf_op jit(solution)/shard_map/ppermute | solution.py:174
  47.9 3.4 %collective-permute-start.14 = (bf16[32,2048]{1,0:T(8,128)(2,1)S(1)}, bf16[32,2048]{1,0:T(8,128)(2,1)S(1)}, u32[]{:S(2)}, u32[]{:S(2)}) collective-permute-start(bf16[32,2048]{1,0:T(8,128)(2,1)S(1)} %slice.160), channel_id=1, source_target_pairs={{0,8},{4,12},{8,0},{12,4},{1,9},{5,13},{9,1},{13,5},{2,10},{6,14},... | collective-permute-start | bytes 393224 | tf_op jit(solution)/shard_map/ppermute | solution.py:174
  53.1 3.4 %collective-permute-start.16 = (bf16[32,2048]{1,0:T(8,128)(2,1)S(1)}, bf16[32,2048]{1,0:T(8,128)(2,1)S(1)}, u32[]{:S(2)}, u32[]{:S(2)}) collective-permute-start(bf16[32,2048]{1,0:T(8,128)(2,1)S(1)} %constant_dynamic-update-slice_fusion.refs_0_), channel_id=1, source_target_pairs={{0,4},{4,0},{8,12},{12,8},{1,5},{5,1},{9,13},{13,9},{2,6},{6,2},{1... | collective-permute-start | bytes 393224 | tf_op jit(solution)/shard_map/ppermute | solution.py:174
  61.1 2.4 %shard_map.103 = (f32[64,2048]{1,0:T(8,128)S(1)}, bf16[64,2048]{1,0:T(8,128)(2,1)S(1)}) custom-call(bf16[32,2048]{1,0:T(8,128)(2,1)S(1)} %constant_dynamic-update-slice_fusion.refs_0_, bf16[32,2048]{1,0:T(8,128)(2,1)S(1)} %collective-permute-done.16.refs_1_, bf16[2048,2048]{1,0:T(8,128)(2,1)S(1)} %get-tuple-element.110.refs_2_.refs_1_.refs_5_), custom_call_target="tpu_custom_call" | custom-call | flops 512 | tf_op jit(solution)/shard_map/pallas_call | solution.py:185
  63.6 3.0 %collective-permute-start.20 = (bf16[32,2048]{1,0:T(8,128)(2,1)S(1)}, bf16[32,2048]{1,0:T(8,128)(2,1)S(1)}, u32[]{:S(2)}, u32[]{:S(2)}) collective-permute-start(bf16[32,2048]{1,0:T(8,128)(2,1)S(1)} %constant_dynamic-update-slice_fusion.2.refs_0_), channel_id=1, source_target_pairs={{0,4},{4,0},{8,12},{12,8},{1,5},{5,1},{9,13},{13,9},{2,6},{6,2},{1... | collective-permute-start | bytes 393224 | tf_op jit(solution)/shard_map/ppermute | solution.py:174
  66.7 2.9 %collective-permute-start.21 = (bf16[16,2048]{1,0:T(8,128)(2,1)S(1)}, bf16[16,2048]{1,0:T(8,128)(2,1)S(1)}, u32[]{:S(2)}, u32[]{:S(2)}) collective-permute-start(bf16[16,2048]{1,0:T(8,128)(2,1)S(1)} %fusion.13), channel_id=1, source_target_pairs={{0,8},{4,12},{8,0},{12,4},{1,9},{5,13},{9,1},{13,5},{2,10},{6,14},... | collective-permute-start | bytes 196616 | tf_op jit(solution)/shard_map/ppermute | solution.py:174
  75.4 2.4 %collective-permute-done.23 = bf16[64,2048]{1,0:T(8,128)(2,1)S(1)} collective-permute-done((bf16[64,2048]{1,0:T(8,128)(2,1)S(1)}, bf16[64,2048]{1,0:T(8,128)(2,1)S(1)}, u32[]{:S(2)}, u32[]{:S(2)}) %collective-permute-start.23) | collective-permute-done | bytes 262176 | tf_op jit(solution)/shard_map/ppermute | solution.py:174
  86.5 2.6 %collective-permute-start.29 = (bf16[16,2048]{1,0:T(8,128)(2,1)S(1)}, bf16[16,2048]{1,0:T(8,128)(2,1)S(1)}, u32[]{:S(2)}, u32[]{:S(2)}) collective-permute-start(bf16[16,2048]{1,0:T(8,128)(2,1)S(1)} %slice.164), channel_id=1, source_target_pairs={{0,8},{4,12},{8,0},{12,4},{1,9},{5,13},{9,1},{13,5},{2,10},{6,14},... | collective-permute-start | bytes 196616 | tf_op jit(solution)/shard_map/ppermute | solution.py:174
  95.0 2.5 %collective-permute-done.30 = bf16[64,2048]{1,0:T(8,128)(2,1)S(1)} collective-permute-done((bf16[64,2048]{1,0:T(8,128)(2,1)S(1)}, bf16[64,2048]{1,0:T(8,128)(2,1)S(1)}, u32[]{:S(2)}, u32[]{:S(2)}) %collective-permute-start.30) | collective-permute-done | bytes 262176 | tf_op jit(solution)/shard_map/ppermute | solution.py:174
  103.5 2.9 %collective-permute-start.38 = (bf16[16,2048]{1,0:T(8,128)(2,1)S(1)}, bf16[16,2048]{1,0:T(8,128)(2,1)S(1)}, u32[]{:S(2)}, u32[]{:S(2)}) collective-permute-start(bf16[16,2048]{1,0:T(8,128)(2,1)S(1)} %fusion.18), channel_id=1, source_target_pairs={{0,8},{4,12},{8,0},{12,4},{1,9},{5,13},{9,1},{13,5},{2,10},{6,14},... | collective-permute-start | bytes 196616 | tf_op jit(solution)/shard_map/ppermute | solution.py:174
  106.5 2.4 %shard_map.109 = (f32[64,2048]{1,0:T(8,128)S(1)}, bf16[64,2048]{1,0:T(8,128)(2,1)S(1)}) custom-call(bf16[32,2048]{1,0:T(8,128)(2,1)S(1)} %constant_dynamic-update-slice_fusion.8.refs_0_, bf16[32,2048]{1,0:T(8,128)(2,1)S(1)} %collective-permute-done.34.refs_1_, bf16[32,2048]{1,0:T(8,128)(2,1)S(1)} %constant_dynamic-update-slice_fusion.6.refs_2_, ...), custom_call_target="tpu_custom_call" | custom-call | flops 1024 | tf_op jit(solution)/shard_map/pallas_call | solution.py:185
  113.0 2.7 %collective-permute-done.39 = bf16[16,2048]{1,0:T(8,128)(2,1)S(1)} collective-permute-done((bf16[16,2048]{1,0:T(8,128)(2,1)S(1)}, bf16[16,2048]{1,0:T(8,128)(2,1)S(1)}, u32[]{:S(2)}, u32[]{:S(2)}) %collective-permute-start.39) | collective-permute-done | bytes 65568 | tf_op jit(solution)/shard_map/ppermute | solution.py:174
  120.3 2.4 %shard_map.110 = (f32[64,2048]{1,0:T(8,128)S(1)}, bf16[64,2048]{1,0:T(8,128)(2,1)S(1)}) custom-call(bf16[32,2048]{1,0:T(8,128)(2,1)S(1)} %constant_dynamic-update-slice_fusion.10.refs_0_, bf16[32,2048]{1,0:T(8,128)(2,1)S(1)} %collective-permute-done.40.refs_1_, bf16[32,2048]{1,0:T(8,128)(2,1)S(1)} %constant_dynamic-update-slice_fusion.6.refs_2_, ...), custom_call_target="tpu_custom_call" | custom-call | flops 1024 | tf_op jit(solution)/shard_map/pallas_call | solution.py:185
  128.2 3.5 %shard_map.111 = (bf16[2048,2048]{1,0:T(8,128)(2,1)S(1)}, f32[8,128]{1,0:T(8,128)S(1)}) custom-call(bf16[4,2048,2048]{2,1,0:T(8,128)(2,1)} %refs_0_.11, bf16[32,2048]{1,0:T(8,128)(2,1)S(1)} %constant_dynamic-update-slice_fusion.14.refs_1_.refs_3_.refs_7_.refs_0_, bf16[64,2048]{1,0:T(8,128)(2,1)S(1)} %get-tuple-element.195.refs_2_.refs_6_, ...), custom_call_target="tpu_custom_call" | custom-call | bytes 16 | tf_op jit(solution)/shard_map/pallas_call | solution.py:185
  132.8 2.7 %shard_map.112 = (f32[64,2048]{1,0:T(8,128)S(1)}, bf16[64,2048]{1,0:T(8,128)(2,1)S(1)}) custom-call(bf16[32,2048]{1,0:T(8,128)(2,1)S(1)} %constant_dynamic-update-slice_fusion.12.refs_0_, bf16[32,2048]{1,0:T(8,128)(2,1)S(1)} %collective-permute-done.44.refs_1_, bf16[32,2048]{1,0:T(8,128)(2,1)S(1)} %constant_dynamic-update-slice_fusion.6.refs_2_, ...), custom_call_target="tpu_custom_call" | custom-call | flops 1024 | tf_op jit(solution)/shard_map/pallas_call | solution.py:185
  142.8 6.2 %collective-permute-done.50 = bf16[64,2048]{1,0:T(8,128)(2,1)S(1)} collective-permute-done((bf16[64,2048]{1,0:T(8,128)(2,1)S(1)}, bf16[64,2048]{1,0:T(8,128)(2,1)S(1)}, u32[]{:S(2)}, u32[]{:S(2)}) %collective-permute-start.50) | collective-permute-done | bytes 262176 | tf_op jit(solution)/shard_map/ppermute | solution.py:174
  149.7 8.3 %shard_map.114 = (bf16[4,256,2048]{2,1,0:T(8,128)(2,1)}, f32[4,256,2048]{2,1,0:T(8,128)}, f32[4,256,2048]{2,1,0:T(8,128)}) custom-call(bf16[64,256]{1,0:T(8,128)(2,1)S(1)} %pad_maximum_fusion.2.hid, bf16[3,64,2048]{2,1,0:T(8,128)(2,1)S(1)} %pad_maximum_fusion.1.grad, bf16[4,256,2048]{2,1,0:T(8,128)(2,1)S(1)} %copy-done.1, f32[4,256,2048]{2,1,0:T(8,128)S(1)} %bitcast.24, ...), custom_call_target="tpu_custom_call" | custom-call | flops 201326592 | bytes 31457280 | tf_op jit(solution)/shard_map/pallas_call | solution.py:349
  158.1 3.5 %shard_map.115 = (bf16[4,256,2048]{2,1,0:T(8,128)(2,1)}, f32[4,256,2048]{2,1,0:T(8,128)}, f32[4,256,2048]{2,1,0:T(8,128)}) custom-call(bf16[64,256]{1,0:T(8,128)(2,1)S(1)} %pad_maximum_fusion.2.hid, bf16[1,64,2048]{2,1,0:T(8,128)(2,1)S(1)} %fusion.11.grad, ...), custom_call_target="tpu_custom_call", output_to_operand_aliasing={{0}: (5, {}), {1}: (6, {}), {2}: (7, {})} | custom-call | flops 67108864 | bytes 10485760 | tf_op jit(solution)/shard_map/pallas_call | solution.py:349
  (201 shorter events, 78.0 us)
Async XLA Ops:
  5.5 8.9 %collective-permute-start.4 = (bf16[64,2048]{1,0:T(8,128)(2,1)S(1)}, bf16[64,2048]{1,0:T(8,128)(2,1)S(1)}, u32[]{:S(2)}, u32[]{:S(2)}) collective-permute-start(bf16[64,2048]{1,0:T(8,128)(2,1)S(1)} %get-tuple-element.99), channel_id=1, source_target_pairs={{0,1},{1,0},{2,3},{3,2},{4,5},{5,4},{6,7},{7,6},{8,9},{9,8},{10,11... | collective-permute-start | bytes 786440 | tf_op jit(solution)/shard_map/ppermute | solution.py:174
  7.3 11.3 %collective-permute-start.1 = (bf16[64,2048]{1,0:T(8,128)(2,1)S(1)}, bf16[64,2048]{1,0:T(8,128)(2,1)S(1)}, u32[]{:S(2)}, u32[]{:S(2)}) collective-permute-start(bf16[64,2048]{1,0:T(8,128)(2,1)S(1)} %get-tuple-element.215.refs_1_), channel_id=1, source_target_pairs={{0,2},{1,3},{2,0},{3,1},{4,6},{5,7},{6,4},{7,5},{8,10},{9,11},{10,... | collective-permute-start | bytes 786440 | tf_op jit(solution)/shard_map/ppermute | solution.py:174
  11.2 15.1 %collective-permute-start.6 = (bf16[64,2048]{1,0:T(8,128)(2,1)S(1)}, bf16[64,2048]{1,0:T(8,128)(2,1)S(1)}, u32[]{:S(2)}, u32[]{:S(2)}) collective-permute-start(bf16[64,2048]{1,0:T(8,128)(2,1)S(1)} %get-tuple-element.213.refs_4_), channel_id=1, source_target_pairs={{0,2},{1,3},{2,0},{3,1},{4,6},{5,7},{6,4},{7,5},{8,10},{9,11},{10,... | collective-permute-start | bytes 786440 | tf_op jit(solution)/shard_map/ppermute | solution.py:174
  12.3 23.4 %collective-permute-start.9 = (bf16[64,2048]{1,0:T(8,128)(2,1)S(1)}, bf16[64,2048]{1,0:T(8,128)(2,1)S(1)}, u32[]{:S(2)}, u32[]{:S(2)}) collective-permute-start(bf16[64,2048]{1,0:T(8,128)(2,1)S(1)} %get-tuple-element.211.refs_3_), channel_id=1, source_target_pairs={{0,2},{1,3},{2,0},{3,1},{4,6},{5,7},{6,4},{7,5},{8,10},{9,11},{10,... | collective-permute-start | bytes 786440 | tf_op jit(solution)/shard_map/ppermute | solution.py:174
  14.5 21.3 %collective-permute-start.8 = (bf16[64,2048]{1,0:T(8,128)(2,1)S(1)}, bf16[64,2048]{1,0:T(8,128)(2,1)S(1)}, u32[]{:S(2)}, u32[]{:S(2)}) collective-permute-start(bf16[64,2048]{1,0:T(8,128)(2,1)S(1)} %get-tuple-element.209.refs_2_), channel_id=1, source_target_pairs={{0,2},{1,3},{2,0},{3,1},{4,6},{5,7},{6,4},{7,5},{8,10},{9,11},{10,... | collective-permute-start | bytes 786440 | tf_op jit(solution)/shard_map/ppermute | solution.py:174
  20.1 12.1 %collective-permute-start.5 = (bf16[64,2048]{1,0:T(8,128)(2,1)S(1)}, bf16[64,2048]{1,0:T(8,128)(2,1)S(1)}, u32[]{:S(2)}, u32[]{:S(2)}) collective-permute-start(bf16[64,2048]{1,0:T(8,128)(2,1)S(1)} %get-tuple-element.112.refs_1_), channel_id=1, source_target_pairs={{0,4},{4,0},{8,12},{12,8},{1,5},{5,1},{9,13},{13,9},{2,6},{6,2},{1... | collective-permute-start | bytes 786440 | tf_op jit(solution)/shard_map/ppermute | solution.py:174
  32.3 12.7 %collective-permute-start.11 = (bf16[32,2048]{1,0:T(8,128)(2,1)S(1)}, bf16[32,2048]{1,0:T(8,128)(2,1)S(1)}, u32[]{:S(2)}, u32[]{:S(2)}) collective-permute-start(bf16[32,2048]{1,0:T(8,128)(2,1)S(1)} %slice.161), channel_id=1, source_target_pairs={{0,8},{4,12},{8,0},{12,4},{1,9},{5,13},{9,1},{13,5},{2,10},{6,14},... | collective-permute-start | bytes 393224 | tf_op jit(solution)/shard_map/ppermute | solution.py:174
  35.4 9.6 %collective-permute-start.10 = (bf16[16,2048]{1,0:T(8,128)(2,1)S(1)}, bf16[16,2048]{1,0:T(8,128)(2,1)S(1)}, u32[]{:S(2)}, u32[]{:S(2)}) collective-permute-start(bf16[16,2048]{1,0:T(8,128)(2,1)S(1)} %slice.165), channel_id=1, source_target_pairs={{0,8},{4,12},{8,0},{12,4},{1,9},{5,13},{9,1},{13,5},{2,10},{6,14},... | collective-permute-start | bytes 196616 | tf_op jit(solution)/shard_map/ppermute | solution.py:174
  37.3 10.5 %collective-permute-start.12 = (bf16[64,2048]{1,0:T(8,128)(2,1)S(1)}, bf16[64,2048]{1,0:T(8,128)(2,1)S(1)}, u32[]{:S(2)}, u32[]{:S(2)}) collective-permute-start(bf16[64,2048]{1,0:T(8,128)(2,1)S(1)} %get-tuple-element.119.refs_1_), channel_id=1, source_target_pairs={{0,4},{4,0},{8,12},{12,8},{1,5},{5,1},{9,13},{13,9},{2,6},{6,2},{1... | collective-permute-start | bytes 786440 | tf_op jit(solution)/shard_map/ppermute | solution.py:174
  44.5 14.4 %collective-permute-start.15 = (bf16[64,2048]{1,0:T(8,128)(2,1)S(1)}, bf16[64,2048]{1,0:T(8,128)(2,1)S(1)}, u32[]{:S(2)}, u32[]{:S(2)}) collective-permute-start(bf16[64,2048]{1,0:T(8,128)(2,1)S(1)} %get-tuple-element.121), channel_id=1, source_target_pairs={{0,4},{4,0},{8,12},{12,8},{1,5},{5,1},{9,13},{13,9},{2,6},{6,2},{1... | collective-permute-start | bytes 786440 | tf_op jit(solution)/shard_map/ppermute | solution.py:174
  45.1 8.0 %collective-permute-start.13 = (bf16[16,2048]{1,0:T(8,128)(2,1)S(1)}, bf16[16,2048]{1,0:T(8,128)(2,1)S(1)}, u32[]{:S(2)}, u32[]{:S(2)}) collective-permute-start(bf16[16,2048]{1,0:T(8,128)(2,1)S(1)} %fusion.17), channel_id=1, source_target_pairs={{0,8},{4,12},{8,0},{12,4},{1,9},{5,13},{9,1},{13,5},{2,10},{6,14},... | collective-permute-start | bytes 196616 | tf_op jit(solution)/shard_map/ppermute | solution.py:174
  47.9 8.6 %collective-permute-start.14 = (bf16[32,2048]{1,0:T(8,128)(2,1)S(1)}, bf16[32,2048]{1,0:T(8,128)(2,1)S(1)}, u32[]{:S(2)}, u32[]{:S(2)}) collective-permute-start(bf16[32,2048]{1,0:T(8,128)(2,1)S(1)} %slice.160), channel_id=1, source_target_pairs={{0,8},{4,12},{8,0},{12,4},{1,9},{5,13},{9,1},{13,5},{2,10},{6,14},... | collective-permute-start | bytes 393224 | tf_op jit(solution)/shard_map/ppermute | solution.py:174
  53.1 7.9 %collective-permute-start.16 = (bf16[32,2048]{1,0:T(8,128)(2,1)S(1)}, bf16[32,2048]{1,0:T(8,128)(2,1)S(1)}, u32[]{:S(2)}, u32[]{:S(2)}) collective-permute-start(bf16[32,2048]{1,0:T(8,128)(2,1)S(1)} %constant_dynamic-update-slice_fusion.refs_0_), channel_id=1, source_target_pairs={{0,4},{4,0},{8,12},{12,8},{1,5},{5,1},{9,13},{13,9},{2,6},{6,2},{1... | collective-permute-start | bytes 393224 | tf_op jit(solution)/shard_map/ppermute | solution.py:174
  69.6 8.1 %collective-permute-start.23 = (bf16[64,2048]{1,0:T(8,128)(2,1)S(1)}, bf16[64,2048]{1,0:T(8,128)(2,1)S(1)}, u32[]{:S(2)}, u32[]{:S(2)}) collective-permute-start(bf16[64,2048]{1,0:T(8,128)(2,1)S(1)} %get-tuple-element.205.refs_3_), channel_id=1, source_target_pairs={{0,2},{1,3},{2,0},{3,1},{4,6},{5,7},{6,4},{7,5},{8,10},{9,11},{10,... | collective-permute-start | bytes 786440 | tf_op jit(solution)/shard_map/ppermute | solution.py:174
  73.8 9.5 %collective-permute-start.24 = (bf16[32,2048]{1,0:T(8,128)(2,1)S(1)}, bf16[32,2048]{1,0:T(8,128)(2,1)S(1)}, u32[]{:S(2)}, u32[]{:S(2)}) collective-permute-start(bf16[32,2048]{1,0:T(8,128)(2,1)S(1)} %constant_dynamic-update-slice_fusion.4.refs_0_), channel_id=1, source_target_pairs={{0,4},{4,0},{8,12},{12,8},{1,5},{5,1},{9,13},{13,9},{2,6},{6,2},{1... | collective-permute-start | bytes 393224 | tf_op jit(solution)/shard_map/ppermute | solution.py:174
  81.6 7.8 %collective-permute-start.28 = (bf16[64,2048]{1,0:T(8,128)(2,1)S(1)}, bf16[64,2048]{1,0:T(8,128)(2,1)S(1)}, u32[]{:S(2)}, u32[]{:S(2)}) collective-permute-start(bf16[64,2048]{1,0:T(8,128)(2,1)S(1)} %get-tuple-element.203), channel_id=1, source_target_pairs={{0,2},{1,3},{2,0},{3,1},{4,6},{5,7},{6,4},{7,5},{8,10},{9,11},{10,... | collective-permute-start | bytes 786440 | tf_op jit(solution)/shard_map/ppermute | solution.py:174
  85.8 20.6 %collective-permute-start.35 = (bf16[32,2048]{1,0:T(8,128)(2,1)S(1)}, bf16[32,2048]{1,0:T(8,128)(2,1)S(1)}, u32[]{:S(2)}, u32[]{:S(2)}) collective-permute-start(bf16[32,2048]{1,0:T(8,128)(2,1)S(1)} %constant_dynamic-update-slice_fusion.6.refs_2_), channel_id=1, source_target_pairs={{0,4},{4,0},{8,12},{12,8},{1,5},{5,1},{9,13},{13,9},{2,6},{6,2},{1... | collective-permute-start | bytes 393224 | tf_op jit(solution)/shard_map/ppermute | solution.py:174
  89.5 8.0 %collective-permute-start.30 = (bf16[64,2048]{1,0:T(8,128)(2,1)S(1)}, bf16[64,2048]{1,0:T(8,128)(2,1)S(1)}, u32[]{:S(2)}, u32[]{:S(2)}) collective-permute-start(bf16[64,2048]{1,0:T(8,128)(2,1)S(1)} %get-tuple-element.201.refs_2_), channel_id=1, source_target_pairs={{0,2},{1,3},{2,0},{3,1},{4,6},{5,7},{6,4},{7,5},{8,10},{9,11},{10,... | collective-permute-start | bytes 786440 | tf_op jit(solution)/shard_map/ppermute | solution.py:174
  103.5 8.0 %collective-permute-start.38 = (bf16[16,2048]{1,0:T(8,128)(2,1)S(1)}, bf16[16,2048]{1,0:T(8,128)(2,1)S(1)}, u32[]{:S(2)}, u32[]{:S(2)}) collective-permute-start(bf16[16,2048]{1,0:T(8,128)(2,1)S(1)} %fusion.18), channel_id=1, source_target_pairs={{0,8},{4,12},{8,0},{12,4},{1,9},{5,13},{9,1},{13,5},{2,10},{6,14},... | collective-permute-start | bytes 196616 | tf_op jit(solution)/shard_map/ppermute | solution.py:174
  111.5 8.9 %collective-permute-start.40 = (bf16[32,2048]{1,0:T(8,128)(2,1)S(1)}, bf16[32,2048]{1,0:T(8,128)(2,1)S(1)}, u32[]{:S(2)}, u32[]{:S(2)}) collective-permute-start(bf16[32,2048]{1,0:T(8,128)(2,1)S(1)} %constant_dynamic-update-slice_fusion.10.refs_0_), channel_id=1, source_target_pairs={{0,4},{4,0},{8,12},{12,8},{1,5},{5,1},{9,13},{13,9},{2,6},{6,2},{1... | collective-permute-start | bytes 393224 | tf_op jit(solution)/shard_map/ppermute | solution.py:174
  115.8 10.3 %collective-permute-start.43 = (bf16[16,2048]{1,0:T(8,128)(2,1)S(1)}, bf16[16,2048]{1,0:T(8,128)(2,1)S(1)}, u32[]{:S(2)}, u32[]{:S(2)}) collective-permute-start(bf16[16,2048]{1,0:T(8,128)(2,1)S(1)} %negate_convert_fusion), channel_id=1, source_target_pairs={{0,8},{4,12},{8,0},{12,4},{1,9},{5,13},{9,1},{13,5},{2,10},{6,14},... | collective-permute-start | bytes 196616 | tf_op jit(solution)/shard_map/ppermute | solution.py:174
  118.7 12.9 %collective-permute-start.46 = (bf16[64,2048]{1,0:T(8,128)(2,1)S(1)}, bf16[64,2048]{1,0:T(8,128)(2,1)S(1)}, u32[]{:S(2)}, u32[]{:S(2)}) collective-permute-start(bf16[64,2048]{1,0:T(8,128)(2,1)S(1)} %get-tuple-element.197.refs_6_), channel_id=1, source_target_pairs={{0,2},{1,3},{2,0},{3,1},{4,6},{5,7},{6,4},{7,5},{8,10},{9,11},{10,... | collective-permute-start | bytes 786440 | tf_op jit(solution)/shard_map/ppermute | solution.py:174
  139.8 9.1 %collective-permute-start.50 = (bf16[64,2048]{1,0:T(8,128)(2,1)S(1)}, bf16[64,2048]{1,0:T(8,128)(2,1)S(1)}, u32[]{:S(2)}, u32[]{:S(2)}) collective-permute-start(bf16[64,2048]{1,0:T(8,128)(2,1)S(1)} %get-tuple-element.193), channel_id=1, source_target_pairs={{0,2},{1,3},{2,0},{3,1},{4,6},{5,7},{6,4},{7,5},{8,10},{9,11},{10,... | collective-permute-start | bytes 786440 | tf_op jit(solution)/shard_map/ppermute | solution.py:174
  141.3 16.7 %collective-permute-start.51 = (bf16[64,2048]{1,0:T(8,128)(2,1)S(1)}, bf16[64,2048]{1,0:T(8,128)(2,1)S(1)}, u32[]{:S(2)}, u32[]{:S(2)}) collective-permute-start(bf16[64,2048]{1,0:T(8,128)(2,1)S(1)} %get-tuple-element.191), channel_id=1, source_target_pairs={{0,2},{1,3},{2,0},{3,1},{4,6},{5,7},{6,4},{7,5},{8,10},{9,11},{10,... | collective-permute-start | bytes 786440 | tf_op jit(solution)/shard_map/ppermute | solution.py:174
  (40 other events, 285.2 us)

commit v4 on v3

--- a/solution.py
+++ b/solution.py
@@ -341,7 +341,9 @@
         spread = 0.999 * two[...] + 0.001 * slope * slope
         new_one[...] = moved
         new_two[...] = spread
-        update = moved * (1.0 / first_fix) / (jnp.sqrt(spread * (1.0 / second_fix)) + 1e-08)
+        scaled = spread * (1.0 / second_fix)
+        root = scaled * lax.rsqrt(scaled)
+        update = moved * (1.0 / first_fix) / (root + 1e-08)
         new_wgt[...] = (wgt[...].astype(f32) - 0.001 * update).astype(bf16)
 
     block = pl.BlockSpec((None, tile, cols), lambda s, i: (first_kind + s, i, 0))

time: 162 us -> 161 us (level)
  no operation moved by 1% of the time
where the time goes in v4:
time: 161 us
  starting transfers between devices  68.4 us (42%)
  Pallas kernels  58.8 us (37%)
  waiting for transfers between devices  22.6 us (14%)
  other arithmetic  6.12 us (4%)
  local copies, waits for them, and re-layouts  3.34 us (2%)
    ppermute x52, starting transfers between devices, swap(): return lax.ppermute(value, axis, [(i, i ^ mask) for i in range(count)])  68.4 us
    pallas_call x19, Pallas kernels, call(): pl.pallas_call(body, out_shape=out_shape, in_specs=[hbm if i in in_hbm el...  47.1 us
    ppermute x52, waiting for transfers between devices, swap(): return lax.ppermute(value, axis, [(i, i ^ mask) for i in range(count)])  22.6 us
    pallas_call x2, Pallas kernels, adam(): pl.pallas_call(kernel, grid=(kinds, depth // tile), out_shape=(jax.ShapeD...  10.8 us
    convert_element_type x11, other arithmetic, join(): kept, sent = (total, total.astype(bf16))  3.55 us
  transfers between devices with their start and end apart: 52, of which 14 were waited for; matrix products, arithmetic and copies ran while one was open for 4% of the time, Pallas kernels for 31%

profile of v4, /device:TPU:0, one launch (start us, length us, event | category | flops | bytes accessed | tf_op | source)
XLA Modules:
  0.0 160.7 jit_solution(6045539722038364132)
XLA Ops:
  7.3 2.9 %collective-permute-start.1 = (bf16[64,2048]{1,0:T(8,128)(2,1)S(1)}, bf16[64,2048]{1,0:T(8,128)(2,1)S(1)}, u32[]{:S(2)}, u32[]{:S(2)}) collective-permute-start(bf16[64,2048]{1,0:T(8,128)(2,1)S(1)} %get-tuple-element.215.refs_1_), channel_id=1, source_target_pairs={{0,2},{1,3},{2,0},{3,1},{4,6},{5,7},{6,4},{7,5},{8,10},{9,11},{10,... | collective-permute-start | bytes 786440 | tf_op jit(solution)/shard_map/ppermute | solution.py:174
  14.6 4.1 %shard_map.95 = (bf16[2048,2048]{1,0:T(8,128)(2,1)S(1)}, f32[8,128]{1,0:T(8,128)}) custom-call(bf16[4,2048,2048]{2,1,0:T(8,128)(2,1)} %refs_0_.11, bf16[64,2048]{1,0:T(8,128)(2,1)S(1)} %get-tuple-element.215.refs_1_, bf16[64,2048]{1,0:T(8,128)(2,1)S(1)} %get-tuple-element.209.refs_2_, bf16[64,2048]{1,0:T(8,128)(2,1)S(1)} %get-tuple-element.211.refs_3_, ...), custom_call_target="tpu_custom_call" | custom-call | bytes 16 | tf_op jit(solution)/shard_map/pallas_call | solution.py:185
  22.2 4.1 %shard_map.97 = (bf16[2048,2048]{1,0:T(8,128)(2,1)S(1)}, f32[8,128]{1,0:T(8,128)}) custom-call(bf16[4,2048,2048]{2,1,0:T(8,128)(2,1)} %refs_0_.11, bf16[64,2048]{1,0:T(8,128)(2,1)S(1)} %get-tuple-element.112.refs_1_), custom_call_target="tpu_custom_call" | custom-call | bytes 16 | tf_op jit(solution)/shard_map/pallas_call | solution.py:185
  28.1 4.1 %shard_map.99 = (bf16[2048,2048]{1,0:T(8,128)(2,1)S(1)}, f32[8,128]{1,0:T(8,128)}) custom-call(bf16[4,2048,2048]{2,1,0:T(8,128)(2,1)} %refs_0_.11, bf16[32,2048]{1,0:T(8,128)(2,1)S(1)} %get-tuple-element.116.refs_1_), custom_call_target="tpu_custom_call" | custom-call | bytes 16 | tf_op jit(solution)/shard_map/pallas_call | solution.py:185
  32.3 3.1 %collective-permute-start.11 = (bf16[32,2048]{1,0:T(8,128)(2,1)S(1)}, bf16[32,2048]{1,0:T(8,128)(2,1)S(1)}, u32[]{:S(2)}, u32[]{:S(2)}) collective-permute-start(bf16[32,2048]{1,0:T(8,128)(2,1)S(1)} %slice.161), channel_id=1, source_target_pairs={{0,8},{4,12},{8,0},{12,4},{1,9},{5,13},{9,1},{13,5},{2,10},{6,14},... | collective-permute-start | bytes 393224 | tf_op jit(solution)/shard_map/ppermute | solution.py:174
  39.0 4.1 %shard_map.101 = (bf16[2048,2048]{1,0:T(8,128)(2,1)S(1)}, f32[8,128]{1,0:T(8,128)}) custom-call(bf16[4,2048,2048]{2,1,0:T(8,128)(2,1)} %refs_0_.11, bf16[64,2048]{1,0:T(8,128)(2,1)S(1)} %get-tuple-element.119.refs_1_), custom_call_target="tpu_custom_call" | custom-call | bytes 16 | tf_op jit(solution)/shard_map/pallas_call | solution.py:185
  45.1 2.7 %collective-permute-start.13 = (bf16[16,2048]{1,0:T(8,128)(2,1)S(1)}, bf16[16,2048]{1,0:T(8,128)(2,1)S(1)}, u32[]{:S(2)}, u32[]{:S(2)}) collective-permute-start(bf16[16,2048]{1,0:T(8,128)(2,1)S(1)} %fusion.17), channel_id=1, source_target_pairs={{0,8},{4,12},{8,0},{12,4},{1,9},{5,13},{9,1},{13,5},{2,10},{6,14},... | collective-permute-start | bytes 196616 | tf_op jit(solution)/shard_map/ppermute | solution.py:174
  47.9 3.4 %collective-permute-start.14 = (bf16[32,2048]{1,0:T(8,128)(2,1)S(1)}, bf16[32,2048]{1,0:T(8,128)(2,1)S(1)}, u32[]{:S(2)}, u32[]{:S(2)}) collective-permute-start(bf16[32,2048]{1,0:T(8,128)(2,1)S(1)} %slice.160), channel_id=1, source_target_pairs={{0,8},{4,12},{8,0},{12,4},{1,9},{5,13},{9,1},{13,5},{2,10},{6,14},... | collective-permute-start | bytes 393224 | tf_op jit(solution)/shard_map/ppermute | solution.py:174
  53.1 3.4 %collective-permute-start.16 = (bf16[32,2048]{1,0:T(8,128)(2,1)S(1)}, bf16[32,2048]{1,0:T(8,128)(2,1)S(1)}, u32[]{:S(2)}, u32[]{:S(2)}) collective-permute-start(bf16[32,2048]{1,0:T(8,128)(2,1)S(1)} %constant_dynamic-update-slice_fusion.refs_0_), channel_id=1, source_target_pairs={{0,4},{4,0},{8,12},{12,8},{1,5},{5,1},{9,13},{13,9},{2,6},{6,2},{1... | collective-permute-start | bytes 393224 | tf_op jit(solution)/shard_map/ppermute | solution.py:174
  61.1 2.4 %shard_map.103 = (f32[64,2048]{1,0:T(8,128)S(1)}, bf16[64,2048]{1,0:T(8,128)(2,1)S(1)}) custom-call(bf16[32,2048]{1,0:T(8,128)(2,1)S(1)} %constant_dynamic-update-slice_fusion.refs_0_, bf16[32,2048]{1,0:T(8,128)(2,1)S(1)} %collective-permute-done.16.refs_1_, bf16[2048,2048]{1,0:T(8,128)(2,1)S(1)} %get-tuple-element.110.refs_2_.refs_1_.refs_5_), custom_call_target="tpu_custom_call" | custom-call | flops 512 | tf_op jit(solution)/shard_map/pallas_call | solution.py:185
  63.6 3.0 %collective-permute-start.20 = (bf16[32,2048]{1,0:T(8,128)(2,1)S(1)}, bf16[32,2048]{1,0:T(8,128)(2,1)S(1)}, u32[]{:S(2)}, u32[]{:S(2)}) collective-permute-start(bf16[32,2048]{1,0:T(8,128)(2,1)S(1)} %constant_dynamic-update-slice_fusion.2.refs_0_), channel_id=1, source_target_pairs={{0,4},{4,0},{8,12},{12,8},{1,5},{5,1},{9,13},{13,9},{2,6},{6,2},{1... | collective-permute-start | bytes 393224 | tf_op jit(solution)/shard_map/ppermute | solution.py:174
  66.7 2.9 %collective-permute-start.21 = (bf16[16,2048]{1,0:T(8,128)(2,1)S(1)}, bf16[16,2048]{1,0:T(8,128)(2,1)S(1)}, u32[]{:S(2)}, u32[]{:S(2)}) collective-permute-start(bf16[16,2048]{1,0:T(8,128)(2,1)S(1)} %fusion.13), channel_id=1, source_target_pairs={{0,8},{4,12},{8,0},{12,4},{1,9},{5,13},{9,1},{13,5},{2,10},{6,14},... | collective-permute-start | bytes 196616 | tf_op jit(solution)/shard_map/ppermute | solution.py:174
  75.4 2.4 %collective-permute-done.23 = bf16[64,2048]{1,0:T(8,128)(2,1)S(1)} collective-permute-done((bf16[64,2048]{1,0:T(8,128)(2,1)S(1)}, bf16[64,2048]{1,0:T(8,128)(2,1)S(1)}, u32[]{:S(2)}, u32[]{:S(2)}) %collective-permute-start.23) | collective-permute-done | bytes 262176 | tf_op jit(solution)/shard_map/ppermute | solution.py:174
  86.5 2.6 %collective-permute-start.29 = (bf16[16,2048]{1,0:T(8,128)(2,1)S(1)}, bf16[16,2048]{1,0:T(8,128)(2,1)S(1)}, u32[]{:S(2)}, u32[]{:S(2)}) collective-permute-start(bf16[16,2048]{1,0:T(8,128)(2,1)S(1)} %slice.164), channel_id=1, source_target_pairs={{0,8},{4,12},{8,0},{12,4},{1,9},{5,13},{9,1},{13,5},{2,10},{6,14},... | collective-permute-start | bytes 196616 | tf_op jit(solution)/shard_map/ppermute | solution.py:174
  95.0 2.5 %collective-permute-done.30 = bf16[64,2048]{1,0:T(8,128)(2,1)S(1)} collective-permute-done((bf16[64,2048]{1,0:T(8,128)(2,1)S(1)}, bf16[64,2048]{1,0:T(8,128)(2,1)S(1)}, u32[]{:S(2)}, u32[]{:S(2)}) %collective-permute-start.30) | collective-permute-done | bytes 262176 | tf_op jit(solution)/shard_map/ppermute | solution.py:174
  103.5 2.9 %collective-permute-start.38 = (bf16[16,2048]{1,0:T(8,128)(2,1)S(1)}, bf16[16,2048]{1,0:T(8,128)(2,1)S(1)}, u32[]{:S(2)}, u32[]{:S(2)}) collective-permute-start(bf16[16,2048]{1,0:T(8,128)(2,1)S(1)} %fusion.18), channel_id=1, source_target_pairs={{0,8},{4,12},{8,0},{12,4},{1,9},{5,13},{9,1},{13,5},{2,10},{6,14},... | collective-permute-start | bytes 196616 | tf_op jit(solution)/shard_map/ppermute | solution.py:174
  106.5 2.4 %shard_map.109 = (f32[64,2048]{1,0:T(8,128)S(1)}, bf16[64,2048]{1,0:T(8,128)(2,1)S(1)}) custom-call(bf16[32,2048]{1,0:T(8,128)(2,1)S(1)} %constant_dynamic-update-slice_fusion.8.refs_0_, bf16[32,2048]{1,0:T(8,128)(2,1)S(1)} %collective-permute-done.34.refs_1_, bf16[32,2048]{1,0:T(8,128)(2,1)S(1)} %constant_dynamic-update-slice_fusion.6.refs_2_, ...), custom_call_target="tpu_custom_call" | custom-call | flops 1024 | tf_op jit(solution)/shard_map/pallas_call | solution.py:185
  113.0 2.7 %collective-permute-done.39 = bf16[16,2048]{1,0:T(8,128)(2,1)S(1)} collective-permute-done((bf16[16,2048]{1,0:T(8,128)(2,1)S(1)}, bf16[16,2048]{1,0:T(8,128)(2,1)S(1)}, u32[]{:S(2)}, u32[]{:S(2)}) %collective-permute-start.39) | collective-permute-done | bytes 65568 | tf_op jit(solution)/shard_map/ppermute | solution.py:174
  120.3 2.4 %shard_map.110 = (f32[64,2048]{1,0:T(8,128)S(1)}, bf16[64,2048]{1,0:T(8,128)(2,1)S(1)}) custom-call(bf16[32,2048]{1,0:T(8,128)(2,1)S(1)} %constant_dynamic-update-slice_fusion.10.refs_0_, bf16[32,2048]{1,0:T(8,128)(2,1)S(1)} %collective-permute-done.40.refs_1_, bf16[32,2048]{1,0:T(8,128)(2,1)S(1)} %constant_dynamic-update-slice_fusion.6.refs_2_, ...), custom_call_target="tpu_custom_call" | custom-call | flops 1024 | tf_op jit(solution)/shard_map/pallas_call | solution.py:185
  128.2 3.5 %shard_map.111 = (bf16[2048,2048]{1,0:T(8,128)(2,1)S(1)}, f32[8,128]{1,0:T(8,128)S(1)}) custom-call(bf16[4,2048,2048]{2,1,0:T(8,128)(2,1)} %refs_0_.11, bf16[32,2048]{1,0:T(8,128)(2,1)S(1)} %constant_dynamic-update-slice_fusion.14.refs_1_.refs_3_.refs_7_.refs_0_, bf16[64,2048]{1,0:T(8,128)(2,1)S(1)} %get-tuple-element.195.refs_2_.refs_6_, ...), custom_call_target="tpu_custom_call" | custom-call | bytes 16 | tf_op jit(solution)/shard_map/pallas_call | solution.py:185
  132.8 2.7 %shard_map.112 = (f32[64,2048]{1,0:T(8,128)S(1)}, bf16[64,2048]{1,0:T(8,128)(2,1)S(1)}) custom-call(bf16[32,2048]{1,0:T(8,128)(2,1)S(1)} %constant_dynamic-update-slice_fusion.12.refs_0_, bf16[32,2048]{1,0:T(8,128)(2,1)S(1)} %collective-permute-done.44.refs_1_, bf16[32,2048]{1,0:T(8,128)(2,1)S(1)} %constant_dynamic-update-slice_fusion.6.refs_2_, ...), custom_call_target="tpu_custom_call" | custom-call | flops 1024 | tf_op jit(solution)/shard_map/pallas_call | solution.py:185
  142.8 6.2 %collective-permute-done.50 = bf16[64,2048]{1,0:T(8,128)(2,1)S(1)} collective-permute-done((bf16[64,2048]{1,0:T(8,128)(2,1)S(1)}, bf16[64,2048]{1,0:T(8,128)(2,1)S(1)}, u32[]{:S(2)}, u32[]{:S(2)}) %collective-permute-start.50) | collective-permute-done | bytes 262176 | tf_op jit(solution)/shard_map/ppermute | solution.py:174
  149.7 7.6 %shard_map.114 = (bf16[4,256,2048]{2,1,0:T(8,128)(2,1)}, f32[4,256,2048]{2,1,0:T(8,128)}, f32[4,256,2048]{2,1,0:T(8,128)}) custom-call(bf16[64,256]{1,0:T(8,128)(2,1)S(1)} %pad_maximum_fusion.2.hid, bf16[3,64,2048]{2,1,0:T(8,128)(2,1)S(1)} %pad_maximum_fusion.1.grad, bf16[4,256,2048]{2,1,0:T(8,128)(2,1)S(1)} %copy-done.1, f32[4,256,2048]{2,1,0:T(8,128)S(1)} %bitcast.24, ...), custom_call_target="tpu_custom_call" | custom-call | flops 201326592 | bytes 31457280 | tf_op jit(solution)/shard_map/pallas_call | solution.py:351
  157.5 3.2 %shard_map.115 = (bf16[4,256,2048]{2,1,0:T(8,128)(2,1)}, f32[4,256,2048]{2,1,0:T(8,128)}, f32[4,256,2048]{2,1,0:T(8,128)}) custom-call(bf16[64,256]{1,0:T(8,128)(2,1)S(1)} %pad_maximum_fusion.2.hid, bf16[1,64,2048]{2,1,0:T(8,128)(2,1)S(1)} %fusion.11.grad, ...), custom_call_target="tpu_custom_call", output_to_operand_aliasing={{0}: (5, {}), {1}: (6, {}), {2}: (7, {})} | custom-call | flops 67108864 | bytes 10485760 | tf_op jit(solution)/shard_map/pallas_call | solution.py:351
  (201 shorter events, 78.0 us)
Async XLA Ops:
  5.5 8.9 %collective-permute-start.4 = (bf16[64,2048]{1,0:T(8,128)(2,1)S(1)}, bf16[64,2048]{1,0:T(8,128)(2,1)S(1)}, u32[]{:S(2)}, u32[]{:S(2)}) collective-permute-start(bf16[64,2048]{1,0:T(8,128)(2,1)S(1)} %get-tuple-element.99), channel_id=1, source_target_pairs={{0,1},{1,0},{2,3},{3,2},{4,5},{5,4},{6,7},{7,6},{8,9},{9,8},{10,11... | collective-permute-start | bytes 786440 | tf_op jit(solution)/shard_map/ppermute | solution.py:174
  7.3 11.3 %collective-permute-start.1 = (bf16[64,2048]{1,0:T(8,128)(2,1)S(1)}, bf16[64,2048]{1,0:T(8,128)(2,1)S(1)}, u32[]{:S(2)}, u32[]{:S(2)}) collective-permute-start(bf16[64,2048]{1,0:T(8,128)(2,1)S(1)} %get-tuple-element.215.refs_1_), channel_id=1, source_target_pairs={{0,2},{1,3},{2,0},{3,1},{4,6},{5,7},{6,4},{7,5},{8,10},{9,11},{10,... | collective-permute-start | bytes 786440 | tf_op jit(solution)/shard_map/ppermute | solution.py:174
  11.2 15.1 %collective-permute-start.6 = (bf16[64,2048]{1,0:T(8,128)(2,1)S(1)}, bf16[64,2048]{1,0:T(8,128)(2,1)S(1)}, u32[]{:S(2)}, u32[]{:S(2)}) collective-permute-start(bf16[64,2048]{1,0:T(8,128)(2,1)S(1)} %get-tuple-element.213.refs_4_), channel_id=1, source_target_pairs={{0,2},{1,3},{2,0},{3,1},{4,6},{5,7},{6,4},{7,5},{8,10},{9,11},{10,... | collective-permute-start | bytes 786440 | tf_op jit(solution)/shard_map/ppermute | solution.py:174
  12.3 23.4 %collective-permute-start.9 = (bf16[64,2048]{1,0:T(8,128)(2,1)S(1)}, bf16[64,2048]{1,0:T(8,128)(2,1)S(1)}, u32[]{:S(2)}, u32[]{:S(2)}) collective-permute-start(bf16[64,2048]{1,0:T(8,128)(2,1)S(1)} %get-tuple-element.211.refs_3_), channel_id=1, source_target_pairs={{0,2},{1,3},{2,0},{3,1},{4,6},{5,7},{6,4},{7,5},{8,10},{9,11},{10,... | collective-permute-start | bytes 786440 | tf_op jit(solution)/shard_map/ppermute | solution.py:174
  14.5 21.3 %collective-permute-start.8 = (bf16[64,2048]{1,0:T(8,128)(2,1)S(1)}, bf16[64,2048]{1,0:T(8,128)(2,1)S(1)}, u32[]{:S(2)}, u32[]{:S(2)}) collective-permute-start(bf16[64,2048]{1,0:T(8,128)(2,1)S(1)} %get-tuple-element.209.refs_2_), channel_id=1, source_target_pairs={{0,2},{1,3},{2,0},{3,1},{4,6},{5,7},{6,4},{7,5},{8,10},{9,11},{10,... | collective-permute-start | bytes 786440 | tf_op jit(solution)/shard_map/ppermute | solution.py:174
  20.1 12.1 %collective-permute-start.5 = (bf16[64,2048]{1,0:T(8,128)(2,1)S(1)}, bf16[64,2048]{1,0:T(8,128)(2,1)S(1)}, u32[]{:S(2)}, u32[]{:S(2)}) collective-permute-start(bf16[64,2048]{1,0:T(8,128)(2,1)S(1)} %get-tuple-element.112.refs_1_), channel_id=1, source_target_pairs={{0,4},{4,0},{8,12},{12,8},{1,5},{5,1},{9,13},{13,9},{2,6},{6,2},{1... | collective-permute-start | bytes 786440 | tf_op jit(solution)/shard_map/ppermute | solution.py:174
  32.3 12.7 %collective-permute-start.11 = (bf16[32,2048]{1,0:T(8,128)(2,1)S(1)}, bf16[32,2048]{1,0:T(8,128)(2,1)S(1)}, u32[]{:S(2)}, u32[]{:S(2)}) collective-permute-start(bf16[32,2048]{1,0:T(8,128)(2,1)S(1)} %slice.161), channel_id=1, source_target_pairs={{0,8},{4,12},{8,0},{12,4},{1,9},{5,13},{9,1},{13,5},{2,10},{6,14},... | collective-permute-start | bytes 393224 | tf_op jit(solution)/shard_map/ppermute | solution.py:174
  35.4 9.6 %collective-permute-start.10 = (bf16[16,2048]{1,0:T(8,128)(2,1)S(1)}, bf16[16,2048]{1,0:T(8,128)(2,1)S(1)}, u32[]{:S(2)}, u32[]{:S(2)}) collective-permute-start(bf16[16,2048]{1,0:T(8,128)(2,1)S(1)} %slice.165), channel_id=1, source_target_pairs={{0,8},{4,12},{8,0},{12,4},{1,9},{5,13},{9,1},{13,5},{2,10},{6,14},... | collective-permute-start | bytes 196616 | tf_op jit(solution)/shard_map/ppermute | solution.py:174
  37.3 10.5 %collective-permute-start.12 = (bf16[64,2048]{1,0:T(8,128)(2,1)S(1)}, bf16[64,2048]{1,0:T(8,128)(2,1)S(1)}, u32[]{:S(2)}, u32[]{:S(2)}) collective-permute-start(bf16[64,2048]{1,0:T(8,128)(2,1)S(1)} %get-tuple-element.119.refs_1_), channel_id=1, source_target_pairs={{0,4},{4,0},{8,12},{12,8},{1,5},{5,1},{9,13},{13,9},{2,6},{6,2},{1... | collective-permute-start | bytes 786440 | tf_op jit(solution)/shard_map/ppermute | solution.py:174
  44.5 14.4 %collective-permute-start.15 = (bf16[64,2048]{1,0:T(8,128)(2,1)S(1)}, bf16[64,2048]{1,0:T(8,128)(2,1)S(1)}, u32[]{:S(2)}, u32[]{:S(2)}) collective-permute-start(bf16[64,2048]{1,0:T(8,128)(2,1)S(1)} %get-tuple-element.121), channel_id=1, source_target_pairs={{0,4},{4,0},{8,12},{12,8},{1,5},{5,1},{9,13},{13,9},{2,6},{6,2},{1... | collective-permute-start | bytes 786440 | tf_op jit(solution)/shard_map/ppermute | solution.py:174
  45.1 8.0 %collective-permute-start.13 = (bf16[16,2048]{1,0:T(8,128)(2,1)S(1)}, bf16[16,2048]{1,0:T(8,128)(2,1)S(1)}, u32[]{:S(2)}, u32[]{:S(2)}) collective-permute-start(bf16[16,2048]{1,0:T(8,128)(2,1)S(1)} %fusion.17), channel_id=1, source_target_pairs={{0,8},{4,12},{8,0},{12,4},{1,9},{5,13},{9,1},{13,5},{2,10},{6,14},... | collective-permute-start | bytes 196616 | tf_op jit(solution)/shard_map/ppermute | solution.py:174
  47.9 8.6 %collective-permute-start.14 = (bf16[32,2048]{1,0:T(8,128)(2,1)S(1)}, bf16[32,2048]{1,0:T(8,128)(2,1)S(1)}, u32[]{:S(2)}, u32[]{:S(2)}) collective-permute-start(bf16[32,2048]{1,0:T(8,128)(2,1)S(1)} %slice.160), channel_id=1, source_target_pairs={{0,8},{4,12},{8,0},{12,4},{1,9},{5,13},{9,1},{13,5},{2,10},{6,14},... | collective-permute-start | bytes 393224 | tf_op jit(solution)/shard_map/ppermute | solution.py:174
  53.1 7.9 %collective-permute-start.16 = (bf16[32,2048]{1,0:T(8,128)(2,1)S(1)}, bf16[32,2048]{1,0:T(8,128)(2,1)S(1)}, u32[]{:S(2)}, u32[]{:S(2)}) collective-permute-start(bf16[32,2048]{1,0:T(8,128)(2,1)S(1)} %constant_dynamic-update-slice_fusion.refs_0_), channel_id=1, source_target_pairs={{0,4},{4,0},{8,12},{12,8},{1,5},{5,1},{9,13},{13,9},{2,6},{6,2},{1... | collective-permute-start | bytes 393224 | tf_op jit(solution)/shard_map/ppermute | solution.py:174
  69.6 8.1 %collective-permute-start.23 = (bf16[64,2048]{1,0:T(8,128)(2,1)S(1)}, bf16[64,2048]{1,0:T(8,128)(2,1)S(1)}, u32[]{:S(2)}, u32[]{:S(2)}) collective-permute-start(bf16[64,2048]{1,0:T(8,128)(2,1)S(1)} %get-tuple-element.205.refs_3_), channel_id=1, source_target_pairs={{0,2},{1,3},{2,0},{3,1},{4,6},{5,7},{6,4},{7,5},{8,10},{9,11},{10,... | collective-permute-start | bytes 786440 | tf_op jit(solution)/shard_map/ppermute | solution.py:174
  73.8 9.5 %collective-permute-start.24 = (bf16[32,2048]{1,0:T(8,128)(2,1)S(1)}, bf16[32,2048]{1,0:T(8,128)(2,1)S(1)}, u32[]{:S(2)}, u32[]{:S(2)}) collective-permute-start(bf16[32,2048]{1,0:T(8,128)(2,1)S(1)} %constant_dynamic-update-slice_fusion.4.refs_0_), channel_id=1, source_target_pairs={{0,4},{4,0},{8,12},{12,8},{1,5},{5,1},{9,13},{13,9},{2,6},{6,2},{1... | collective-permute-start | bytes 393224 | tf_op jit(solution)/shard_map/ppermute | solution.py:174
  81.6 7.8 %collective-permute-start.28 = (bf16[64,2048]{1,0:T(8,128)(2,1)S(1)}, bf16[64,2048]{1,0:T(8,128)(2,1)S(1)}, u32[]{:S(2)}, u32[]{:S(2)}) collective-permute-start(bf16[64,2048]{1,0:T(8,128)(2,1)S(1)} %get-tuple-element.203), channel_id=1, source_target_pairs={{0,2},{1,3},{2,0},{3,1},{4,6},{5,7},{6,4},{7,5},{8,10},{9,11},{10,... | collective-permute-start | bytes 786440 | tf_op jit(solution)/shard_map/ppermute | solution.py:174
  85.8 20.6 %collective-permute-start.35 = (bf16[32,2048]{1,0:T(8,128)(2,1)S(1)}, bf16[32,2048]{1,0:T(8,128)(2,1)S(1)}, u32[]{:S(2)}, u32[]{:S(2)}) collective-permute-start(bf16[32,2048]{1,0:T(8,128)(2,1)S(1)} %constant_dynamic-update-slice_fusion.6.refs_2_), channel_id=1, source_target_pairs={{0,4},{4,0},{8,12},{12,8},{1,5},{5,1},{9,13},{13,9},{2,6},{6,2},{1... | collective-permute-start | bytes 393224 | tf_op jit(solution)/shard_map/ppermute | solution.py:174
  89.5 8.0 %collective-permute-start.30 = (bf16[64,2048]{1,0:T(8,128)(2,1)S(1)}, bf16[64,2048]{1,0:T(8,128)(2,1)S(1)}, u32[]{:S(2)}, u32[]{:S(2)}) collective-permute-start(bf16[64,2048]{1,0:T(8,128)(2,1)S(1)} %get-tuple-element.201.refs_2_), channel_id=1, source_target_pairs={{0,2},{1,3},{2,0},{3,1},{4,6},{5,7},{6,4},{7,5},{8,10},{9,11},{10,... | collective-permute-start | bytes 786440 | tf_op jit(solution)/shard_map/ppermute | solution.py:174
  103.5 8.0 %collective-permute-start.38 = (bf16[16,2048]{1,0:T(8,128)(2,1)S(1)}, bf16[16,2048]{1,0:T(8,128)(2,1)S(1)}, u32[]{:S(2)}, u32[]{:S(2)}) collective-permute-start(bf16[16,2048]{1,0:T(8,128)(2,1)S(1)} %fusion.18), channel_id=1, source_target_pairs={{0,8},{4,12},{8,0},{12,4},{1,9},{5,13},{9,1},{13,5},{2,10},{6,14},... | collective-permute-start | bytes 196616 | tf_op jit(solution)/shard_map/ppermute | solution.py:174
  111.5 8.9 %collective-permute-start.40 = (bf16[32,2048]{1,0:T(8,128)(2,1)S(1)}, bf16[32,2048]{1,0:T(8,128)(2,1)S(1)}, u32[]{:S(2)}, u32[]{:S(2)}) collective-permute-start(bf16[32,2048]{1,0:T(8,128)(2,1)S(1)} %constant_dynamic-update-slice_fusion.10.refs_0_), channel_id=1, source_target_pairs={{0,4},{4,0},{8,12},{12,8},{1,5},{5,1},{9,13},{13,9},{2,6},{6,2},{1... | collective-permute-start | bytes 393224 | tf_op jit(solution)/shard_map/ppermute | solution.py:174
  115.8 10.3 %collective-permute-start.43 = (bf16[16,2048]{1,0:T(8,128)(2,1)S(1)}, bf16[16,2048]{1,0:T(8,128)(2,1)S(1)}, u32[]{:S(2)}, u32[]{:S(2)}) collective-permute-start(bf16[16,2048]{1,0:T(8,128)(2,1)S(1)} %negate_convert_fusion), channel_id=1, source_target_pairs={{0,8},{4,12},{8,0},{12,4},{1,9},{5,13},{9,1},{13,5},{2,10},{6,14},... | collective-permute-start | bytes 196616 | tf_op jit(solution)/shard_map/ppermute | solution.py:174
  118.7 12.9 %collective-permute-start.46 = (bf16[64,2048]{1,0:T(8,128)(2,1)S(1)}, bf16[64,2048]{1,0:T(8,128)(2,1)S(1)}, u32[]{:S(2)}, u32[]{:S(2)}) collective-permute-start(bf16[64,2048]{1,0:T(8,128)(2,1)S(1)} %get-tuple-element.197.refs_6_), channel_id=1, source_target_pairs={{0,2},{1,3},{2,0},{3,1},{4,6},{5,7},{6,4},{7,5},{8,10},{9,11},{10,... | collective-permute-start | bytes 786440 | tf_op jit(solution)/shard_map/ppermute | solution.py:174
  139.8 9.1 %collective-permute-start.50 = (bf16[64,2048]{1,0:T(8,128)(2,1)S(1)}, bf16[64,2048]{1,0:T(8,128)(2,1)S(1)}, u32[]{:S(2)}, u32[]{:S(2)}) collective-permute-start(bf16[64,2048]{1,0:T(8,128)(2,1)S(1)} %get-tuple-element.193), channel_id=1, source_target_pairs={{0,2},{1,3},{2,0},{3,1},{4,6},{5,7},{6,4},{7,5},{8,10},{9,11},{10,... | collective-permute-start | bytes 786440 | tf_op jit(solution)/shard_map/ppermute | solution.py:174
  141.3 16.1 %collective-permute-start.51 = (bf16[64,2048]{1,0:T(8,128)(2,1)S(1)}, bf16[64,2048]{1,0:T(8,128)(2,1)S(1)}, u32[]{:S(2)}, u32[]{:S(2)}) collective-permute-start(bf16[64,2048]{1,0:T(8,128)(2,1)S(1)} %get-tuple-element.191), channel_id=1, source_target_pairs={{0,2},{1,3},{2,0},{3,1},{4,6},{5,7},{6,4},{7,5},{8,10},{9,11},{10,... | collective-permute-start | bytes 786440 | tf_op jit(solution)/shard_map/ppermute | solution.py:174
  (40 other events, 285.2 us)

commit v5 on v4

--- a/solution.py
+++ b/solution.py
@@ -343,8 +343,8 @@
         new_two[...] = spread
         scaled = spread * (1.0 / second_fix)
         root = scaled * lax.rsqrt(scaled)
-        update = moved * (1.0 / first_fix) / (root + 1e-08)
-        new_wgt[...] = (wgt[...].astype(f32) - 0.001 * update).astype(bf16)
+        update = moved * (0.001 / first_fix) / (root + 1e-08)
+        new_wgt[...] = (wgt[...].astype(f32) - update).astype(bf16)
 
     block = pl.BlockSpec((None, tile, cols), lambda s, i: (first_kind + s, i, 0))
     made = () if made is None else made

time: 161 us -> 161 us (level)
  no operation moved by 1% of the time
where the time goes in v5:
time: 161 us
  starting transfers between devices  68.4 us (42%)
  Pallas kernels  58.8 us (37%)
  waiting for transfers between devices  22.6 us (14%)
  other arithmetic  6.12 us (4%)
  local copies, waits for them, and re-layouts  3.34 us (2%)
    ppermute x52, starting transfers between devices, swap(): return lax.ppermute(value, axis, [(i, i ^ mask) for i in range(count)])  68.4 us
    pallas_call x19, Pallas kernels, call(): pl.pallas_call(body, out_shape=out_shape, in_specs=[hbm if i in in_hbm el...  47.1 us
    ppermute x52, waiting for transfers between devices, swap(): return lax.ppermute(value, axis, [(i, i ^ mask) for i in range(count)])  22.6 us
    pallas_call x2, Pallas kernels, adam(): pl.pallas_call(kernel, grid=(kinds, depth // tile), out_shape=(jax.ShapeD...  10.8 us
    convert_element_type x11, other arithmetic, join(): kept, sent = (total, total.astype(bf16))  3.55 us
  transfers between devices with their start and end apart: 52, of which 14 were waited for; matrix products, arithmetic and copies ran while one was open for 4% of the time, Pallas kernels for 31%

profile of v5, /device:TPU:0, one launch (start us, length us, event | category | flops | bytes accessed | tf_op | source)
XLA Modules:
  0.0 160.7 jit_solution(8227348901653356903)
XLA Ops:
  7.3 2.9 %collective-permute-start.1 = (bf16[64,2048]{1,0:T(8,128)(2,1)S(1)}, bf16[64,2048]{1,0:T(8,128)(2,1)S(1)}, u32[]{:S(2)}, u32[]{:S(2)}) collective-permute-start(bf16[64,2048]{1,0:T(8,128)(2,1)S(1)} %get-tuple-element.215.refs_1_), channel_id=1, source_target_pairs={{0,2},{1,3},{2,0},{3,1},{4,6},{5,7},{6,4},{7,5},{8,10},{9,11},{10,... | collective-permute-start | bytes 786440 | tf_op jit(solution)/shard_map/ppermute | solution.py:174
  14.6 4.1 %shard_map.95 = (bf16[2048,2048]{1,0:T(8,128)(2,1)S(1)}, f32[8,128]{1,0:T(8,128)}) custom-call(bf16[4,2048,2048]{2,1,0:T(8,128)(2,1)} %refs_0_.11, bf16[64,2048]{1,0:T(8,128)(2,1)S(1)} %get-tuple-element.215.refs_1_, bf16[64,2048]{1,0:T(8,128)(2,1)S(1)} %get-tuple-element.209.refs_2_, bf16[64,2048]{1,0:T(8,128)(2,1)S(1)} %get-tuple-element.211.refs_3_, ...), custom_call_target="tpu_custom_call" | custom-call | bytes 16 | tf_op jit(solution)/shard_map/pallas_call | solution.py:185
  22.2 4.1 %shard_map.97 = (bf16[2048,2048]{1,0:T(8,128)(2,1)S(1)}, f32[8,128]{1,0:T(8,128)}) custom-call(bf16[4,2048,2048]{2,1,0:T(8,128)(2,1)} %refs_0_.11, bf16[64,2048]{1,0:T(8,128)(2,1)S(1)} %get-tuple-element.112.refs_1_), custom_call_target="tpu_custom_call" | custom-call | bytes 16 | tf_op jit(solution)/shard_map/pallas_call | solution.py:185
  28.1 4.1 %shard_map.99 = (bf16[2048,2048]{1,0:T(8,128)(2,1)S(1)}, f32[8,128]{1,0:T(8,128)}) custom-call(bf16[4,2048,2048]{2,1,0:T(8,128)(2,1)} %refs_0_.11, bf16[32,2048]{1,0:T(8,128)(2,1)S(1)} %get-tuple-element.116.refs_1_), custom_call_target="tpu_custom_call" | custom-call | bytes 16 | tf_op jit(solution)/shard_map/pallas_call | solution.py:185
  32.3 3.1 %collective-permute-start.11 = (bf16[32,2048]{1,0:T(8,128)(2,1)S(1)}, bf16[32,2048]{1,0:T(8,128)(2,1)S(1)}, u32[]{:S(2)}, u32[]{:S(2)}) collective-permute-start(bf16[32,2048]{1,0:T(8,128)(2,1)S(1)} %slice.161), channel_id=1, source_target_pairs={{0,8},{4,12},{8,0},{12,4},{1,9},{5,13},{9,1},{13,5},{2,10},{6,14},... | collective-permute-start | bytes 393224 | tf_op jit(solution)/shard_map/ppermute | solution.py:174
  39.0 4.1 %shard_map.101 = (bf16[2048,2048]{1,0:T(8,128)(2,1)S(1)}, f32[8,128]{1,0:T(8,128)}) custom-call(bf16[4,2048,2048]{2,1,0:T(8,128)(2,1)} %refs_0_.11, bf16[64,2048]{1,0:T(8,128)(2,1)S(1)} %get-tuple-element.119.refs_1_), custom_call_target="tpu_custom_call" | custom-call | bytes 16 | tf_op jit(solution)/shard_map/pallas_call | solution.py:185
  45.1 2.7 %collective-permute-start.13 = (bf16[16,2048]{1,0:T(8,128)(2,1)S(1)}, bf16[16,2048]{1,0:T(8,128)(2,1)S(1)}, u32[]{:S(2)}, u32[]{:S(2)}) collective-permute-start(bf16[16,2048]{1,0:T(8,128)(2,1)S(1)} %fusion.17), channel_id=1, source_target_pairs={{0,8},{4,12},{8,0},{12,4},{1,9},{5,13},{9,1},{13,5},{2,10},{6,14},... | collective-permute-start | bytes 196616 | tf_op jit(solution)/shard_map/ppermute | solution.py:174
  47.9 3.4 %collective-permute-start.14 = (bf16[32,2048]{1,0:T(8,128)(2,1)S(1)}, bf16[32,2048]{1,0:T(8,128)(2,1)S(1)}, u32[]{:S(2)}, u32[]{:S(2)}) collective-permute-start(bf16[32,2048]{1,0:T(8,128)(2,1)S(1)} %slice.160), channel_id=1, source_target_pairs={{0,8},{4,12},{8,0},{12,4},{1,9},{5,13},{9,1},{13,5},{2,10},{6,14},... | collective-permute-start | bytes 393224 | tf_op jit(solution)/shard_map/ppermute | solution.py:174
  53.1 3.4 %collective-permute-start.16 = (bf16[32,2048]{1,0:T(8,128)(2,1)S(1)}, bf16[32,2048]{1,0:T(8,128)(2,1)S(1)}, u32[]{:S(2)}, u32[]{:S(2)}) collective-permute-start(bf16[32,2048]{1,0:T(8,128)(2,1)S(1)} %constant_dynamic-update-slice_fusion.refs_0_), channel_id=1, source_target_pairs={{0,4},{4,0},{8,12},{12,8},{1,5},{5,1},{9,13},{13,9},{2,6},{6,2},{1... | collective-permute-start | bytes 393224 | tf_op jit(solution)/shard_map/ppermute | solution.py:174
  61.1 2.4 %shard_map.103 = (f32[64,2048]{1,0:T(8,128)S(1)}, bf16[64,2048]{1,0:T(8,128)(2,1)S(1)}) custom-call(bf16[32,2048]{1,0:T(8,128)(2,1)S(1)} %constant_dynamic-update-slice_fusion.refs_0_, bf16[32,2048]{1,0:T(8,128)(2,1)S(1)} %collective-permute-done.16.refs_1_, bf16[2048,2048]{1,0:T(8,128)(2,1)S(1)} %get-tuple-element.110.refs_2_.refs_1_.refs_5_), custom_call_target="tpu_custom_call" | custom-call | flops 512 | tf_op jit(solution)/shard_map/pallas_call | solution.py:185
  63.6 3.0 %collective-permute-start.20 = (bf16[32,2048]{1,0:T(8,128)(2,1)S(1)}, bf16[32,2048]{1,0:T(8,128)(2,1)S(1)}, u32[]{:S(2)}, u32[]{:S(2)}) collective-permute-start(bf16[32,2048]{1,0:T(8,128)(2,1)S(1)} %constant_dynamic-update-slice_fusion.2.refs_0_), channel_id=1, source_target_pairs={{0,4},{4,0},{8,12},{12,8},{1,5},{5,1},{9,13},{13,9},{2,6},{6,2},{1... | collective-permute-start | bytes 393224 | tf_op jit(solution)/shard_map/ppermute | solution.py:174
  66.7 2.9 %collective-permute-start.21 = (bf16[16,2048]{1,0:T(8,128)(2,1)S(1)}, bf16[16,2048]{1,0:T(8,128)(2,1)S(1)}, u32[]{:S(2)}, u32[]{:S(2)}) collective-permute-start(bf16[16,2048]{1,0:T(8,128)(2,1)S(1)} %fusion.13), channel_id=1, source_target_pairs={{0,8},{4,12},{8,0},{12,4},{1,9},{5,13},{9,1},{13,5},{2,10},{6,14},... | collective-permute-start | bytes 196616 | tf_op jit(solution)/shard_map/ppermute | solution.py:174
  75.4 2.4 %collective-permute-done.23 = bf16[64,2048]{1,0:T(8,128)(2,1)S(1)} collective-permute-done((bf16[64,2048]{1,0:T(8,128)(2,1)S(1)}, bf16[64,2048]{1,0:T(8,128)(2,1)S(1)}, u32[]{:S(2)}, u32[]{:S(2)}) %collective-permute-start.23) | collective-permute-done | bytes 262176 | tf_op jit(solution)/shard_map/ppermute | solution.py:174
  86.5 2.6 %collective-permute-start.29 = (bf16[16,2048]{1,0:T(8,128)(2,1)S(1)}, bf16[16,2048]{1,0:T(8,128)(2,1)S(1)}, u32[]{:S(2)}, u32[]{:S(2)}) collective-permute-start(bf16[16,2048]{1,0:T(8,128)(2,1)S(1)} %slice.164), channel_id=1, source_target_pairs={{0,8},{4,12},{8,0},{12,4},{1,9},{5,13},{9,1},{13,5},{2,10},{6,14},... | collective-permute-start | bytes 196616 | tf_op jit(solution)/shard_map/ppermute | solution.py:174
  95.0 2.5 %collective-permute-done.30 = bf16[64,2048]{1,0:T(8,128)(2,1)S(1)} collective-permute-done((bf16[64,2048]{1,0:T(8,128)(2,1)S(1)}, bf16[64,2048]{1,0:T(8,128)(2,1)S(1)}, u32[]{:S(2)}, u32[]{:S(2)}) %collective-permute-start.30) | collective-permute-done | bytes 262176 | tf_op jit(solution)/shard_map/ppermute | solution.py:174
  103.5 2.9 %collective-permute-start.38 = (bf16[16,2048]{1,0:T(8,128)(2,1)S(1)}, bf16[16,2048]{1,0:T(8,128)(2,1)S(1)}, u32[]{:S(2)}, u32[]{:S(2)}) collective-permute-start(bf16[16,2048]{1,0:T(8,128)(2,1)S(1)} %fusion.18), channel_id=1, source_target_pairs={{0,8},{4,12},{8,0},{12,4},{1,9},{5,13},{9,1},{13,5},{2,10},{6,14},... | collective-permute-start | bytes 196616 | tf_op jit(solution)/shard_map/ppermute | solution.py:174
  106.5 2.4 %shard_map.109 = (f32[64,2048]{1,0:T(8,128)S(1)}, bf16[64,2048]{1,0:T(8,128)(2,1)S(1)}) custom-call(bf16[32,2048]{1,0:T(8,128)(2,1)S(1)} %constant_dynamic-update-slice_fusion.8.refs_0_, bf16[32,2048]{1,0:T(8,128)(2,1)S(1)} %collective-permute-done.34.refs_1_, bf16[32,2048]{1,0:T(8,128)(2,1)S(1)} %constant_dynamic-update-slice_fusion.6.refs_2_, ...), custom_call_target="tpu_custom_call" | custom-call | flops 1024 | tf_op jit(solution)/shard_map/pallas_call | solution.py:185
  113.0 2.7 %collective-permute-done.39 = bf16[16,2048]{1,0:T(8,128)(2,1)S(1)} collective-permute-done((bf16[16,2048]{1,0:T(8,128)(2,1)S(1)}, bf16[16,2048]{1,0:T(8,128)(2,1)S(1)}, u32[]{:S(2)}, u32[]{:S(2)}) %collective-permute-start.39) | collective-permute-done | bytes 65568 | tf_op jit(solution)/shard_map/ppermute | solution.py:174
  120.3 2.4 %shard_map.110 = (f32[64,2048]{1,0:T(8,128)S(1)}, bf16[64,2048]{1,0:T(8,128)(2,1)S(1)}) custom-call(bf16[32,2048]{1,0:T(8,128)(2,1)S(1)} %constant_dynamic-update-slice_fusion.10.refs_0_, bf16[32,2048]{1,0:T(8,128)(2,1)S(1)} %collective-permute-done.40.refs_1_, bf16[32,2048]{1,0:T(8,128)(2,1)S(1)} %constant_dynamic-update-slice_fusion.6.refs_2_, ...), custom_call_target="tpu_custom_call" | custom-call | flops 1024 | tf_op jit(solution)/shard_map/pallas_call | solution.py:185
  128.2 3.5 %shard_map.111 = (bf16[2048,2048]{1,0:T(8,128)(2,1)S(1)}, f32[8,128]{1,0:T(8,128)S(1)}) custom-call(bf16[4,2048,2048]{2,1,0:T(8,128)(2,1)} %refs_0_.11, bf16[32,2048]{1,0:T(8,128)(2,1)S(1)} %constant_dynamic-update-slice_fusion.14.refs_1_.refs_3_.refs_7_.refs_0_, bf16[64,2048]{1,0:T(8,128)(2,1)S(1)} %get-tuple-element.195.refs_2_.refs_6_, ...), custom_call_target="tpu_custom_call" | custom-call | bytes 16 | tf_op jit(solution)/shard_map/pallas_call | solution.py:185
  132.8 2.7 %shard_map.112 = (f32[64,2048]{1,0:T(8,128)S(1)}, bf16[64,2048]{1,0:T(8,128)(2,1)S(1)}) custom-call(bf16[32,2048]{1,0:T(8,128)(2,1)S(1)} %constant_dynamic-update-slice_fusion.12.refs_0_, bf16[32,2048]{1,0:T(8,128)(2,1)S(1)} %collective-permute-done.44.refs_1_, bf16[32,2048]{1,0:T(8,128)(2,1)S(1)} %constant_dynamic-update-slice_fusion.6.refs_2_, ...), custom_call_target="tpu_custom_call" | custom-call | flops 1024 | tf_op jit(solution)/shard_map/pallas_call | solution.py:185
  142.8 6.2 %collective-permute-done.50 = bf16[64,2048]{1,0:T(8,128)(2,1)S(1)} collective-permute-done((bf16[64,2048]{1,0:T(8,128)(2,1)S(1)}, bf16[64,2048]{1,0:T(8,128)(2,1)S(1)}, u32[]{:S(2)}, u32[]{:S(2)}) %collective-permute-start.50) | collective-permute-done | bytes 262176 | tf_op jit(solution)/shard_map/ppermute | solution.py:174
  149.7 7.6 %shard_map.114 = (bf16[4,256,2048]{2,1,0:T(8,128)(2,1)}, f32[4,256,2048]{2,1,0:T(8,128)}, f32[4,256,2048]{2,1,0:T(8,128)}) custom-call(bf16[64,256]{1,0:T(8,128)(2,1)S(1)} %pad_maximum_fusion.2.hid, bf16[3,64,2048]{2,1,0:T(8,128)(2,1)S(1)} %pad_maximum_fusion.1.grad, bf16[4,256,2048]{2,1,0:T(8,128)(2,1)S(1)} %copy-done.1, f32[4,256,2048]{2,1,0:T(8,128)S(1)} %bitcast.24, ...), custom_call_target="tpu_custom_call" | custom-call | flops 201326592 | bytes 31457280 | tf_op jit(solution)/shard_map/pallas_call | solution.py:351
  157.5 3.2 %shard_map.115 = (bf16[4,256,2048]{2,1,0:T(8,128)(2,1)}, f32[4,256,2048]{2,1,0:T(8,128)}, f32[4,256,2048]{2,1,0:T(8,128)}) custom-call(bf16[64,256]{1,0:T(8,128)(2,1)S(1)} %pad_maximum_fusion.2.hid, bf16[1,64,2048]{2,1,0:T(8,128)(2,1)S(1)} %fusion.11.grad, ...), custom_call_target="tpu_custom_call", output_to_operand_aliasing={{0}: (5, {}), {1}: (6, {}), {2}: (7, {})} | custom-call | flops 67108864 | bytes 10485760 | tf_op jit(solution)/shard_map/pallas_call | solution.py:351
  (201 shorter events, 78.0 us)
Async XLA Ops:
  5.5 8.9 %collective-permute-start.4 = (bf16[64,2048]{1,0:T(8,128)(2,1)S(1)}, bf16[64,2048]{1,0:T(8,128)(2,1)S(1)}, u32[]{:S(2)}, u32[]{:S(2)}) collective-permute-start(bf16[64,2048]{1,0:T(8,128)(2,1)S(1)} %get-tuple-element.99), channel_id=1, source_target_pairs={{0,1},{1,0},{2,3},{3,2},{4,5},{5,4},{6,7},{7,6},{8,9},{9,8},{10,11... | collective-permute-start | bytes 786440 | tf_op jit(solution)/shard_map/ppermute | solution.py:174
  7.3 11.3 %collective-permute-start.1 = (bf16[64,2048]{1,0:T(8,128)(2,1)S(1)}, bf16[64,2048]{1,0:T(8,128)(2,1)S(1)}, u32[]{:S(2)}, u32[]{:S(2)}) collective-permute-start(bf16[64,2048]{1,0:T(8,128)(2,1)S(1)} %get-tuple-element.215.refs_1_), channel_id=1, source_target_pairs={{0,2},{1,3},{2,0},{3,1},{4,6},{5,7},{6,4},{7,5},{8,10},{9,11},{10,... | collective-permute-start | bytes 786440 | tf_op jit(solution)/shard_map/ppermute | solution.py:174
  11.2 15.1 %collective-permute-start.6 = (bf16[64,2048]{1,0:T(8,128)(2,1)S(1)}, bf16[64,2048]{1,0:T(8,128)(2,1)S(1)}, u32[]{:S(2)}, u32[]{:S(2)}) collective-permute-start(bf16[64,2048]{1,0:T(8,128)(2,1)S(1)} %get-tuple-element.213.refs_4_), channel_id=1, source_target_pairs={{0,2},{1,3},{2,0},{3,1},{4,6},{5,7},{6,4},{7,5},{8,10},{9,11},{10,... | collective-permute-start | bytes 786440 | tf_op jit(solution)/shard_map/ppermute | solution.py:174
  12.3 23.4 %collective-permute-start.9 = (bf16[64,2048]{1,0:T(8,128)(2,1)S(1)}, bf16[64,2048]{1,0:T(8,128)(2,1)S(1)}, u32[]{:S(2)}, u32[]{:S(2)}) collective-permute-start(bf16[64,2048]{1,0:T(8,128)(2,1)S(1)} %get-tuple-element.211.refs_3_), channel_id=1, source_target_pairs={{0,2},{1,3},{2,0},{3,1},{4,6},{5,7},{6,4},{7,5},{8,10},{9,11},{10,... | collective-permute-start | bytes 786440 | tf_op jit(solution)/shard_map/ppermute | solution.py:174
  14.5 21.3 %collective-permute-start.8 = (bf16[64,2048]{1,0:T(8,128)(2,1)S(1)}, bf16[64,2048]{1,0:T(8,128)(2,1)S(1)}, u32[]{:S(2)}, u32[]{:S(2)}) collective-permute-start(bf16[64,2048]{1,0:T(8,128)(2,1)S(1)} %get-tuple-element.209.refs_2_), channel_id=1, source_target_pairs={{0,2},{1,3},{2,0},{3,1},{4,6},{5,7},{6,4},{7,5},{8,10},{9,11},{10,... | collective-permute-start | bytes 786440 | tf_op jit(solution)/shard_map/ppermute | solution.py:174
  20.1 12.1 %collective-permute-start.5 = (bf16[64,2048]{1,0:T(8,128)(2,1)S(1)}, bf16[64,2048]{1,0:T(8,128)(2,1)S(1)}, u32[]{:S(2)}, u32[]{:S(2)}) collective-permute-start(bf16[64,2048]{1,0:T(8,128)(2,1)S(1)} %get-tuple-element.112.refs_1_), channel_id=1, source_target_pairs={{0,4},{4,0},{8,12},{12,8},{1,5},{5,1},{9,13},{13,9},{2,6},{6,2},{1... | collective-permute-start | bytes 786440 | tf_op jit(solution)/shard_map/ppermute | solution.py:174
  32.3 12.7 %collective-permute-start.11 = (bf16[32,2048]{1,0:T(8,128)(2,1)S(1)}, bf16[32,2048]{1,0:T(8,128)(2,1)S(1)}, u32[]{:S(2)}, u32[]{:S(2)}) collective-permute-start(bf16[32,2048]{1,0:T(8,128)(2,1)S(1)} %slice.161), channel_id=1, source_target_pairs={{0,8},{4,12},{8,0},{12,4},{1,9},{5,13},{9,1},{13,5},{2,10},{6,14},... | collective-permute-start | bytes 393224 | tf_op jit(solution)/shard_map/ppermute | solution.py:174
  35.4 9.6 %collective-permute-start.10 = (bf16[16,2048]{1,0:T(8,128)(2,1)S(1)}, bf16[16,2048]{1,0:T(8,128)(2,1)S(1)}, u32[]{:S(2)}, u32[]{:S(2)}) collective-permute-start(bf16[16,2048]{1,0:T(8,128)(2,1)S(1)} %slice.165), channel_id=1, source_target_pairs={{0,8},{4,12},{8,0},{12,4},{1,9},{5,13},{9,1},{13,5},{2,10},{6,14},... | collective-permute-start | bytes 196616 | tf_op jit(solution)/shard_map/ppermute | solution.py:174
  37.3 10.5 %collective-permute-start.12 = (bf16[64,2048]{1,0:T(8,128)(2,1)S(1)}, bf16[64,2048]{1,0:T(8,128)(2,1)S(1)}, u32[]{:S(2)}, u32[]{:S(2)}) collective-permute-start(bf16[64,2048]{1,0:T(8,128)(2,1)S(1)} %get-tuple-element.119.refs_1_), channel_id=1, source_target_pairs={{0,4},{4,0},{8,12},{12,8},{1,5},{5,1},{9,13},{13,9},{2,6},{6,2},{1... | collective-permute-start | bytes 786440 | tf_op jit(solution)/shard_map/ppermute | solution.py:174
  44.5 14.4 %collective-permute-start.15 = (bf16[64,2048]{1,0:T(8,128)(2,1)S(1)}, bf16[64,2048]{1,0:T(8,128)(2,1)S(1)}, u32[]{:S(2)}, u32[]{:S(2)}) collective-permute-start(bf16[64,2048]{1,0:T(8,128)(2,1)S(1)} %get-tuple-element.121), channel_id=1, source_target_pairs={{0,4},{4,0},{8,12},{12,8},{1,5},{5,1},{9,13},{13,9},{2,6},{6,2},{1... | collective-permute-start | bytes 786440 | tf_op jit(solution)/shard_map/ppermute | solution.py:174
  45.1 8.0 %collective-permute-start.13 = (bf16[16,2048]{1,0:T(8,128)(2,1)S(1)}, bf16[16,2048]{1,0:T(8,128)(2,1)S(1)}, u32[]{:S(2)}, u32[]{:S(2)}) collective-permute-start(bf16[16,2048]{1,0:T(8,128)(2,1)S(1)} %fusion.17), channel_id=1, source_target_pairs={{0,8},{4,12},{8,0},{12,4},{1,9},{5,13},{9,1},{13,5},{2,10},{6,14},... | collective-permute-start | bytes 196616 | tf_op jit(solution)/shard_map/ppermute | solution.py:174
  47.9 8.6 %collective-permute-start.14 = (bf16[32,2048]{1,0:T(8,128)(2,1)S(1)}, bf16[32,2048]{1,0:T(8,128)(2,1)S(1)}, u32[]{:S(2)}, u32[]{:S(2)}) collective-permute-start(bf16[32,2048]{1,0:T(8,128)(2,1)S(1)} %slice.160), channel_id=1, source_target_pairs={{0,8},{4,12},{8,0},{12,4},{1,9},{5,13},{9,1},{13,5},{2,10},{6,14},... | collective-permute-start | bytes 393224 | tf_op jit(solution)/shard_map/ppermute | solution.py:174
  53.1 7.9 %collective-permute-start.16 = (bf16[32,2048]{1,0:T(8,128)(2,1)S(1)}, bf16[32,2048]{1,0:T(8,128)(2,1)S(1)}, u32[]{:S(2)}, u32[]{:S(2)}) collective-permute-start(bf16[32,2048]{1,0:T(8,128)(2,1)S(1)} %constant_dynamic-update-slice_fusion.refs_0_), channel_id=1, source_target_pairs={{0,4},{4,0},{8,12},{12,8},{1,5},{5,1},{9,13},{13,9},{2,6},{6,2},{1... | collective-permute-start | bytes 393224 | tf_op jit(solution)/shard_map/ppermute | solution.py:174
  69.6 8.1 %collective-permute-start.23 = (bf16[64,2048]{1,0:T(8,128)(2,1)S(1)}, bf16[64,2048]{1,0:T(8,128)(2,1)S(1)}, u32[]{:S(2)}, u32[]{:S(2)}) collective-permute-start(bf16[64,2048]{1,0:T(8,128)(2,1)S(1)} %get-tuple-element.205.refs_3_), channel_id=1, source_target_pairs={{0,2},{1,3},{2,0},{3,1},{4,6},{5,7},{6,4},{7,5},{8,10},{9,11},{10,... | collective-permute-start | bytes 786440 | tf_op jit(solution)/shard_map/ppermute | solution.py:174
  73.8 9.5 %collective-permute-start.24 = (bf16[32,2048]{1,0:T(8,128)(2,1)S(1)}, bf16[32,2048]{1,0:T(8,128)(2,1)S(1)}, u32[]{:S(2)}, u32[]{:S(2)}) collective-permute-start(bf16[32,2048]{1,0:T(8,128)(2,1)S(1)} %constant_dynamic-update-slice_fusion.4.refs_0_), channel_id=1, source_target_pairs={{0,4},{4,0},{8,12},{12,8},{1,5},{5,1},{9,13},{13,9},{2,6},{6,2},{1... | collective-permute-start | bytes 393224 | tf_op jit(solution)/shard_map/ppermute | solution.py:174
  81.6 7.8 %collective-permute-start.28 = (bf16[64,2048]{1,0:T(8,128)(2,1)S(1)}, bf16[64,2048]{1,0:T(8,128)(2,1)S(1)}, u32[]{:S(2)}, u32[]{:S(2)}) collective-permute-start(bf16[64,2048]{1,0:T(8,128)(2,1)S(1)} %get-tuple-element.203), channel_id=1, source_target_pairs={{0,2},{1,3},{2,0},{3,1},{4,6},{5,7},{6,4},{7,5},{8,10},{9,11},{10,... | collective-permute-start | bytes 786440 | tf_op jit(solution)/shard_map/ppermute | solution.py:174
  85.8 20.6 %collective-permute-start.35 = (bf16[32,2048]{1,0:T(8,128)(2,1)S(1)}, bf16[32,2048]{1,0:T(8,128)(2,1)S(1)}, u32[]{:S(2)}, u32[]{:S(2)}) collective-permute-start(bf16[32,2048]{1,0:T(8,128)(2,1)S(1)} %constant_dynamic-update-slice_fusion.6.refs_2_), channel_id=1, source_target_pairs={{0,4},{4,0},{8,12},{12,8},{1,5},{5,1},{9,13},{13,9},{2,6},{6,2},{1... | collective-permute-start | bytes 393224 | tf_op jit(solution)/shard_map/ppermute | solution.py:174
  89.5 8.0 %collective-permute-start.30 = (bf16[64,2048]{1,0:T(8,128)(2,1)S(1)}, bf16[64,2048]{1,0:T(8,128)(2,1)S(1)}, u32[]{:S(2)}, u32[]{:S(2)}) collective-permute-start(bf16[64,2048]{1,0:T(8,128)(2,1)S(1)} %get-tuple-element.201.refs_2_), channel_id=1, source_target_pairs={{0,2},{1,3},{2,0},{3,1},{4,6},{5,7},{6,4},{7,5},{8,10},{9,11},{10,... | collective-permute-start | bytes 786440 | tf_op jit(solution)/shard_map/ppermute | solution.py:174
  103.5 8.0 %collective-permute-start.38 = (bf16[16,2048]{1,0:T(8,128)(2,1)S(1)}, bf16[16,2048]{1,0:T(8,128)(2,1)S(1)}, u32[]{:S(2)}, u32[]{:S(2)}) collective-permute-start(bf16[16,2048]{1,0:T(8,128)(2,1)S(1)} %fusion.18), channel_id=1, source_target_pairs={{0,8},{4,12},{8,0},{12,4},{1,9},{5,13},{9,1},{13,5},{2,10},{6,14},... | collective-permute-start | bytes 196616 | tf_op jit(solution)/shard_map/ppermute | solution.py:174
  111.5 8.9 %collective-permute-start.40 = (bf16[32,2048]{1,0:T(8,128)(2,1)S(1)}, bf16[32,2048]{1,0:T(8,128)(2,1)S(1)}, u32[]{:S(2)}, u32[]{:S(2)}) collective-permute-start(bf16[32,2048]{1,0:T(8,128)(2,1)S(1)} %constant_dynamic-update-slice_fusion.10.refs_0_), channel_id=1, source_target_pairs={{0,4},{4,0},{8,12},{12,8},{1,5},{5,1},{9,13},{13,9},{2,6},{6,2},{1... | collective-permute-start | bytes 393224 | tf_op jit(solution)/shard_map/ppermute | solution.py:174
  115.8 10.3 %collective-permute-start.43 = (bf16[16,2048]{1,0:T(8,128)(2,1)S(1)}, bf16[16,2048]{1,0:T(8,128)(2,1)S(1)}, u32[]{:S(2)}, u32[]{:S(2)}) collective-permute-start(bf16[16,2048]{1,0:T(8,128)(2,1)S(1)} %negate_convert_fusion), channel_id=1, source_target_pairs={{0,8},{4,12},{8,0},{12,4},{1,9},{5,13},{9,1},{13,5},{2,10},{6,14},... | collective-permute-start | bytes 196616 | tf_op jit(solution)/shard_map/ppermute | solution.py:174
  118.7 12.9 %collective-permute-start.46 = (bf16[64,2048]{1,0:T(8,128)(2,1)S(1)}, bf16[64,2048]{1,0:T(8,128)(2,1)S(1)}, u32[]{:S(2)}, u32[]{:S(2)}) collective-permute-start(bf16[64,2048]{1,0:T(8,128)(2,1)S(1)} %get-tuple-element.197.refs_6_), channel_id=1, source_target_pairs={{0,2},{1,3},{2,0},{3,1},{4,6},{5,7},{6,4},{7,5},{8,10},{9,11},{10,... | collective-permute-start | bytes 786440 | tf_op jit(solution)/shard_map/ppermute | solution.py:174
  139.8 9.1 %collective-permute-start.50 = (bf16[64,2048]{1,0:T(8,128)(2,1)S(1)}, bf16[64,2048]{1,0:T(8,128)(2,1)S(1)}, u32[]{:S(2)}, u32[]{:S(2)}) collective-permute-start(bf16[64,2048]{1,0:T(8,128)(2,1)S(1)} %get-tuple-element.193), channel_id=1, source_target_pairs={{0,2},{1,3},{2,0},{3,1},{4,6},{5,7},{6,4},{7,5},{8,10},{9,11},{10,... | collective-permute-start | bytes 786440 | tf_op jit(solution)/shard_map/ppermute | solution.py:174
  141.3 16.0 %collective-permute-start.51 = (bf16[64,2048]{1,0:T(8,128)(2,1)S(1)}, bf16[64,2048]{1,0:T(8,128)(2,1)S(1)}, u32[]{:S(2)}, u32[]{:S(2)}) collective-permute-start(bf16[64,2048]{1,0:T(8,128)(2,1)S(1)} %get-tuple-element.191), channel_id=1, source_target_pairs={{0,2},{1,3},{2,0},{3,1},{4,6},{5,7},{6,4},{7,5},{8,10},{9,11},{10,... | collective-permute-start | bytes 786440 | tf_op jit(solution)/shard_map/ppermute | solution.py:174
  (40 other events, 285.2 us)
